TPU v7x, 256 devices: a whole 4x4x8 slice. The times are simulated.
256 devices in a mesh: section: 4 (over y), dp: 64 (over x, z, core).
Axes of the slice: x: 4, y: 4, z: 8, core: 2. Of those that a mesh axis runs over, the one named last changes fastest.
Arguments:
- hidden_in: bfloat16 [2, 4, 4, 1024, 4096], P(None, 'section', None, 'dp'), may hold values from -6 to 6
- out_grad: bfloat16 [4, 1024, 4096], P(None, 'dp'), may hold values from -6 to 6
- gate_probs: float32 [2, 4, 4, 1024, 2], P(None, 'section', None, 'dp'), may hold values from 0.1 to 1
- expert_ids: int32 [2, 4, 4, 1024, 2], P(None, 'section', None, 'dp'), may hold values from 0 to 7, all different within a row
- task_ids: int32 [4, 64], P(None, 'dp'), may hold values from 0 to 1
- task_embed: float32 [2, 256], replicated, may hold values from -5 to 5
- slot_embed: float32 [2, 4, 8, 256], P(None, 'section'), may hold values from -5 to 5
- gen_down: bfloat16 [256, 65536], P(None, 'dp'), may hold values from -0.0078125 to 0.0078125
- gen_up: bfloat16 [256, 65536], P(None, 'dp'), may hold values from -0.09375 to 0.09375
Outputs:
- d_hidden: bfloat16 [4, 4, 1024, 4096], P('section', None, 'dp')
- d_gen_down: float32 [256, 65536], P(None, 'dp')
- d_gen_up: float32 [256, 65536], P(None, 'dp')
- d_task_embed: float32 [2, 256], replicated
- d_slot_embed: float32 [2, 4, 8, 256], P(None, 'section')
Inputs may be any that keep to these rules, and one draw needn't show every extreme that they name: `expert_ids`: the two experts of a token differ.
All inputs are finite; a program needn't handle non-finite values.
Results may differ from a plain program's by a relative error of at most 0.025.
Values may be sent and summed in bfloat16 or wider, within the bound.
No kernel may reach another device: no remote copies, remote signals or barrier semaphores. Data moves between devices by JAX's collectives and lax.ppermute only.
A program may use at most 64 MiB of HBM per device.

v0:
```python
import functools

import jax
import jax.numpy as jnp
from jax import lax
from jax.experimental import pallas as pl
from jax.experimental.pallas import tpu as pltpu
from jax.sharding import Mesh, PartitionSpec as P

eps = 1e-05
bf16 = jnp.bfloat16
f32 = jnp.float32

AXES = ("s", "x", "zh", "zl", "c")
DP = ("x", "zh", "zl", "c")
RANKS = ("x", "zh")
QUARTERS = ("zl", "c")
VMEM = pl.BlockSpec(memory_space=pltpu.VMEM)
SMEM = pl.BlockSpec(memory_space=pltpu.SMEM)
LAST = (((1,), (1,)), ((), ()))
FIRST = (((0,), (0,)), ((), ()))
VMEM_LIMIT = 6 * 1024 * 1024
ADAPTER_LIMIT = 53 * 1024 * 1024


def adapter_copies(g_ref, block, which, held_ref, sems):
    return [
        pltpu.make_async_copy(g_ref.at[:, q, block, which], held_ref.at[q], sems.at[q])
        for q in range(g_ref.shape[1])
    ]


def adapter_rows(held_ref, q):
    part = held_ref[q]
    return part.reshape(part.shape[0] * part.shape[1], part.shape[2])


def prep_kernel(x_ref, xn_ref, inv_ref, sent_ref):
    items, rows, _ = x_ref.shape
    width = sent_ref.shape[2]
    for item in range(items):
        values = x_ref[item].astype(f32)
        inv = lax.rsqrt(jnp.mean(values * values, axis=1, keepdims=True) + eps)
        inv_ref[item] = jnp.broadcast_to(inv, (rows, inv_ref.shape[2]))
        normed = (values * inv).astype(bf16)
        where = slice(item * rows, (item + 1) * rows)
        xn_ref[where, :] = normed
        for q in range(sent_ref.shape[0]):
            sent_ref[q, where, :] = normed[:, q * width : (q + 1) * width]


def low_kernel(xn_ref, weights_ref, g_ref, out_ref, held_ref, sems):
    blocks, tokens, _ = out_ref.shape
    quarters, width = g_ref.shape[1], g_ref.shape[5]
    copies = [adapter_copies(g_ref, j, 0, held_ref.at[j], sems.at[j]) for j in range(blocks)]
    for copy in sum(copies, []):
        copy.start()
    for j in range(blocks):
        low = jnp.zeros(out_ref.shape[1:], f32)
        for q in range(quarters):
            copies[j][q].wait()
            low += lax.dot_general(
                xn_ref[j * tokens : (j + 1) * tokens, q * width : (q + 1) * width],
                adapter_rows(held_ref.at[j], q),
                LAST,
                preferred_element_type=f32,
            )
        out_ref[j] = (weights_ref[j] * low).astype(bf16)


def tick_kernel(tick, sections, micros, where_ref, *refs):
    refs = list(refs)
    x_ref, inv_ref, weights_ref, g_ref, dx_ref, du_ref, held_ref, sems = refs[-8:]
    blocks, items = g_ref.shape[2], x_ref.shape[0]
    quarters, width = g_ref.shape[1], g_ref.shape[5]
    section = where_ref[0]
    position = jnp.clip(tick - (sections - 1 - section), 0, items - 1)
    late = (position >= micros).astype(jnp.int32)
    block = blocks - 1 - late
    item = block * micros + position - late * micros
    copies = [adapter_copies(g_ref, block, i, held_ref.at[i], sems.at[i]) for i in (0, 1)]
    for copy in copies[1] + copies[0]:
        copy.start()
    if tick < micros:
        grad = refs.pop(0)[tick]
        if tick:
            cot = jnp.where(section == sections - 1, grad, refs.pop(0)[...])
        else:
            cot = grad
    else:
        cot = refs.pop(0)[...]
    back = jnp.zeros(du_ref.shape, f32)
    for q in range(quarters):
        copies[1][q].wait()
        back += lax.dot_general(
            cot[:, q * width : (q + 1) * width],
            adapter_rows(held_ref.at[1], q),
            LAST,
            preferred_element_type=f32,
        )
    du = (weights_ref[item] * back).astype(bf16)
    du_ref[...] = du
    inv = inv_ref[item][:, :1]
    dxn, xf = [], []
    total = jnp.zeros((du.shape[0], 1), f32)
    for q in range(quarters):
        xf.append(x_ref[item, :, q * width : (q + 1) * width].astype(f32) * inv)
        copies[0][q].wait()
        dxn.append(jnp.dot(du, adapter_rows(held_ref.at[0], q), preferred_element_type=f32))
        total += jnp.sum(dxn[q] * xf[q], axis=1, keepdims=True)
    mean = total * (1.0 / (quarters * width))
    for q in range(quarters):
        cols = slice(q * width, (q + 1) * width)
        dx_ref[:, cols] = (
            cot[:, cols].astype(f32) + inv * (dxn[q] - xf[q] * mean)
        ).astype(bf16)


def pack_kernel(block, micros, sections, fresh, where_ref, low_ref, *refs):
    out_ref = refs[-1]
    grad_ref = refs[0]
    cots, dus = refs[1 : sections + micros], refs[sections + micros : -1]
    quarters, tokens, _ = out_ref.shape
    rows, wide = dus[0].shape
    width = cots[0].shape[1] // quarters
    section = where_ref[0]
    for m in range(micros):
        cot = grad_ref[m] if fresh else cots[m][...]
        du = dus[m][...]
        for s in range(sections - 1):
            at = m + sections - 1 - s
            cot = jnp.where(section == s, cots[at][...], cot)
            du = jnp.where(section == s, dus[at][...], du)
        where = slice(m * rows, (m + 1) * rows)
        for q in range(quarters):
            out_ref[q, where, :width] = cot[:, q * width : (q + 1) * width]
            out_ref[q, where, width : width + wide] = du
    for q in range(quarters):
        out_ref[q, :, width + wide :] = low_ref[block]


def grads_kernel(block, mixed_ref, xn_ref, out_ref):
    quarters, _, width = xn_ref.shape
    tokens = mixed_ref.shape[0] // quarters
    ranks, combos = out_ref.shape[0], out_ref.shape[1] // 2
    wide = ranks * combos
    xn = jnp.concatenate(
        [xn_ref[q, block * tokens : (block + 1) * tokens, :] for q in range(quarters)]
    )
    dy = mixed_ref[:, :width]
    du = mixed_ref[:, width : width + wide]
    low = mixed_ref[:, width + wide :]
    grad_a = lax.dot_general(du, xn, FIRST, preferred_element_type=f32)
    out_ref[:, :combos, :] = grad_a.astype(bf16).reshape(ranks, combos, width)
    grad_b = lax.dot_general(low, dy, FIRST, preferred_element_type=f32)
    out_ref[:, combos:, :] = grad_b.astype(bf16).reshape(ranks, combos, width)


def generate_kernel(cond_ref, down_ref, up_ref, out_ref):
    blocks, _, combos, _ = out_ref.shape
    cond = cond_ref[...]
    first = cond.astype(bf16)
    rest = cond - first.astype(f32)
    second = rest.astype(bf16)
    third = (rest - second.astype(f32)).astype(bf16)
    parts = jnp.concatenate([first, second, third])
    rows = cond.shape[0]
    for which, gen_ref in enumerate((down_ref, up_ref)):
        made = jnp.dot(parts, gen_ref[...], preferred_element_type=f32)
        made = made[:rows] + (made[rows : 2 * rows] + made[2 * rows :])
        out_ref[:, which] = made.astype(bf16).reshape(blocks, combos, -1)


def call(kernel, out_shape, operands, flops, moved, adapters=None):
    scalars = 1 if operands[0].dtype == jnp.int32 else 0
    specs = [SMEM] * scalars + [VMEM] * (len(operands) - scalars)
    scratch = []
    if adapters is not None:
        ranks, quarters, _, _, combos, width = adapters.shape
        operands = (*operands, adapters)
        specs.append(pl.BlockSpec(memory_space=pltpu.HBM))
        scratch = [
            pltpu.VMEM((2, quarters, ranks, combos, width), bf16),
            pltpu.SemaphoreType.DMA((2, quarters)),
        ]
    return pl.pallas_call(
        kernel,
        out_shape=out_shape,
        in_specs=specs,
        out_specs=jax.tree.map(lambda _: VMEM, out_shape),
        scratch_shapes=scratch,
        compiler_params=pltpu.CompilerParams(
            vmem_limit_bytes=VMEM_LIMIT if adapters is None else ADAPTER_LIMIT
        ),
        cost_estimate=pl.CostEstimate(flops=flops, bytes_accessed=moved, transcendentals=0),
    )(*operands)


def from_sections(part):
    count = lax.axis_size("s")
    got = [part] + [
        lax.ppermute(part, "s", [((i + d) % count, i) for i in range(count)])
        for d in range(1, count)
    ]
    me = lax.axis_index("s")
    return jnp.stack([lax.select_n(lax.rem(i + count - me, count), *got) for i in range(count)])


def on_device(
    hidden_in, out_grad, gate_probs, expert_ids, task_ids, task_embed, slot_embed, gen_down, gen_up
):
    high = lax.Precision.HIGHEST
    sections = lax.axis_size("s")
    section_id = lax.axis_index("s")
    quarters = lax.axis_size(QUARTERS)
    ranks = lax.axis_size(RANKS)
    blocks, _, micros, rows, model = hidden_in.shape
    tasks, cond_width = task_embed.shape
    experts = slot_embed.shape[2]
    combos = tasks * experts
    width = model // quarters
    wide = ranks * combos
    items = blocks * micros
    tokens = micros * rows
    where = section_id.reshape(1).astype(jnp.int32)

    def shaped(*shape, dtype=bf16):
        return jax.ShapeDtypeStruct(shape, dtype)

    pre = task_embed[None, :, None, :] + slot_embed[:, 0][:, None, :, :]
    cond = jax.nn.silu(pre).reshape(blocks, combos, cond_width)
    mine = call(
        generate_kernel,
        shaped(blocks, 2, combos, width),
        (cond.reshape(blocks * combos, cond_width), gen_down, gen_up),
        12 * blocks * combos * cond_width * width,
        5 << 18,
    )
    filled = lax.all_gather(mine.reshape(blocks * 2 * combos, width), DP, axis=0, tiled=True)

    slots = from_sections(slot_embed[:, 0])
    x_items = hidden_in[:, 0].reshape(items, rows, model)
    normed, inv_items, sent = call(
        prep_kernel,
        [
            shaped(items * rows, model),
            shaped(items, rows, 128, dtype=f32),
            shaped(quarters, items * rows, width),
        ],
        (x_items,),
        8 * items * rows * model,
        3 << 20,
    )
    normed_quarter = lax.all_to_all(sent, QUARTERS, 0, 0)
    lane = jnp.arange(wide, dtype=jnp.int32)
    expert_of, task_of = lane % experts, (lane // experts) % tasks
    ids, gates = expert_ids[:, 0], gate_probs[:, 0]
    weights = jnp.where(ids[..., 0:1] == expert_of, gates[..., 0:1], 0.0) + jnp.where(
        ids[..., 1:2] == expert_of, gates[..., 1:2], 0.0
    )
    weights = jnp.where(task_ids[None, :, :, None] == task_of, weights, 0.0)
    weights_items = weights.reshape(items, rows, wide)

    filled, slots, normed, inv_items, normed_quarter, weights_items = lax.optimization_barrier(
        (filled, slots, normed, inv_items, normed_quarter, weights_items)
    )
    adapters = filled.reshape(ranks, quarters, blocks, 2, combos, width)
    pairs = [(i, (i - 1) % sections) for i in range(sections)]
    last = items + sections - 2

    def packed(block):
        span = slice((blocks - 1 - block) * micros, (blocks - block) * micros + sections - 1)
        fresh = block == blocks - 1
        cots = [out_grad[0] if cot is None else cot for cot in incoming[span]]
        return call(
            functools.partial(pack_kernel, block, micros, sections, fresh),
            shaped(quarters, tokens, width + 2 * wide),
            (where, low, out_grad, *cots, *dus[span]),
            0,
            3 << 20,
        )

    def partial_grads(block, mixed):
        return call(
            functools.partial(grads_kernel, block),
            shaped(ranks, 2 * combos, width),
            (mixed.reshape(quarters * tokens, width + 2 * wide), normed_quarter),
            4 * quarters * tokens * wide * width,
            5 << 20,
        )

    def summed(got):
        scale = 1.0 / (micros * rows * lax.axis_size(DP))
        return (jnp.sum(got.astype(f32), axis=0) * scale).astype(bf16)

    incoming, dus, results = [None], [], []
    for tick in range(last + 1):
        operands = [where]
        if tick < micros:
            operands.append(out_grad)
        if tick:
            operands.append(incoming[tick])
        result, du = call(
            functools.partial(tick_kernel, tick, sections, micros),
            [shaped(rows, model), shaped(rows, wide)],
            (*operands, x_items, inv_items, weights_items),
            4 * rows * wide * model,
            5 << 20,
            adapters,
        )
        results.append(result)
        dus.append(du)
        if tick == last:
            break
        arriving = lax.ppermute(result, "s", pairs)
        if tick == 1:
            low = call(
                low_kernel,
                shaped(blocks, tokens, wide),
                (normed, weights_items.reshape(blocks, tokens, wide)),
                2 * blocks * tokens * wide * model,
                3 << 21,
                adapters,
            )
            arriving, low = lax.optimization_barrier((arriving, low))
        if tick == micros + sections - 2:
            mixed = lax.all_to_all(packed(1), QUARTERS, 0, 0)
        if tick == micros + sections - 1:
            early = partial_grads(1, mixed)
            arriving, early = lax.optimization_barrier((arriving, early))
            early_got = lax.all_to_all(early, RANKS, 0, 0)
        incoming.append(arriving)
    late, early_got = lax.optimization_barrier((packed(0), early_got))
    mixed = lax.all_to_all(late, QUARTERS, 0, 0)
    late_got = lax.all_to_all(partial_grads(0, mixed), RANKS, 0, 0)

    hidden_out = jnp.stack(
        [
            lax.select_n(
                section_id,
                *[results[micros + m + sections - 1 - s] for s in range(sections)],
            )
            for m in range(micros)
        ]
    )
    hidden_out, late_got = lax.optimization_barrier((hidden_out, late_got))
    reduced = jnp.stack([summed(late_got), summed(early_got)])
    pre_all = task_embed[None, None, :, None, :] + slots[:, :, None, :, :]
    cond_all = jax.nn.silu(pre_all).reshape(sections * blocks * combos, cond_width)
    grads = from_sections(reduced).reshape(sections * blocks, 2, combos, width)
    grad_a = grads[:, 0].reshape(-1, width)
    grad_b = grads[:, 1].reshape(-1, width)
    d_cond = jnp.einsum("nf,wf->nw", grad_a, gen_down, preferred_element_type=f32)
    d_cond = d_cond + jnp.einsum("nf,wf->nw", grad_b, gen_up, preferred_element_type=f32)
    gate = jax.nn.sigmoid(pre_all)
    d_pre = d_cond.reshape(pre_all.shape) * gate * (1.0 + pre_all * (1.0 - gate))
    own = lax.dynamic_index_in_dim(d_pre, section_id, 0, keepdims=False)
    d_slot = jnp.sum(own, axis=1).reshape(blocks * experts, cond_width)
    d_task = jnp.sum(d_pre, axis=(0, 1, 3))
    small = jnp.concatenate([d_slot, d_task])
    held = small.reshape(-1, 128)
    held = jnp.pad(held, ((0, -held.shape[0] % 8), (0, 0)))
    for axes in (QUARTERS, "x", "zh"):
        got = lax.all_gather(held, axes, axis=0, tiled=True)
        held = jnp.sum(got.reshape(-1, *held.shape), axis=0)
    small = held[: small.size // 128].reshape(small.shape)
    d_slot = small[: blocks * experts].reshape(blocks, 1, experts, cond_width)
    d_task = small[blocks * experts :]
    d_gen_down = jnp.einsum("nw,nf->wf", cond_all, grad_a.astype(f32), precision=high)
    d_gen_up = jnp.einsum("nw,nf->wf", cond_all, grad_b.astype(f32), precision=high)
    return (hidden_out[None], d_gen_down, d_gen_up, d_task, d_slot)


def solution(mesh):
    split = Mesh(mesh.devices.reshape(mesh.devices.shape[0], 4, 4, 2, 2), AXES)
    placed = (
        P(None, "s", None, DP, None),
        P(None, DP, None),
        P(None, "s", None, DP, None),
        P(None, "s", None, DP, None),
        P(None, DP),
        P(),
        P(None, "s", None, None),
        P(None, DP),
        P(None, DP),
    )
    return jax.shard_map(
        on_device,
        mesh=split,
        in_specs=placed,
        out_specs=(
            P("s", None, DP, None),
            P(None, DP),
            P(None, DP),
            P(),
            P(None, "s", None, None),
        ),
        check_vma=False,
    )
```

profile of v0, /device:TPU:1, one launch (start us, length us, event | category | flops | bytes accessed | tf_op | source)
XLA Modules:
  0.0 334.3 jit_solution(6369778179809518262)
XLA Ops:
  13.5 6.7 %all-to-all-start = ((bf16[4,128,1024]{2,1,0:T(8,128)(2,1)}), bf16[4,128,1024]{2,1,0:T(8,128)(2,1)S(1)}, u32[]{:S(2)}, u32[]{:S(2)}) async-start(bf16[4,128,1024]{2,1,0:T(8,128)(2,1)} %get-tuple-element.46), calls=%async_computation | async-start | bytes 2097152 | tf_op jit(solution)/shard_map/all_to_all | solution.py:254
  26.1 8.5 %all-to-all-done.xn_ref = bf16[4,128,1024]{2,1,0:T(8,128)(2,1)S(1)} async-done(((bf16[4,128,1024]{2,1,0:T(8,128)(2,1)}), bf16[4,128,1024]{2,1,0:T(8,128)(2,1)S(1)}, u32[]{:S(2)}, u32[]{:S(2)}) %all-to-all-start) | async-done | bytes 1048608 | tf_op jit(solution)/shard_map/all_to_all | solution.py:254
  34.6 64.0 %all-gather.2.cloned.1.call-done = bf16[4096,1024]{1,0:T(8,128)(2,1)} async-done(((bf16[64,1024]{1,0:T(8,128)(2,1)}), bf16[4096,1024]{1,0:T(8,128)(2,1)}) %all-gather.2.cloned.1.call-update) | async-done | bytes 8388624 | tf_op jit(solution)/shard_map/all_gather | solution.py:239
  98.6 4.9 %shard_map.130 = (bf16[16,4096]{1,0:T(8,128)(2,1)S(1)}, bf16[16,256]{1,0:T(8,128)(2,1)S(1)}) custom-call(s32[1]{0:T(128)} %bitcast.where_ref, bf16[4,16,4096]{2,1,0:T(8,128)(2,1)S(1)} %copy-done.1, bf16[8,16,4096]{2,1,0:T(8,128)(2,1)} %bitcast.79, f32[8,16,128]{2,1,0:T(8,128)S(1)} %get-tuple-element.47.refs_2_.refs_3_, ...), custom_call_target="tpu_custom_call" | custom-call | flops 67108864 | bytes 5242880 | tf_op jit(solution)/shard_map/pallas_call | solution.py:186
  108.8 5.1 %shard_map.131 = (bf16[16,4096]{1,0:T(8,128)(2,1)S(1)}, bf16[16,256]{1,0:T(8,128)(2,1)S(1)}) custom-call(s32[1]{0:T(128)} %bitcast.where_ref, bf16[4,16,4096]{2,1,0:T(8,128)(2,1)} %refs_0_.11, bf16[16,4096]{1,0:T(8,128)(2,1)S(1)} %collective-permute-done.3.refs_1_.refs_2_, bf16[8,16,4096]{2,1,0:T(8,128)(2,1)} %bitcast.80, ...), custom_call_target="tpu_custom_call" | custom-call | flops 67108864 | bytes 5242880 | tf_op jit(solution)/shard_map/pallas_call | solution.py:186
  117.4 5.1 %shard_map.132.low_ref = bf16[2,64,256]{2,1,0:T(8,128)(2,1)S(1)} custom-call(bf16[128,4096]{1,0:T(8,128)(2,1)} %copy-done.7, f32[2,64,256]{2,1,0:T(8,128)S(1)} %bitcast.91, bf16[16,4,2,2,16,1024]{5,4,3,2,1,0:T(8,128)(2,1)} %bitcast.96), custom_call_target="tpu_custom_call" | custom-call | flops 268435456 | bytes 6291456 | tf_op jit(solution)/shard_map/pallas_call | solution.py:186
  122.5 5.1 %shard_map.133 = (bf16[16,4096]{1,0:T(8,128)(2,1)S(1)}, bf16[16,256]{1,0:T(8,128)(2,1)S(1)}) custom-call(s32[1]{0:T(128)} %bitcast.where_ref, bf16[4,16,4096]{2,1,0:T(8,128)(2,1)} %refs_0_.11, bf16[16,4096]{1,0:T(8,128)(2,1)S(1)} %collective-permute-done.4.refs_1_.refs_3_, bf16[8,16,4096]{2,1,0:T(8,128)(2,1)} %bitcast.81, ...), custom_call_target="tpu_custom_call" | custom-call | flops 67108864 | bytes 5242880 | tf_op jit(solution)/shard_map/pallas_call | solution.py:186
  127.7 3.8 %collective-permute-done.5.refs_1_.refs_4_ = bf16[16,4096]{1,0:T(8,128)(2,1)S(1)} collective-permute-done((bf16[16,4096]{1,0:T(8,128)(2,1)S(1)}, bf16[16,4096]{1,0:T(8,128)(2,1)S(1)}, u32[]{:S(2)}, u32[]{:S(2)}) %collective-permute-start.5) | collective-permute-done | bytes 131104 | tf_op jit(solution)/shard_map/ppermute | solution.py:315
  131.5 5.1 %shard_map.134 = (bf16[16,4096]{1,0:T(8,128)(2,1)S(1)}, bf16[16,256]{1,0:T(8,128)(2,1)S(1)}) custom-call(s32[1]{0:T(128)} %bitcast.where_ref, bf16[4,16,4096]{2,1,0:T(8,128)(2,1)} %refs_0_.11, bf16[16,4096]{1,0:T(8,128)(2,1)S(1)} %collective-permute-done.5.refs_1_.refs_4_, bf16[8,16,4096]{2,1,0:T(8,128)(2,1)} %bitcast.82, ...), custom_call_target="tpu_custom_call" | custom-call | flops 67108864 | bytes 5242880 | tf_op jit(solution)/shard_map/pallas_call | solution.py:186
  140.7 4.9 %shard_map.135 = (bf16[16,4096]{1,0:T(8,128)(2,1)S(1)}, bf16[16,256]{1,0:T(8,128)(2,1)S(1)}) custom-call(s32[1]{0:T(128)} %bitcast.where_ref, bf16[16,4096]{1,0:T(8,128)(2,1)S(1)} %collective-permute-done.6.refs_0_.refs_5_.refs_1_, bf16[8,16,4096]{2,1,0:T(8,128)(2,1)} %bitcast.83, f32[8,16,128]{2,1,0:T(8,128)S(1)} %get-tuple-element.47.refs_2_.refs_3_, ...), custom_call_target="tpu_custom_call" | custom-call | flops 67108864 | bytes 5242880 | tf_op jit(solution)/shard_map/pallas_call | solution.py:186
  150.1 4.9 %shard_map.136 = (bf16[16,4096]{1,0:T(8,128)(2,1)S(1)}, bf16[16,256]{1,0:T(8,128)(2,1)S(1)}) custom-call(s32[1]{0:T(128)} %bitcast.where_ref, bf16[16,4096]{1,0:T(8,128)(2,1)S(1)} %collective-permute-done.7.refs_0_.refs_6_.refs_2_, bf16[8,16,4096]{2,1,0:T(8,128)(2,1)} %bitcast.84, f32[8,16,128]{2,1,0:T(8,128)S(1)} %get-tuple-element.47.refs_2_.refs_3_, ...), custom_call_target="tpu_custom_call" | custom-call | flops 67108864 | bytes 5242880 | tf_op jit(solution)/shard_map/pallas_call | solution.py:186
  160.1 4.9 %shard_map.137 = (bf16[16,4096]{1,0:T(8,128)(2,1)S(1)}, bf16[16,256]{1,0:T(8,128)(2,1)S(1)}) custom-call(s32[1]{0:T(128)} %bitcast.where_ref, bf16[16,4096]{1,0:T(8,128)(2,1)S(1)} %collective-permute-done.8.refs_0_.refs_7_.refs_3_, bf16[8,16,4096]{2,1,0:T(8,128)(2,1)} %bitcast.85, f32[8,16,128]{2,1,0:T(8,128)S(1)} %get-tuple-element.47.refs_2_.refs_3_, ...), custom_call_target="tpu_custom_call" | custom-call | flops 67108864 | bytes 5242880 | tf_op jit(solution)/shard_map/pallas_call | solution.py:186
  166.1 9.9 %all-to-all-start.1 = ((bf16[4,64,1536]{2,1,0:T(8,128)(2,1)}), bf16[4,64,1536]{2,1,0:T(8,128)(2,1)S(1)}, u32[]{:S(2)}, u32[]{:S(2)}) async-start(bf16[4,64,1536]{2,1,0:T(8,128)(2,1)} %shard_map.139), calls=%async_computation.1 | async-start | bytes 1572864 | tf_op jit(solution)/shard_map/all_to_all | solution.py:327
  182.1 5.6 %shard_map.138 = (bf16[16,4096]{1,0:T(8,128)(2,1)}, bf16[16,256]{1,0:T(8,128)(2,1)S(1)}) custom-call(s32[1]{0:T(128)} %bitcast.where_ref, bf16[16,4096]{1,0:T(8,128)(2,1)S(1)} %collective-permute-done.9.refs_0_.refs_4_, bf16[8,16,4096]{2,1,0:T(8,128)(2,1)} %bitcast.86, f32[8,16,128]{2,1,0:T(8,128)S(1)} %get-tuple-element.47.refs_2_.refs_3_, ...), custom_call_target="tpu_custom_call" | custom-call | flops 67108864 | bytes 5242880 | tf_op jit(solution)/shard_map/pallas_call | solution.py:186
  194.0 5.0 %all-to-all-start.2 = ((bf16[16,32,1024]{2,1,0:T(8,128)(2,1)}), bf16[16,32,1024]{2,1,0:T(8,128)(2,1)}, u32[]{:S(2)}, u32[]{:S(2)}) async-start(bf16[16,32,1024]{2,1,0:T(8,128)(2,1)} %shard_map.140), calls=%async_computation.2 | async-start | bytes 2097152 | tf_op jit(solution)/shard_map/all_to_all | solution.py:331
  199.0 4.9 %shard_map.141 = (bf16[16,4096]{1,0:T(8,128)(2,1)S(1)}, bf16[16,256]{1,0:T(8,128)(2,1)S(1)}) custom-call(s32[1]{0:T(128)} %bitcast.where_ref, bf16[16,4096]{1,0:T(8,128)(2,1)S(1)} %collective-permute-done.10.refs_0_.refs_5_, bf16[8,16,4096]{2,1,0:T(8,128)(2,1)} %bitcast.87, f32[8,16,128]{2,1,0:T(8,128)S(1)} %get-tuple-element.47.refs_2_.refs_3_, ...), custom_call_target="tpu_custom_call" | custom-call | flops 67108864 | bytes 5242880 | tf_op jit(solution)/shard_map/pallas_call | solution.py:186
  209.0 4.9 %shard_map.142 = (bf16[16,4096]{1,0:T(8,128)(2,1)S(1)}, bf16[16,256]{1,0:T(8,128)(2,1)S(1)}) custom-call(s32[1]{0:T(128)} %bitcast.where_ref, bf16[16,4096]{1,0:T(8,128)(2,1)S(1)} %collective-permute-done.11.refs_0_.refs_6_, bf16[8,16,4096]{2,1,0:T(8,128)(2,1)} %bitcast.88, f32[8,16,128]{2,1,0:T(8,128)S(1)} %get-tuple-element.47.refs_2_.refs_3_, ...), custom_call_target="tpu_custom_call" | custom-call | flops 67108864 | bytes 5242880 | tf_op jit(solution)/shard_map/pallas_call | solution.py:186
  220.0 4.9 %shard_map.143 = (bf16[16,4096]{1,0:T(8,128)(2,1)S(1)}, bf16[16,256]{1,0:T(8,128)(2,1)S(1)}) custom-call(s32[1]{0:T(128)} %bitcast.where_ref, bf16[16,4096]{1,0:T(8,128)(2,1)S(1)} %collective-permute-done.12.refs_0_.refs_7_, bf16[8,16,4096]{2,1,0:T(8,128)(2,1)} %bitcast.89, f32[8,16,128]{2,1,0:T(8,128)S(1)} %get-tuple-element.47.refs_2_.refs_3_, ...), custom_call_target="tpu_custom_call" | custom-call | flops 67108864 | bytes 5242880 | tf_op jit(solution)/shard_map/pallas_call | solution.py:186
  225.7 17.3 %all_to_all.25 = bf16[4,64,1536]{2,1,0:T(8,128)(2,1)S(1)} all-to-all(bf16[4,64,1536]{2,1,0:T(8,128)(2,1)S(1)} %shard_map.144), channel_id=1, replica_groups=mesh['s'=4,'x'=4,'zh'=4,'zl'=2,'c'=2] {'zl','c'}, dimensions={0} | all-to-all | bytes 1572864 | tf_op jit(solution)/shard_map/all_to_all | solution.py:334
  244.5 9.3 %all-to-all-start.4 = ((bf16[16,32,1024]{2,1,0:T(8,128)(2,1)}), bf16[16,32,1024]{2,1,0:T(8,128)(2,1)S(1)}, u32[]{:S(2)}, u32[]{:S(2)}) async-start(bf16[16,32,1024]{2,1,0:T(8,128)(2,1)} %shard_map.145), calls=%async_computation.4 | async-start | bytes 2097152 | tf_op jit(solution)/shard_map/all_to_all | solution.py:335
  257.1 24.1 %all-to-all-done.4 = bf16[16,32,1024]{2,1,0:T(8,128)(2,1)S(1)} async-done(((bf16[16,32,1024]{2,1,0:T(8,128)(2,1)}), bf16[16,32,1024]{2,1,0:T(8,128)(2,1)S(1)}, u32[]{:S(2)}, u32[]{:S(2)}) %all-to-all-start.4) | async-done | bytes 1048608 | tf_op jit(solution)/shard_map/all_to_all | solution.py:335
  292.9 10.4 %all_gather.13 = f32[160,128]{1,0:T(8,128)S(1)} all-gather(f32[40,128]{1,0:T(8,128)S(1)} %pad.4), channel_id=1, replica_groups=mesh['s'=4,'x'=4,'zh'=4,'zl'=2,'c'=2] {'zl','c'}, dimensions={0}, use_global_device_ids=true | all-gather | bytes 102400 | tf_op jit(solution)/shard_map/all_gather | solution.py:364
  303.3 9.0 %all_gather.14 = f32[160,128]{1,0:T(8,128)S(1)} all-gather(f32[40,128]{1,0:T(8,128)S(1)} %reduce_sum.67), channel_id=1, replica_groups=mesh['s'=4,'x'=4,'zh'=4,'zl'=2,'c'=2] {'x'}, dimensions={0}, use_global_device_ids=true | all-gather | bytes 102400 | tf_op jit(solution)/shard_map/all_gather | solution.py:364
  312.3 10.8 %all_gather.15 = f32[160,128]{1,0:T(8,128)S(1)} all-gather(f32[40,128]{1,0:T(8,128)S(1)} %reduce_sum.68), channel_id=1, replica_groups=mesh['s'=4,'x'=4,'zh'=4,'zl'=2,'c'=2] {'zh'}, dimensions={0}, use_global_device_ids=true | all-gather | bytes 102400 | tf_op jit(solution)/shard_map/all_gather | solution.py:364
  (132 shorter events, 80.4 us)
Async XLA Ops:
  7.2 91.5 %all-gather.2.cloned.1.call-start = ((), (), s32[]{:S(2)}) async-start(), calls=%async_computation.5 | async-start | bytes 8519680 | tf_op jit(solution)/shard_map/all_gather | solution.py:239
  11.1 87.5 %copy-start.1 = (bf16[4,16,4096]{2,1,0:T(8,128)(2,1)S(1)}, bf16[4,16,4096]{2,1,0:T(8,128)(2,1)}, u32[]{:S(2)}) copy-start(bf16[4,16,4096]{2,1,0:T(8,128)(2,1)} %refs_0_.11) | copy-start | bytes 1572868
  13.5 21.1 %all-to-all-start = ((bf16[4,128,1024]{2,1,0:T(8,128)(2,1)}), bf16[4,128,1024]{2,1,0:T(8,128)(2,1)S(1)}, u32[]{:S(2)}, u32[]{:S(2)}) async-start(bf16[4,128,1024]{2,1,0:T(8,128)(2,1)} %get-tuple-element.46), calls=%async_computation | async-start | bytes 2097152 | tf_op jit(solution)/shard_map/all_to_all | solution.py:254
  20.2 2.9 collective-permute-start
  21.2 4.1 %collective-permute-start.1 = (f32[2,8,256]{2,1,0:T(8,128)S(1)}, f32[2,8,256]{2,1,0:T(8,128)S(1)}, u32[]{:S(2)}, u32[]{:S(2)}) collective-permute-start(f32[2,8,256]{2,1,0:T(8,128)S(1)} %bitcast.120), channel_id=1, source_target_pairs={{128,0},{192,64},{0,128},{64,192},{129,1},{193,65},{1,129},{65,193... | collective-permute-start | bytes 49160 | tf_op jit(solution)/shard_map/ppermute | solution.py:202
  21.6 3.9 %collective-permute-start.2 = (f32[2,8,256]{2,1,0:T(8,128)S(1)}, f32[2,8,256]{2,1,0:T(8,128)S(1)}, u32[]{:S(2)}, u32[]{:S(2)}) collective-permute-start(f32[2,8,256]{2,1,0:T(8,128)S(1)} %bitcast.121), channel_id=1, source_target_pairs={{192,0},{0,64},{64,128},{128,192},{193,1},{1,65},{65,129},{129,193... | collective-permute-start | bytes 49160 | tf_op jit(solution)/shard_map/ppermute | solution.py:202
  103.6 5.2 %collective-permute-start.3 = (bf16[16,4096]{1,0:T(8,128)(2,1)S(1)}, bf16[16,4096]{1,0:T(8,128)(2,1)S(1)}, u32[]{:S(2)}, u32[]{:S(2)}) collective-permute-start(bf16[16,4096]{1,0:T(8,128)(2,1)S(1)} %get-tuple-element.50), channel_id=1, source_target_pairs={{0,192},{64,0},{128,64},{192,128},{1,193},{65,1},{129,65},{193,129... | collective-permute-start | bytes 393224 | tf_op jit(solution)/shard_map/ppermute | solution.py:315
  113.9 8.6 %collective-permute-start.4 = (bf16[16,4096]{1,0:T(8,128)(2,1)S(1)}, bf16[16,4096]{1,0:T(8,128)(2,1)S(1)}, u32[]{:S(2)}, u32[]{:S(2)}) collective-permute-start(bf16[16,4096]{1,0:T(8,128)(2,1)S(1)} %get-tuple-element.51), channel_id=1, source_target_pairs={{0,192},{64,0},{128,64},{192,128},{1,193},{65,1},{129,65},{193,129... | collective-permute-start | bytes 393224 | tf_op jit(solution)/shard_map/ppermute | solution.py:315
  127.6 3.9 %collective-permute-start.5 = (bf16[16,4096]{1,0:T(8,128)(2,1)S(1)}, bf16[16,4096]{1,0:T(8,128)(2,1)S(1)}, u32[]{:S(2)}, u32[]{:S(2)}) collective-permute-start(bf16[16,4096]{1,0:T(8,128)(2,1)S(1)} %get-tuple-element.54), channel_id=1, source_target_pairs={{0,192},{64,0},{128,64},{192,128},{1,193},{65,1},{129,65},{193,129... | collective-permute-start | bytes 393224 | tf_op jit(solution)/shard_map/ppermute | solution.py:315
  136.6 4.1 %collective-permute-start.6 = (bf16[16,4096]{1,0:T(8,128)(2,1)S(1)}, bf16[16,4096]{1,0:T(8,128)(2,1)S(1)}, u32[]{:S(2)}, u32[]{:S(2)}) collective-permute-start(bf16[16,4096]{1,0:T(8,128)(2,1)S(1)} %get-tuple-element.55), channel_id=1, source_target_pairs={{0,192},{64,0},{128,64},{192,128},{1,193},{65,1},{129,65},{193,129... | collective-permute-start | bytes 393224 | tf_op jit(solution)/shard_map/ppermute | solution.py:315
  145.6 12.6 %copy-start.2 = (bf16[4,16,4096]{2,1,0:T(8,128)(2,1)S(1)}, bf16[4,16,4096]{2,1,0:T(8,128)(2,1)}, u32[]{:S(2)}) copy-start(bf16[4,16,4096]{2,1,0:T(8,128)(2,1)} %refs_0_.11) | copy-start | bytes 1572868
  145.6 4.5 %collective-permute-start.7 = (bf16[16,4096]{1,0:T(8,128)(2,1)S(1)}, bf16[16,4096]{1,0:T(8,128)(2,1)S(1)}, u32[]{:S(2)}, u32[]{:S(2)}) collective-permute-start(bf16[16,4096]{1,0:T(8,128)(2,1)S(1)} %get-tuple-element.56), channel_id=1, source_target_pairs={{0,192},{64,0},{128,64},{192,128},{1,193},{65,1},{129,65},{193,129... | collective-permute-start | bytes 393224 | tf_op jit(solution)/shard_map/ppermute | solution.py:315
  155.0 5.1 %collective-permute-start.8 = (bf16[16,4096]{1,0:T(8,128)(2,1)S(1)}, bf16[16,4096]{1,0:T(8,128)(2,1)S(1)}, u32[]{:S(2)}, u32[]{:S(2)}) collective-permute-start(bf16[16,4096]{1,0:T(8,128)(2,1)S(1)} %get-tuple-element.57), channel_id=1, source_target_pairs={{0,192},{64,0},{128,64},{192,128},{1,193},{65,1},{129,65},{193,129... | collective-permute-start | bytes 393224 | tf_op jit(solution)/shard_map/ppermute | solution.py:315
  165.1 22.7 %copy-start.8 = (bf16[16,4096]{1,0:T(8,128)(2,1)}, bf16[16,4096]{1,0:T(8,128)(2,1)S(1)}, u32[]{:S(2)}) copy-start(bf16[16,4096]{1,0:T(8,128)(2,1)S(1)} %get-tuple-element.58) | copy-start | bytes 393220
  166.1 25.7 %all-to-all-start.1 = ((bf16[4,64,1536]{2,1,0:T(8,128)(2,1)}), bf16[4,64,1536]{2,1,0:T(8,128)(2,1)S(1)}, u32[]{:S(2)}, u32[]{:S(2)}) async-start(bf16[4,64,1536]{2,1,0:T(8,128)(2,1)} %shard_map.139), calls=%async_computation.1 | async-start | bytes 1572864 | tf_op jit(solution)/shard_map/all_to_all | solution.py:327
  176.0 6.1 %collective-permute-start.9 = (bf16[16,4096]{1,0:T(8,128)(2,1)S(1)}, bf16[16,4096]{1,0:T(8,128)(2,1)S(1)}, u32[]{:S(2)}, u32[]{:S(2)}) collective-permute-start(bf16[16,4096]{1,0:T(8,128)(2,1)S(1)} %get-tuple-element.58), channel_id=1, source_target_pairs={{0,192},{64,0},{128,64},{192,128},{1,193},{65,1},{129,65},{193,129... | collective-permute-start | bytes 393224 | tf_op jit(solution)/shard_map/ppermute | solution.py:315
  188.4 5.7 %collective-permute-start.10 = (bf16[16,4096]{1,0:T(8,128)(2,1)}, bf16[16,4096]{1,0:T(8,128)(2,1)S(1)}, u32[]{:S(2)}, u32[]{:S(2)}) collective-permute-start(bf16[16,4096]{1,0:T(8,128)(2,1)} %get-tuple-element.59), channel_id=1, source_target_pairs={{0,192},{64,0},{128,64},{192,128},{1,193},{65,1},{129,65},{193,129... | collective-permute-start | bytes 393224 | tf_op jit(solution)/shard_map/ppermute | solution.py:315
  194.0 31.7 %all-to-all-start.2 = ((bf16[16,32,1024]{2,1,0:T(8,128)(2,1)}), bf16[16,32,1024]{2,1,0:T(8,128)(2,1)}, u32[]{:S(2)}, u32[]{:S(2)}) async-start(bf16[16,32,1024]{2,1,0:T(8,128)(2,1)} %shard_map.140), calls=%async_computation.2 | async-start | bytes 2097152 | tf_op jit(solution)/shard_map/all_to_all | solution.py:331
  204.0 5.0 %collective-permute-start.11 = (bf16[16,4096]{1,0:T(8,128)(2,1)S(1)}, bf16[16,4096]{1,0:T(8,128)(2,1)S(1)}, u32[]{:S(2)}, u32[]{:S(2)}) collective-permute-start(bf16[16,4096]{1,0:T(8,128)(2,1)S(1)} %get-tuple-element.70), channel_id=1, source_target_pairs={{0,192},{64,0},{128,64},{192,128},{1,193},{65,1},{129,65},{193,129... | collective-permute-start | bytes 393224 | tf_op jit(solution)/shard_map/ppermute | solution.py:315
  214.6 5.4 %collective-permute-start.12 = (bf16[16,4096]{1,0:T(8,128)(2,1)S(1)}, bf16[16,4096]{1,0:T(8,128)(2,1)S(1)}, u32[]{:S(2)}, u32[]{:S(2)}) collective-permute-start(bf16[16,4096]{1,0:T(8,128)(2,1)S(1)} %get-tuple-element.71), channel_id=1, source_target_pairs={{0,192},{64,0},{128,64},{192,128},{1,193},{65,1},{129,65},{193,129... | collective-permute-start | bytes 393224 | tf_op jit(solution)/shard_map/ppermute | solution.py:315
  244.5 36.7 %all-to-all-start.4 = ((bf16[16,32,1024]{2,1,0:T(8,128)(2,1)}), bf16[16,32,1024]{2,1,0:T(8,128)(2,1)S(1)}, u32[]{:S(2)}, u32[]{:S(2)}) async-start(bf16[16,32,1024]{2,1,0:T(8,128)(2,1)} %shard_map.145), calls=%async_computation.4 | async-start | bytes 2097152 | tf_op jit(solution)/shard_map/all_to_all | solution.py:335
  281.4 6.8 %collective-permute-start.13 = (bf16[2,32,1024]{2,1,0:T(8,128)(2,1)S(1)}, bf16[2,32,1024]{2,1,0:T(8,128)(2,1)S(1)}, u32[]{:S(2)}, u32[]{:S(2)}) collective-permute-start(bf16[2,32,1024]{2,1,0:T(8,128)(2,1)S(1)} %pad_maximum_fusion.2), channel_id=1, source_target_pairs={{64,0},{128,64},{192,128},{0,192},{65,1},{129,65},{193,129},{1,193... | collective-permute-start | bytes 393224 | tf_op jit(solution)/shard_map/ppermute | solution.py:202
  284.9 5.4 %collective-permute-start.14 = (bf16[2,32,1024]{2,1,0:T(8,128)(2,1)S(1)}, bf16[2,32,1024]{2,1,0:T(8,128)(2,1)S(1)}, u32[]{:S(2)}, u32[]{:S(2)}) collective-permute-start(bf16[2,32,1024]{2,1,0:T(8,128)(2,1)S(1)} %pad_maximum_fusion.2), channel_id=1, source_target_pairs={{128,0},{192,64},{0,128},{64,192},{129,1},{193,65},{1,129},{65,193... | collective-permute-start | bytes 393224 | tf_op jit(solution)/shard_map/ppermute | solution.py:202
  284.9 6.4 %collective-permute-start.15 = (bf16[2,32,1024]{2,1,0:T(8,128)(2,1)S(1)}, bf16[2,32,1024]{2,1,0:T(8,128)(2,1)S(1)}, u32[]{:S(2)}, u32[]{:S(2)}) collective-permute-start(bf16[2,32,1024]{2,1,0:T(8,128)(2,1)S(1)} %pad_maximum_fusion.2), channel_id=1, source_target_pairs={{192,0},{0,64},{64,128},{128,192},{193,1},{1,65},{65,129},{129,193... | collective-permute-start | bytes 393224 | tf_op jit(solution)/shard_map/ppermute | solution.py:202
  (23 other events, 155.5 us)
Sparse Core Ops, SparseCore 0:
  11.4 87.2 all-gather.1
where the time goes:
time: 338 us; the launch traced here: 334 us
  waiting for transfers between devices  126 us (37%)
  Pallas kernels  66.9 us (20%)
  starting transfers between devices  63.7 us (19%)
  blocking collectives  47.5 us (14%)
  between operations  14.6 us (4%)
  local copies, waits for them, and re-layouts  6.8 us (2%)
  other arithmetic  5.43 us (2%)
  matrix products  3.8 us (1%)
    pallas_call x18, Pallas kernels, call(): pl.pallas_call(kernel, out_shape=out_shape, in_specs=specs, out_specs=jax...  66.9 us
    all_gather x1, waiting for transfers between devices, on_device(): lax.all_gather(mine.reshape(blocks * 2 * combos, width), DP, axis=0, tile...  64 us
    all_gather x3, blocking collectives, on_device(): got = lax.all_gather(held, axes, axis=0, tiled=True)  30.2 us
    ppermute x10, starting transfers between devices, on_device(): arriving = lax.ppermute(result, 's', pairs)  26.6 us
    all_to_all x1, waiting for transfers between devices, on_device(): late_got = lax.all_to_all(partial_grads(0, mixed), RANKS, 0, 0)  24.1 us
    ppermute x10, waiting for transfers between devices, on_device(): arriving = lax.ppermute(result, 's', pairs)  20.4 us
    all_to_all x1, blocking collectives, on_device(): mixed = lax.all_to_all(late, QUARTERS, 0, 0)  17.3 us
    all_to_all x1, starting transfers between devices, on_device(): mixed = lax.all_to_all(packed(1), QUARTERS, 0, 0)  9.9 us
  transfers between devices with their start and end apart: 21, of which 18 were waited for; matrix products, arithmetic and copies ran while one was open for 1% of the time, Pallas kernels for 9%

commit v1 on v0

v1 whole, which is shorter than its diff:
```python
import functools

import jax
import jax.numpy as jnp
from jax import lax
from jax.experimental import pallas as pl
from jax.experimental.pallas import tpu as pltpu
from jax.sharding import Mesh, PartitionSpec as P

eps = 1e-05
bf16 = jnp.bfloat16
f32 = jnp.float32

AXES = ("s", "x", "zh", "zl", "c")
DP = ("x", "zh", "zl", "c")
RANKS = ("x", "zh")
QUARTERS = ("zl", "c")
VMEM = pl.BlockSpec(memory_space=pltpu.VMEM)
SMEM = pl.BlockSpec(memory_space=pltpu.SMEM)
LAST = (((1,), (1,)), ((), ()))
FIRST = (((0,), (0,)), ((), ()))
VMEM_LIMIT = 4 * 1024 * 1024


def adapter_rows(g_ref, which, q):
    part = g_ref[:, q, which]
    return part.reshape(part.shape[0] * part.shape[1], part.shape[2])


def chosen_quarter(value, index, quarters):
    width = value.shape[1] // quarters
    part = value[:, :width]
    for q in range(1, quarters):
        part = jnp.where(index == q, value[:, q * width : (q + 1) * width], part)
    return part


def prep_kernel(where_ref, x_ref, xn_ref, inv_ref, *sent):
    items, rows, _ = x_ref.shape
    for item in range(items):
        values = x_ref[item].astype(f32)
        inv = lax.rsqrt(jnp.mean(values * values, axis=1, keepdims=True) + eps)
        inv_ref[item] = jnp.broadcast_to(inv, (rows, inv_ref.shape[2]))
        normed = (values * inv).astype(bf16)
        where = slice(item * rows, (item + 1) * rows)
        xn_ref[where, :] = normed
        for d, out_ref in enumerate(sent):
            out_ref[where, :] = chosen_quarter(normed, where_ref[1] ^ d, len(sent))


def low_kernel(block, xn_ref, weights_ref, g_ref, out_ref):
    tokens, _ = out_ref.shape
    quarters, width = g_ref.shape[1], g_ref.shape[4]
    low = jnp.zeros(out_ref.shape, f32)
    for q in range(quarters):
        low += lax.dot_general(
            xn_ref[block * tokens : (block + 1) * tokens, q * width : (q + 1) * width],
            adapter_rows(g_ref, 0, q),
            LAST,
            preferred_element_type=f32,
        )
    weights = weights_ref[block * tokens : (block + 1) * tokens, :]
    out_ref[...] = (weights * low).astype(bf16)


def tick_kernel(tick, sections, micros, where_ref, *refs):
    refs = list(refs)
    section = where_ref[0]
    if tick < micros:
        grad = refs.pop(0)[tick]
        if tick:
            cot = jnp.where(section == sections - 1, grad, refs.pop(0)[...])
        else:
            cot = grad
    else:
        cot = refs.pop(0)[...]
    x_ref, inv_ref, weights_ref = refs[:3]
    dx_ref, du_ref = refs[-2:]
    adapters = refs[3:-2]
    position = jnp.clip(tick - (sections - 1 - section), 0, x_ref.shape[0] - 1)

    def layer(block, g_ref, item):
        quarters, width = g_ref.shape[1], g_ref.shape[4]
        back = jnp.zeros(du_ref.shape, f32)
        for q in range(quarters):
            back += lax.dot_general(
                cot[:, q * width : (q + 1) * width],
                adapter_rows(g_ref, 1, q),
                LAST,
                preferred_element_type=f32,
            )
        du = (weights_ref[item] * back).astype(bf16)
        du_ref[...] = du
        inv = inv_ref[item][:, :1]
        dxn, xf = [], []
        total = jnp.zeros((du.shape[0], 1), f32)
        for q in range(quarters):
            xf.append(x_ref[item, :, q * width : (q + 1) * width].astype(f32) * inv)
            dxn.append(jnp.dot(du, adapter_rows(g_ref, 0, q), preferred_element_type=f32))
            total += jnp.sum(dxn[q] * xf[q], axis=1, keepdims=True)
        mean = total * (1.0 / (quarters * width))
        for q in range(quarters):
            cols = slice(q * width, (q + 1) * width)
            dx_ref[:, cols] = (
                cot[:, cols].astype(f32) + inv * (dxn[q] - xf[q] * mean)
            ).astype(bf16)

    if tick < micros:
        layer(1, adapters[0], micros + position)
    elif tick >= micros + sections - 1:
        layer(0, adapters[0], position - micros)
    else:
        pl.when(position < micros)(lambda: layer(1, adapters[0], micros + position))
        pl.when(position >= micros)(lambda: layer(0, adapters[1], position - micros))


def pack_kernel(micros, sections, fresh, where_ref, low_ref, *refs):
    spans = micros + sections - 1
    grad_ref, cots, dus, sent = refs[0], refs[1 : 1 + spans], refs[1 + spans : 1 + 2 * spans], refs[1 + 2 * spans :]
    rows, wide = dus[0].shape
    quarters = len(sent)
    width = cots[0].shape[1] // quarters
    section = where_ref[0]
    for m in range(micros):
        cot = grad_ref[m] if fresh else cots[m][...]
        du = dus[m][...]
        for s in range(sections - 1):
            at = m + sections - 1 - s
            cot = jnp.where(section == s, cots[at][...], cot)
            du = jnp.where(section == s, dus[at][...], du)
        where = slice(m * rows, (m + 1) * rows)
        for d, out_ref in enumerate(sent):
            out_ref[where, :width] = chosen_quarter(cot, where_ref[1] ^ d, quarters)
            out_ref[where, width : width + wide] = du
    for out_ref in sent:
        out_ref[:, width + wide :] = low_ref[...]


def grads_kernel(block, *refs):
    out_ref = refs[-1]
    quarters = len(refs) // 2
    xns = refs[quarters:-1]
    tokens, width = refs[0].shape[0], xns[0].shape[1]
    ranks, combos = out_ref.shape[0], out_ref.shape[1] // 2
    wide = ranks * combos
    xn = jnp.concatenate([ref[block * tokens : (block + 1) * tokens, :] for ref in xns])
    mixed = jnp.concatenate([ref[...] for ref in refs[:quarters]])
    dy = mixed[:, :width]
    du = mixed[:, width : width + wide]
    low = mixed[:, width + wide :]
    grad_a = lax.dot_general(du, xn, FIRST, preferred_element_type=f32)
    out_ref[:, :combos, :] = grad_a.astype(bf16).reshape(ranks, combos, width)
    grad_b = lax.dot_general(low, dy, FIRST, preferred_element_type=f32)
    out_ref[:, combos:, :] = grad_b.astype(bf16).reshape(ranks, combos, width)


def generate_kernel(cond_ref, down_ref, up_ref, out_ref):
    blocks, _, combos, _ = out_ref.shape
    cond = cond_ref[...]
    first = cond.astype(bf16)
    rest = cond - first.astype(f32)
    second = rest.astype(bf16)
    third = (rest - second.astype(f32)).astype(bf16)
    parts = jnp.concatenate([first, second, third])
    rows = cond.shape[0]
    for which, gen_ref in enumerate((down_ref, up_ref)):
        made = jnp.dot(parts, gen_ref[...], preferred_element_type=f32)
        made = made[:rows] + (made[rows : 2 * rows] + made[2 * rows :])
        out_ref[:, which] = made.astype(bf16).reshape(blocks, combos, -1)


def call(kernel, out_shape, operands, flops, moved):
    scalars = 1 if operands[0].dtype == jnp.int32 else 0
    return pl.pallas_call(
        kernel,
        out_shape=out_shape,
        in_specs=[SMEM] * scalars + [VMEM] * (len(operands) - scalars),
        out_specs=jax.tree.map(lambda _: VMEM, out_shape),
        compiler_params=pltpu.CompilerParams(vmem_limit_bytes=VMEM_LIMIT),
        cost_estimate=pl.CostEstimate(flops=flops, bytes_accessed=moved, transcendentals=0),
    )(*operands)


def swapped(parts, axes):
    count = lax.axis_size(axes)
    return [parts[0]] + [
        lax.ppermute(parts[d], axes, [(i, i ^ d) for i in range(count)])
        for d in range(1, count)
    ]


def from_sections(part):
    count = lax.axis_size("s")
    got = [part] + [
        lax.ppermute(part, "s", [((i + d) % count, i) for i in range(count)])
        for d in range(1, count)
    ]
    me = lax.axis_index("s")
    return jnp.stack([lax.select_n(lax.rem(i + count - me, count), *got) for i in range(count)])


def on_device(
    hidden_in, out_grad, gate_probs, expert_ids, task_ids, task_embed, slot_embed, gen_down, gen_up
):
    high = lax.Precision.HIGHEST
    sections = lax.axis_size("s")
    section_id = lax.axis_index("s")
    quarters = lax.axis_size(QUARTERS)
    ranks = lax.axis_size(RANKS)
    blocks, _, micros, rows, model = hidden_in.shape
    tasks, cond_width = task_embed.shape
    experts = slot_embed.shape[2]
    combos = tasks * experts
    width = model // quarters
    wide = ranks * combos
    items = blocks * micros
    tokens = micros * rows
    where = jnp.stack([section_id, lax.axis_index(QUARTERS)]).astype(jnp.int32)

    def shaped(*shape, dtype=bf16):
        return jax.ShapeDtypeStruct(shape, dtype)

    pre = task_embed[None, :, None, :] + slot_embed[:, 0][:, None, :, :]
    cond = jax.nn.silu(pre).reshape(blocks, combos, cond_width)
    mine = call(
        generate_kernel,
        shaped(blocks, 2, combos, width),
        (cond.reshape(blocks * combos, cond_width), gen_down, gen_up),
        12 * blocks * combos * cond_width * width,
        5 << 18,
    )
    filled = lax.all_gather(mine.reshape(blocks * 2 * combos, width), DP, axis=0, tiled=True)

    slots = from_sections(slot_embed[:, 0])
    x_items = hidden_in[:, 0].reshape(items, rows, model)
    normed, inv_items, *sent = call(
        prep_kernel,
        [shaped(items * rows, model), shaped(items, rows, 128, dtype=f32)]
        + [shaped(items * rows, width)] * quarters,
        (where, x_items),
        8 * items * rows * model,
        3 << 20,
    )
    normed_quarter = swapped(sent, QUARTERS)
    lane = jnp.arange(wide, dtype=jnp.int32)
    expert_of, task_of = lane % experts, (lane // experts) % tasks
    ids, gates = expert_ids[:, 0], gate_probs[:, 0]
    weights = jnp.where(ids[..., 0:1] == expert_of, gates[..., 0:1], 0.0) + jnp.where(
        ids[..., 1:2] == expert_of, gates[..., 1:2], 0.0
    )
    weights = jnp.where(task_ids[None, :, :, None] == task_of, weights, 0.0)
    weights_items = weights.reshape(items, rows, wide)

    filled, slots, normed, inv_items, normed_quarter, weights_items = lax.optimization_barrier(
        (filled, slots, normed, inv_items, normed_quarter, weights_items)
    )
    adapters = filled.reshape(ranks, quarters, blocks, 2, combos, width)
    adapters = [adapters[:, :, j] for j in range(blocks)]
    pairs = [(i, (i - 1) % sections) for i in range(sections)]
    last = items + sections - 2

    def low_of(block):
        return call(
            functools.partial(low_kernel, block),
            shaped(tokens, wide),
            (normed, weights_items.reshape(blocks * tokens, wide), adapters[block]),
            2 * tokens * wide * model,
            3 << 20,
        )

    def exchanged(block, low):
        span = slice((blocks - 1 - block) * micros, (blocks - block) * micros + sections - 1)
        fresh = block == blocks - 1
        cots = [out_grad[0] if cot is None else cot for cot in incoming[span]]
        parts = call(
            functools.partial(pack_kernel, micros, sections, fresh),
            [shaped(tokens, width + 2 * wide)] * quarters,
            (where, low, out_grad, *cots, *dus[span]),
            0,
            3 << 20,
        )
        return swapped(parts, QUARTERS)

    def partial_grads(block, mixed):
        return call(
            functools.partial(grads_kernel, block),
            shaped(ranks, 2 * combos, width),
            (*mixed, *normed_quarter),
            4 * quarters * tokens * wide * width,
            5 << 20,
        )

    def summed(got):
        scale = 1.0 / (micros * rows * lax.axis_size(DP))
        return (jnp.sum(got.astype(f32), axis=0) * scale).astype(bf16)

    def rank_rows(part):
        part = part.reshape(lax.axis_size("x"), -1, *part.shape[1:])
        got = lax.all_to_all(part, "x", 0, 0)
        part = jnp.sum(got.astype(f32), axis=0).astype(bf16)
        return lax.all_to_all(part, "zh", 0, 0)

    incoming, dus, results = [None], [], []
    for tick in range(last + 1):
        operands = [where]
        if tick < micros:
            operands.append(out_grad)
        if tick:
            operands.append(incoming[tick])
        if tick < micros:
            used = [adapters[1]]
        elif tick >= micros + sections - 1:
            used = [adapters[0]]
        else:
            used = [adapters[1], adapters[0]]
        result, du = call(
            functools.partial(tick_kernel, tick, sections, micros),
            [shaped(rows, model), shaped(rows, wide)],
            (*operands, x_items, inv_items, weights_items, *used),
            4 * rows * wide * model,
            5 << 20,
        )
        results.append(result)
        dus.append(du)
        if tick == last:
            break
        arriving = lax.ppermute(result, "s", pairs)
        if tick == 1:
            low_first = low_of(1)
            arriving, low_first = lax.optimization_barrier((arriving, low_first))
        if tick == 4:
            low_second = low_of(0)
            arriving, low_second = lax.optimization_barrier((arriving, low_second))
        if tick == micros + sections - 2:
            mixed = exchanged(1, low_first)
        if tick == micros + sections - 1:
            early = partial_grads(1, mixed)
            arriving, early = lax.optimization_barrier((arriving, early))
            early_got = lax.all_to_all(early, RANKS, 0, 0)
        incoming.append(arriving)
    mixed = exchanged(0, low_second)
    mixed[0], early_got = lax.optimization_barrier((mixed[0], early_got))
    late_got = rank_rows(partial_grads(0, mixed))

    hidden_out = jnp.stack(
        [
            lax.select_n(
                section_id,
                *[results[micros + m + sections - 1 - s] for s in range(sections)],
            )
            for m in range(micros)
        ]
    )
    hidden_out, late_got = lax.optimization_barrier((hidden_out, late_got))
    reduced = jnp.stack([summed(late_got), summed(early_got)])
    pre_all = task_embed[None, None, :, None, :] + slots[:, :, None, :, :]
    cond_all = jax.nn.silu(pre_all).reshape(sections * blocks * combos, cond_width)
    grads = from_sections(reduced).reshape(sections * blocks, 2, combos, width)
    grad_a = grads[:, 0].reshape(-1, width)
    grad_b = grads[:, 1].reshape(-1, width)
    d_cond = jnp.einsum("nf,wf->nw", grad_a, gen_down, preferred_element_type=f32)
    d_cond = d_cond + jnp.einsum("nf,wf->nw", grad_b, gen_up, preferred_element_type=f32)
    gate = jax.nn.sigmoid(pre_all)
    d_pre = d_cond.reshape(pre_all.shape) * gate * (1.0 + pre_all * (1.0 - gate))
    own = lax.dynamic_index_in_dim(d_pre, section_id, 0, keepdims=False)
    d_slot = jnp.sum(own, axis=1).reshape(blocks * experts, cond_width)
    d_task = jnp.sum(d_pre, axis=(0, 1, 3))
    small = jnp.concatenate([d_slot, d_task])
    held = small.reshape(-1, 128)
    held = jnp.pad(held, ((0, -held.shape[0] % 8), (0, 0)))
    got = lax.all_gather(held, QUARTERS, axis=0, tiled=True)
    held = jnp.sum(got.reshape(-1, *held.shape), axis=0)
    held = jnp.broadcast_to(held[None], (ranks, *held.shape))
    held = jnp.sum(lax.all_to_all(held, RANKS, 0, 0), axis=0)
    small = held[: small.size // 128].reshape(small.shape)
    d_slot = small[: blocks * experts].reshape(blocks, 1, experts, cond_width)
    d_task = small[blocks * experts :]
    d_gen_down = jnp.einsum("nw,nf->wf", cond_all, grad_a.astype(f32), precision=high)
    d_gen_up = jnp.einsum("nw,nf->wf", cond_all, grad_b.astype(f32), precision=high)
    return (hidden_out[None], d_gen_down, d_gen_up, d_task, d_slot)


def solution(mesh):
    split = Mesh(mesh.devices.reshape(mesh.devices.shape[0], 4, 4, 2, 2), AXES)
    placed = (
        P(None, "s", None, DP, None),
        P(None, DP, None),
        P(None, "s", None, DP, None),
        P(None, "s", None, DP, None),
        P(None, DP),
        P(),
        P(None, "s", None, None),
        P(None, DP),
        P(None, DP),
    )
    return jax.shard_map(
        on_device,
        mesh=split,
        in_specs=placed,
        out_specs=(
            P("s", None, DP, None),
            P(None, DP),
            P(None, DP),
            P(),
            P(None, "s", None, None),
        ),
        check_vma=False,
    )
```

time: 338 us -> 309 us (0.914)
  blocking collectives: 47.5 us -> 10.1 us
  Pallas kernels: 66.9 us -> 33.2 us
  starting transfers between devices: 63.7 us -> 80.7 us
  waiting for transfers between devices: 126 us -> 139 us
  local copies, waits for them, and re-layouts: 6.8 us -> 15.3 us
    pallas_call x18 -> x19, Pallas kernels: 66.9 us -> 33.2 us  [call(): pl.pallas_call(kernel, out_shape=out_shape, in_specs=[SMEM] * scalars + [...]
    all_gather x3 -> x1, blocking collectives: 30.2 us -> 10.1 us  [on_device(): got = lax.all_gather(held, QUARTERS, axis=0, tiled=True)]
    ppermute x0 -> x9, starting transfers between devices: none -> 19.5 us  [swapped(): lax.ppermute(parts[d], axes, [(i, i ^ d) for i in range(count)])]
    ppermute x0 -> x9, waiting for transfers between devices: none -> 18.2 us  [swapped(): lax.ppermute(parts[d], axes, [(i, i ^ d) for i in range(count)])]
    all_to_all x1 -> x0, blocking collectives: 17.3 us -> none  [on_device(): mixed = lax.all_to_all(late, QUARTERS, 0, 0)]
    all_to_all x3, starting transfers between devices: 25.9 us -> 14.6 us  [the longest x1 6.47 us: rank_rows(): return lax.all_to_all(part, 'zh', 0, 0)]
    ppermute x10, starting transfers between devices: 26.6 us -> 32.8 us  [on_device(): arriving = lax.ppermute(result, 's', pairs)]
    squeeze x1 -> x2, local copies, waits for them, and re-layouts: 0.01 us -> 4.06 us  [the longest x1 4.05 us: on_device(): adapters = [adapters[:, :, j] for j in range(blocks)]]
  transfers between devices with their start and end apart: 21 -> 30, of which waited for: 18 -> 20; matrix products, arithmetic and copies ran while one was open for 1% -> 3% of each run, Pallas kernels for 9% -> 5%
where the time goes in v1:
time: 309 us; the launch traced here: 303 us
  waiting for transfers between devices  139 us (45%)
  starting transfers between devices  80.7 us (26%)
  Pallas kernels  33.2 us (11%)
  local copies, waits for them, and re-layouts  15.3 us (5%)
  between operations  14.9 us (5%)
  blocking collectives  10.1 us (3%)
  other arithmetic  6.72 us (2%)
  matrix products  3.8 us (1%)
    all_gather x1, waiting for transfers between devices, on_device(): lax.all_gather(mine.reshape(blocks * 2 * combos, width), DP, axis=0, tile...  62.8 us
    pallas_call x19, Pallas kernels, call(): pl.pallas_call(kernel, out_shape=out_shape, in_specs=[SMEM] * scalars + [...  33.2 us
    ppermute x10, starting transfers between devices, on_device(): arriving = lax.ppermute(result, 's', pairs)  32.8 us
    ppermute x10, waiting for transfers between devices, on_device(): arriving = lax.ppermute(result, 's', pairs)  21.2 us
    ppermute x9, starting transfers between devices, swapped(): lax.ppermute(parts[d], axes, [(i, i ^ d) for i in range(count)])  19.5 us
    ppermute x9, waiting for transfers between devices, swapped(): lax.ppermute(parts[d], axes, [(i, i ^ d) for i in range(count)])  18.2 us
    all_to_all x1, waiting for transfers between devices, rank_rows(): got = lax.all_to_all(part, 'x', 0, 0)  14.4 us
    all_gather x1, blocking collectives, on_device(): got = lax.all_gather(held, QUARTERS, axis=0, tiled=True)  10.1 us
  transfers between devices with their start and end apart: 30, of which 20 were waited for; matrix products, arithmetic and copies ran while one was open for 3% of the time, Pallas kernels for 5%

profile of v1, /device:TPU:1, one launch (start us, length us, event | category | flops | bytes accessed | tf_op | source)
XLA Modules:
  0.0 303.1 jit_solution(7608325581713198161)
XLA Ops:
  11.0 3.6 %collective-permute-start = (f32[2,8,256]{2,1,0:T(8,128)}, f32[2,8,256]{2,1,0:T(8,128)S(1)}, u32[]{:S(2)}, u32[]{:S(2)}) collective-permute-start(f32[2,8,256]{2,1,0:T(8,128)} %bitcast.111), channel_id=1, source_target_pairs={{64,0},{128,64},{192,128},{0,192},{65,1},{129,65},{193,129},{1,193... | collective-permute-start | bytes 49160 | tf_op jit(solution)/shard_map/ppermute | solution.py:195
  28.6 6.3 %collective-permute-done.5.refs_7_ = bf16[128,1024]{1,0:T(8,128)(2,1)S(1)} collective-permute-done((bf16[128,1024]{1,0:T(8,128)(2,1)S(1)}, bf16[128,1024]{1,0:T(8,128)(2,1)S(1)}, u32[]{:S(2)}, u32[]{:S(2)}) %collective-permute-start.5) | collective-permute-done | bytes 262176 | tf_op jit(solution)/shard_map/ppermute | solution.py:187
  35.6 62.8 %all-gather.2.cloned.1.call-done = bf16[4096,1024]{1,0:T(8,128)(2,1)} async-done(((bf16[64,1024]{1,0:T(8,128)(2,1)}), bf16[4096,1024]{1,0:T(8,128)(2,1)}) %all-gather.2.cloned.1.call-update) | async-done | bytes 8388624 | tf_op jit(solution)/shard_map/all_gather | solution.py:232
  98.4 4.1 %slice_bitcast_fusion = (bf16[16,4,2,16,1024]{4,3,2,1,0:T(8,128)(2,1)S(1)}, bf16[16,4,2,16,1024]{4,3,2,1,0:T(8,128)(2,1)S(1)}) fusion(bf16[16,4,2,2,16,1024]{5,4,3,2,1,0:T(8,128)(2,1)} %bitcast.99), kind=kLoop, calls=%fused_computation | loop fusion | bytes 16777216 | tf_op jit(solution)/shard_map/squeeze | solution.py:258
  112.2 3.5 %collective-permute-start.7 = (bf16[16,4096]{1,0:T(8,128)(2,1)S(1)}, bf16[16,4096]{1,0:T(8,128)(2,1)S(1)}, u32[]{:S(2)}, u32[]{:S(2)}) collective-permute-start(bf16[16,4096]{1,0:T(8,128)(2,1)S(1)} %get-tuple-element.70), channel_id=1, source_target_pairs={{0,192},{64,0},{128,64},{192,128},{1,193},{65,1},{129,65},{193,129... | collective-permute-start | bytes 393224 | tf_op jit(solution)/shard_map/ppermute | solution.py:327
  119.8 3.2 %collective-permute-start.8 = (bf16[16,4096]{1,0:T(8,128)(2,1)S(1)}, bf16[16,4096]{1,0:T(8,128)(2,1)S(1)}, u32[]{:S(2)}, u32[]{:S(2)}) collective-permute-start(bf16[16,4096]{1,0:T(8,128)(2,1)S(1)} %get-tuple-element.73), channel_id=1, source_target_pairs={{0,192},{64,0},{128,64},{192,128},{1,193},{65,1},{129,65},{193,129... | collective-permute-start | bytes 393224 | tf_op jit(solution)/shard_map/ppermute | solution.py:327
  127.2 3.4 %collective-permute-start.9 = (bf16[16,4096]{1,0:T(8,128)(2,1)S(1)}, bf16[16,4096]{1,0:T(8,128)(2,1)S(1)}, u32[]{:S(2)}, u32[]{:S(2)}) collective-permute-start(bf16[16,4096]{1,0:T(8,128)(2,1)S(1)} %get-tuple-element.74), channel_id=1, source_target_pairs={{0,192},{64,0},{128,64},{192,128},{1,193},{65,1},{129,65},{193,129... | collective-permute-start | bytes 393224 | tf_op jit(solution)/shard_map/ppermute | solution.py:327
  134.8 3.2 %collective-permute-start.10 = (bf16[16,4096]{1,0:T(8,128)(2,1)S(1)}, bf16[16,4096]{1,0:T(8,128)(2,1)S(1)}, u32[]{:S(2)}, u32[]{:S(2)}) collective-permute-start(bf16[16,4096]{1,0:T(8,128)(2,1)S(1)} %get-tuple-element.75), channel_id=1, source_target_pairs={{0,192},{64,0},{128,64},{192,128},{1,193},{65,1},{129,65},{193,129... | collective-permute-start | bytes 393224 | tf_op jit(solution)/shard_map/ppermute | solution.py:327
  153.5 7.3 %collective-permute-start.14 = (bf16[64,1536]{1,0:T(8,128)(2,1)S(1)}, bf16[64,1536]{1,0:T(8,128)(2,1)S(1)}, u32[]{:S(2)}, u32[]{:S(2)}) collective-permute-start(bf16[64,1536]{1,0:T(8,128)(2,1)S(1)} %get-tuple-element.89), channel_id=1, source_target_pairs={{0,1},{1,0},{2,3},{3,2},{4,5},{5,4},{6,7},{7,6},{8,9},{9,8},{10,11... | collective-permute-start | bytes 589832 | tf_op jit(solution)/shard_map/ppermute | solution.py:187
  164.7 9.1 %collective-permute-start.13 = (bf16[16,4096]{1,0:T(8,128)(2,1)S(1)}, bf16[16,4096]{1,0:T(8,128)(2,1)S(1)}, u32[]{:S(2)}, u32[]{:S(2)}) collective-permute-start(bf16[16,4096]{1,0:T(8,128)(2,1)S(1)} %get-tuple-element.79), channel_id=1, source_target_pairs={{0,192},{64,0},{128,64},{192,128},{1,193},{65,1},{129,65},{193,129... | collective-permute-start | bytes 393224 | tf_op jit(solution)/shard_map/ppermute | solution.py:327
  175.3 3.4 %collective-permute-done.13.refs_0_.refs_5_ = bf16[16,4096]{1,0:T(8,128)(2,1)S(1)} collective-permute-done((bf16[16,4096]{1,0:T(8,128)(2,1)S(1)}, bf16[16,4096]{1,0:T(8,128)(2,1)S(1)}, u32[]{:S(2)}, u32[]{:S(2)}) %collective-permute-start.13) | collective-permute-done | bytes 131104 | tf_op jit(solution)/shard_map/ppermute | solution.py:327
  178.7 4.9 %all-to-all-start = ((bf16[16,32,1024]{2,1,0:T(8,128)(2,1)}), bf16[16,32,1024]{2,1,0:T(8,128)(2,1)}, u32[]{:S(2)}, u32[]{:S(2)}) async-start(bf16[16,32,1024]{2,1,0:T(8,128)(2,1)} %shard_map.141), calls=%async_computation | async-start | bytes 2097152 | tf_op jit(solution)/shard_map/all_to_all | solution.py:339
  188.3 4.1 %collective-permute-done.17.refs_0_.refs_6_ = bf16[16,4096]{1,0:T(8,128)(2,1)S(1)} collective-permute-done((bf16[16,4096]{1,0:T(8,128)(2,1)S(1)}, bf16[16,4096]{1,0:T(8,128)(2,1)S(1)}, u32[]{:S(2)}, u32[]{:S(2)}) %collective-permute-start.17) | collective-permute-done | bytes 131104 | tf_op jit(solution)/shard_map/ppermute | solution.py:327
  203.3 5.4 %collective-permute-start.19 = (bf16[64,1536]{1,0:T(8,128)(2,1)}, bf16[64,1536]{1,0:T(8,128)(2,1)S(1)}, u32[]{:S(2)}, u32[]{:S(2)}) collective-permute-start(bf16[64,1536]{1,0:T(8,128)(2,1)} %get-tuple-element.108), channel_id=1, source_target_pairs={{0,1},{1,0},{2,3},{3,2},{4,5},{5,4},{6,7},{7,6},{8,9},{9,8},{10,11... | collective-permute-start | bytes 589832 | tf_op jit(solution)/shard_map/ppermute | solution.py:187
  210.4 5.2 %collective-permute-done.20.refs_2_ = bf16[64,1536]{1,0:T(8,128)(2,1)S(1)} collective-permute-done((bf16[64,1536]{1,0:T(8,128)(2,1)}, bf16[64,1536]{1,0:T(8,128)(2,1)S(1)}, u32[]{:S(2)}, u32[]{:S(2)}) %collective-permute-start.20) | collective-permute-done | bytes 196640 | tf_op jit(solution)/shard_map/ppermute | solution.py:187
  215.6 4.2 %collective-permute-done.21.refs_3_ = bf16[64,1536]{1,0:T(8,128)(2,1)S(1)} collective-permute-done((bf16[64,1536]{1,0:T(8,128)(2,1)}, bf16[64,1536]{1,0:T(8,128)(2,1)S(1)}, u32[]{:S(2)}, u32[]{:S(2)}) %collective-permute-start.21) | collective-permute-done | bytes 196640 | tf_op jit(solution)/shard_map/ppermute | solution.py:187
  221.2 4.4 %all-to-all-start.1 = ((bf16[4,4,32,1024]{3,2,1,0:T(8,128)(2,1)}), bf16[4,4,32,1024]{3,2,1,0:T(8,128)(2,1)S(1)}, u32[]{:S(2)}, u32[]{:S(2)}) async-start(bf16[4,4,32,1024]{3,2,1,0:T(8,128)(2,1)} %bitcast.26), calls=%async_computation.1 | async-start | bytes 2097152 | tf_op jit(solution)/shard_map/all_to_all | solution.py:299
  225.8 14.4 %all-to-all-done.1 = bf16[4,4,32,1024]{3,2,1,0:T(8,128)(2,1)S(1)} async-done(((bf16[4,4,32,1024]{3,2,1,0:T(8,128)(2,1)}), bf16[4,4,32,1024]{3,2,1,0:T(8,128)(2,1)S(1)}, u32[]{:S(2)}, u32[]{:S(2)}) %all-to-all-start.1) | async-done | bytes 1048608 | tf_op jit(solution)/shard_map/all_to_all | solution.py:299
  241.1 6.5 %all-to-all-start.2 = ((bf16[4,32,1024]{2,1,0:T(8,128)(2,1)}), bf16[4,32,1024]{2,1,0:T(8,128)(2,1)S(1)}, u32[]{:S(2)}, u32[]{:S(2)}) async-start(bf16[4,32,1024]{2,1,0:T(8,128)(2,1)} %reduce_sum.66), calls=%async_computation.2 | async-start | bytes 524288 | tf_op jit(solution)/shard_map/all_to_all | solution.py:301
  249.9 6.3 %all-to-all-done.2 = bf16[4,32,1024]{2,1,0:T(8,128)(2,1)S(1)} async-done(((bf16[4,32,1024]{2,1,0:T(8,128)(2,1)}), bf16[4,32,1024]{2,1,0:T(8,128)(2,1)S(1)}, u32[]{:S(2)}, u32[]{:S(2)}) %all-to-all-start.2) | async-done | bytes 262176 | tf_op jit(solution)/shard_map/all_to_all | solution.py:301
  256.3 3.4 %collective-permute-start.22 = (bf16[2,32,1024]{2,1,0:T(8,128)(2,1)S(1)}, bf16[2,32,1024]{2,1,0:T(8,128)(2,1)S(1)}, u32[]{:S(2)}, u32[]{:S(2)}) collective-permute-start(bf16[2,32,1024]{2,1,0:T(8,128)(2,1)S(1)} %pad_maximum_fusion.2), channel_id=1, source_target_pairs={{64,0},{128,64},{192,128},{0,192},{65,1},{129,65},{193,129},{1,193... | collective-permute-start | bytes 393224 | tf_op jit(solution)/shard_map/ppermute | solution.py:195
  267.2 10.1 %all_gather.7 = f32[160,128]{1,0:T(8,128)S(1)} all-gather(f32[40,128]{1,0:T(8,128)S(1)} %pad.4), channel_id=1, replica_groups=mesh['s'=4,'x'=4,'zh'=4,'zl'=2,'c'=2] {'zl','c'}, dimensions={0}, use_global_device_ids=true | all-gather | bytes 102400 | tf_op jit(solution)/shard_map/all_gather | solution.py:371
  278.0 3.8 %all-to-all-start.3 = ((f32[16,40,128]{2,1,0:T(8,128)}), f32[16,40,128]{2,1,0:T(8,128)S(1)}, u32[]{:S(2)}, u32[]{:S(2)}) async-start(f32[16,40,128]{2,1,0:T(8,128)} %broadcast_in_dim.61), calls=%async_computation.3 | async-start | bytes 655360 | tf_op jit(solution)/shard_map/all_to_all | solution.py:374
  285.0 9.8 %all-to-all-done.3 = f32[16,40,128]{2,1,0:T(8,128)S(1)} async-done(((f32[16,40,128]{2,1,0:T(8,128)}), f32[16,40,128]{2,1,0:T(8,128)S(1)}, u32[]{:S(2)}, u32[]{:S(2)}) %all-to-all-start.3) | async-done | bytes 327712 | tf_op jit(solution)/shard_map/all_to_all | solution.py:374
  (161 shorter events, 95.9 us)
Async XLA Ops:
  7.2 91.3 %all-gather.2.cloned.1.call-start = ((), (), s32[]{:S(2)}) async-start(), calls=%async_computation.4 | async-start | bytes 8519680 | tf_op jit(solution)/shard_map/all_gather | solution.py:232
  11.0 12.9 %collective-permute-start = (f32[2,8,256]{2,1,0:T(8,128)}, f32[2,8,256]{2,1,0:T(8,128)S(1)}, u32[]{:S(2)}, u32[]{:S(2)}) collective-permute-start(f32[2,8,256]{2,1,0:T(8,128)} %bitcast.111), channel_id=1, source_target_pairs={{64,0},{128,64},{192,128},{0,192},{65,1},{129,65},{193,129},{1,193... | collective-permute-start | bytes 49160 | tf_op jit(solution)/shard_map/ppermute | solution.py:195
  14.7 9.4 %collective-permute-start.1 = (f32[2,8,256]{2,1,0:T(8,128)}, f32[2,8,256]{2,1,0:T(8,128)S(1)}, u32[]{:S(2)}, u32[]{:S(2)}) collective-permute-start(f32[2,8,256]{2,1,0:T(8,128)} %bitcast.112), channel_id=1, source_target_pairs={{128,0},{192,64},{0,128},{64,192},{129,1},{193,65},{1,129},{65,193... | collective-permute-start | bytes 49160 | tf_op jit(solution)/shard_map/ppermute | solution.py:195
  15.0 9.1 %collective-permute-start.2 = (f32[2,8,256]{2,1,0:T(8,128)}, f32[2,8,256]{2,1,0:T(8,128)S(1)}, u32[]{:S(2)}, u32[]{:S(2)}) collective-permute-start(f32[2,8,256]{2,1,0:T(8,128)} %bitcast.113), channel_id=1, source_target_pairs={{192,0},{0,64},{64,128},{128,192},{193,1},{1,65},{65,129},{129,193... | collective-permute-start | bytes 49160 | tf_op jit(solution)/shard_map/ppermute | solution.py:195
  18.1 7.3 %collective-permute-start.3 = (bf16[128,1024]{1,0:T(8,128)(2,1)S(1)}, bf16[128,1024]{1,0:T(8,128)(2,1)S(1)}, u32[]{:S(2)}, u32[]{:S(2)}) collective-permute-start(bf16[128,1024]{1,0:T(8,128)(2,1)S(1)} %get-tuple-element.63), channel_id=1, source_target_pairs={{0,1},{1,0},{2,3},{3,2},{4,5},{5,4},{6,7},{7,6},{8,9},{9,8},{10,11... | collective-permute-start | bytes 786440 | tf_op jit(solution)/shard_map/ppermute | solution.py:187
  19.7 8.2 %collective-permute-start.4 = (bf16[128,1024]{1,0:T(8,128)(2,1)S(1)}, bf16[128,1024]{1,0:T(8,128)(2,1)S(1)}, u32[]{:S(2)}, u32[]{:S(2)}) collective-permute-start(bf16[128,1024]{1,0:T(8,128)(2,1)S(1)} %get-tuple-element.64), channel_id=1, source_target_pairs={{0,2},{1,3},{2,0},{3,1},{4,6},{5,7},{6,4},{7,5},{8,10},{9,11},{10,... | collective-permute-start | bytes 786440 | tf_op jit(solution)/shard_map/ppermute | solution.py:187
  23.9 11.0 %collective-permute-start.5 = (bf16[128,1024]{1,0:T(8,128)(2,1)S(1)}, bf16[128,1024]{1,0:T(8,128)(2,1)S(1)}, u32[]{:S(2)}, u32[]{:S(2)}) collective-permute-start(bf16[128,1024]{1,0:T(8,128)(2,1)S(1)} %get-tuple-element.65), channel_id=1, source_target_pairs={{0,3},{1,2},{2,1},{3,0},{4,7},{5,6},{6,5},{7,4},{8,11},{9,10},{10,... | collective-permute-start | bytes 786440 | tf_op jit(solution)/shard_map/ppermute | solution.py:187
  112.2 5.4 %collective-permute-start.7 = (bf16[16,4096]{1,0:T(8,128)(2,1)S(1)}, bf16[16,4096]{1,0:T(8,128)(2,1)S(1)}, u32[]{:S(2)}, u32[]{:S(2)}) collective-permute-start(bf16[16,4096]{1,0:T(8,128)(2,1)S(1)} %get-tuple-element.70), channel_id=1, source_target_pairs={{0,192},{64,0},{128,64},{192,128},{1,193},{65,1},{129,65},{193,129... | collective-permute-start | bytes 393224 | tf_op jit(solution)/shard_map/ppermute | solution.py:327
  127.2 5.4 %collective-permute-start.9 = (bf16[16,4096]{1,0:T(8,128)(2,1)S(1)}, bf16[16,4096]{1,0:T(8,128)(2,1)S(1)}, u32[]{:S(2)}, u32[]{:S(2)}) collective-permute-start(bf16[16,4096]{1,0:T(8,128)(2,1)S(1)} %get-tuple-element.74), channel_id=1, source_target_pairs={{0,192},{64,0},{128,64},{192,128},{1,193},{65,1},{129,65},{193,129... | collective-permute-start | bytes 393224 | tf_op jit(solution)/shard_map/ppermute | solution.py:327
  149.6 12.9 %collective-permute-start.12 = (bf16[16,4096]{1,0:T(8,128)(2,1)S(1)}, bf16[16,4096]{1,0:T(8,128)(2,1)S(1)}, u32[]{:S(2)}, u32[]{:S(2)}) collective-permute-start(bf16[16,4096]{1,0:T(8,128)(2,1)S(1)} %get-tuple-element.78), channel_id=1, source_target_pairs={{0,192},{64,0},{128,64},{192,128},{1,193},{65,1},{129,65},{193,129... | collective-permute-start | bytes 393224 | tf_op jit(solution)/shard_map/ppermute | solution.py:327
  153.5 20.3 %collective-permute-start.14 = (bf16[64,1536]{1,0:T(8,128)(2,1)S(1)}, bf16[64,1536]{1,0:T(8,128)(2,1)S(1)}, u32[]{:S(2)}, u32[]{:S(2)}) collective-permute-start(bf16[64,1536]{1,0:T(8,128)(2,1)S(1)} %get-tuple-element.89), channel_id=1, source_target_pairs={{0,1},{1,0},{2,3},{3,2},{4,5},{5,4},{6,7},{7,6},{8,9},{9,8},{10,11... | collective-permute-start | bytes 589832 | tf_op jit(solution)/shard_map/ppermute | solution.py:187
  160.7 13.1 %collective-permute-start.15 = (bf16[64,1536]{1,0:T(8,128)(2,1)S(1)}, bf16[64,1536]{1,0:T(8,128)(2,1)S(1)}, u32[]{:S(2)}, u32[]{:S(2)}) collective-permute-start(bf16[64,1536]{1,0:T(8,128)(2,1)S(1)} %get-tuple-element.90), channel_id=1, source_target_pairs={{0,2},{1,3},{2,0},{3,1},{4,6},{5,7},{6,4},{7,5},{8,10},{9,11},{10,... | collective-permute-start | bytes 589832 | tf_op jit(solution)/shard_map/ppermute | solution.py:187
  162.2 11.6 %collective-permute-start.16 = (bf16[64,1536]{1,0:T(8,128)(2,1)S(1)}, bf16[64,1536]{1,0:T(8,128)(2,1)S(1)}, u32[]{:S(2)}, u32[]{:S(2)}) collective-permute-start(bf16[64,1536]{1,0:T(8,128)(2,1)S(1)} %get-tuple-element.91), channel_id=1, source_target_pairs={{0,3},{1,2},{2,1},{3,0},{4,7},{5,6},{6,5},{7,4},{8,11},{9,10},{10,... | collective-permute-start | bytes 589832 | tf_op jit(solution)/shard_map/ppermute | solution.py:187
  164.7 14.0 %collective-permute-start.13 = (bf16[16,4096]{1,0:T(8,128)(2,1)S(1)}, bf16[16,4096]{1,0:T(8,128)(2,1)S(1)}, u32[]{:S(2)}, u32[]{:S(2)}) collective-permute-start(bf16[16,4096]{1,0:T(8,128)(2,1)S(1)} %get-tuple-element.79), channel_id=1, source_target_pairs={{0,192},{64,0},{128,64},{192,128},{1,193},{65,1},{129,65},{193,129... | collective-permute-start | bytes 393224 | tf_op jit(solution)/shard_map/ppermute | solution.py:327
  178.7 31.6 %all-to-all-start = ((bf16[16,32,1024]{2,1,0:T(8,128)(2,1)}), bf16[16,32,1024]{2,1,0:T(8,128)(2,1)}, u32[]{:S(2)}, u32[]{:S(2)}) async-start(bf16[16,32,1024]{2,1,0:T(8,128)(2,1)} %shard_map.141), calls=%async_computation | async-start | bytes 2097152 | tf_op jit(solution)/shard_map/all_to_all | solution.py:339
  203.3 7.1 %collective-permute-start.19 = (bf16[64,1536]{1,0:T(8,128)(2,1)}, bf16[64,1536]{1,0:T(8,128)(2,1)S(1)}, u32[]{:S(2)}, u32[]{:S(2)}) collective-permute-start(bf16[64,1536]{1,0:T(8,128)(2,1)} %get-tuple-element.108), channel_id=1, source_target_pairs={{0,1},{1,0},{2,3},{3,2},{4,5},{5,4},{6,7},{7,6},{8,9},{9,8},{10,11... | collective-permute-start | bytes 589832 | tf_op jit(solution)/shard_map/ppermute | solution.py:187
  208.7 6.9 %collective-permute-start.20 = (bf16[64,1536]{1,0:T(8,128)(2,1)}, bf16[64,1536]{1,0:T(8,128)(2,1)S(1)}, u32[]{:S(2)}, u32[]{:S(2)}) collective-permute-start(bf16[64,1536]{1,0:T(8,128)(2,1)} %get-tuple-element.109), channel_id=1, source_target_pairs={{0,2},{1,3},{2,0},{3,1},{4,6},{5,7},{6,4},{7,5},{8,10},{9,11},{10,... | collective-permute-start | bytes 589832 | tf_op jit(solution)/shard_map/ppermute | solution.py:187
  210.2 9.6 %collective-permute-start.21 = (bf16[64,1536]{1,0:T(8,128)(2,1)}, bf16[64,1536]{1,0:T(8,128)(2,1)S(1)}, u32[]{:S(2)}, u32[]{:S(2)}) collective-permute-start(bf16[64,1536]{1,0:T(8,128)(2,1)} %get-tuple-element.110), channel_id=1, source_target_pairs={{0,3},{1,2},{2,1},{3,0},{4,7},{5,6},{6,5},{7,4},{8,11},{9,10},{10,... | collective-permute-start | bytes 589832 | tf_op jit(solution)/shard_map/ppermute | solution.py:187
  221.2 18.9 %all-to-all-start.1 = ((bf16[4,4,32,1024]{3,2,1,0:T(8,128)(2,1)}), bf16[4,4,32,1024]{3,2,1,0:T(8,128)(2,1)S(1)}, u32[]{:S(2)}, u32[]{:S(2)}) async-start(bf16[4,4,32,1024]{3,2,1,0:T(8,128)(2,1)} %bitcast.26), calls=%async_computation.1 | async-start | bytes 2097152 | tf_op jit(solution)/shard_map/all_to_all | solution.py:299
  241.1 15.1 %all-to-all-start.2 = ((bf16[4,32,1024]{2,1,0:T(8,128)(2,1)}), bf16[4,32,1024]{2,1,0:T(8,128)(2,1)S(1)}, u32[]{:S(2)}, u32[]{:S(2)}) async-start(bf16[4,32,1024]{2,1,0:T(8,128)(2,1)} %reduce_sum.66), calls=%async_computation.2 | async-start | bytes 524288 | tf_op jit(solution)/shard_map/all_to_all | solution.py:301
  256.3 6.8 %collective-permute-start.22 = (bf16[2,32,1024]{2,1,0:T(8,128)(2,1)S(1)}, bf16[2,32,1024]{2,1,0:T(8,128)(2,1)S(1)}, u32[]{:S(2)}, u32[]{:S(2)}) collective-permute-start(bf16[2,32,1024]{2,1,0:T(8,128)(2,1)S(1)} %pad_maximum_fusion.2), channel_id=1, source_target_pairs={{64,0},{128,64},{192,128},{0,192},{65,1},{129,65},{193,129},{1,193... | collective-permute-start | bytes 393224 | tf_op jit(solution)/shard_map/ppermute | solution.py:195
  259.7 5.4 %collective-permute-start.23 = (bf16[2,32,1024]{2,1,0:T(8,128)(2,1)S(1)}, bf16[2,32,1024]{2,1,0:T(8,128)(2,1)S(1)}, u32[]{:S(2)}, u32[]{:S(2)}) collective-permute-start(bf16[2,32,1024]{2,1,0:T(8,128)(2,1)S(1)} %pad_maximum_fusion.2), channel_id=1, source_target_pairs={{128,0},{192,64},{0,128},{64,192},{129,1},{193,65},{1,129},{65,193... | collective-permute-start | bytes 393224 | tf_op jit(solution)/shard_map/ppermute | solution.py:195
  259.7 6.4 %collective-permute-start.24 = (bf16[2,32,1024]{2,1,0:T(8,128)(2,1)S(1)}, bf16[2,32,1024]{2,1,0:T(8,128)(2,1)S(1)}, u32[]{:S(2)}, u32[]{:S(2)}) collective-permute-start(bf16[2,32,1024]{2,1,0:T(8,128)(2,1)S(1)} %pad_maximum_fusion.2), channel_id=1, source_target_pairs={{192,0},{0,64},{64,128},{128,192},{193,1},{1,65},{65,129},{129,193... | collective-permute-start | bytes 393224 | tf_op jit(solution)/shard_map/ppermute | solution.py:195
  278.0 16.8 %all-to-all-start.3 = ((f32[16,40,128]{2,1,0:T(8,128)}), f32[16,40,128]{2,1,0:T(8,128)S(1)}, u32[]{:S(2)}, u32[]{:S(2)}) async-start(f32[16,40,128]{2,1,0:T(8,128)} %broadcast_in_dim.61), calls=%async_computation.3 | async-start | bytes 655360 | tf_op jit(solution)/shard_map/all_to_all | solution.py:374
  (37 other events, 588.1 us)
Sparse Core Ops, SparseCore 0:
  11.2 87.2 all-gather.1

commit v2 on v1

--- a/solution.py
+++ b/solution.py
@@ -114,8 +114,10 @@
         pl.when(position >= micros)(lambda: layer(0, adapters[1], position - micros))
 
 
-def pack_kernel(micros, sections, fresh, where_ref, low_ref, *refs):
+def pack_kernel(micros, sections, fresh, where_ref, *refs):
     spans = micros + sections - 1
+    lows = refs[:2] if fresh else ()
+    refs = refs[len(lows) :]
     grad_ref, cots, dus, sent = refs[0], refs[1 : 1 + spans], refs[1 + spans : 1 + 2 * spans], refs[1 + 2 * spans :]
     rows, wide = dus[0].shape
     quarters = len(sent)
@@ -133,30 +135,38 @@
             out_ref[where, :width] = chosen_quarter(cot, where_ref[1] ^ d, quarters)
             out_ref[where, width : width + wide] = du
     for out_ref in sent:
-        out_ref[:, width + wide :] = low_ref[...]
-
-
-def grads_kernel(block, *refs):
+        for i, low_ref in enumerate(lows):
+            out_ref[:, width + (1 + i) * wide : width + (2 + i) * wide] = low_ref[...]
+
+
+def grads_kernel(block, low_at, *refs):
     out_ref = refs[-1]
-    quarters = len(refs) // 2
-    xns = refs[quarters:-1]
+    quarters = len(refs) // 3
+    lows, xns = refs[quarters : 2 * quarters], refs[2 * quarters : -1]
     tokens, width = refs[0].shape[0], xns[0].shape[1]
     ranks, combos = out_ref.shape[0], out_ref.shape[1] // 2
     wide = ranks * combos
     xn = jnp.concatenate([ref[block * tokens : (block + 1) * tokens, :] for ref in xns])
-    mixed = jnp.concatenate([ref[...] for ref in refs[:quarters]])
+    mixed = jnp.concatenate([ref[:, : width + wide] for ref in refs[:quarters]])
     dy = mixed[:, :width]
     du = mixed[:, width : width + wide]
-    low = mixed[:, width + wide :]
+    low = jnp.concatenate([ref[:, low_at : low_at + wide] for ref in lows])
     grad_a = lax.dot_general(du, xn, FIRST, preferred_element_type=f32)
     out_ref[:, :combos, :] = grad_a.astype(bf16).reshape(ranks, combos, width)
     grad_b = lax.dot_general(low, dy, FIRST, preferred_element_type=f32)
     out_ref[:, combos:, :] = grad_b.astype(bf16).reshape(ranks, combos, width)
 
 
-def generate_kernel(cond_ref, down_ref, up_ref, out_ref):
+def generate_kernel(task_ref, slot_ref, down_ref, up_ref, out_ref):
     blocks, _, combos, _ = out_ref.shape
-    cond = cond_ref[...]
+    pre = jnp.concatenate(
+        [
+            slot_ref[j] + task_ref[t : t + 1, :]
+            for j in range(blocks)
+            for t in range(task_ref.shape[0])
+        ]
+    )
+    cond = pre / (1.0 + jnp.exp(-pre))
     first = cond.astype(bf16)
     rest = cond - first.astype(f32)
     second = rest.astype(bf16)
@@ -220,12 +230,10 @@
     def shaped(*shape, dtype=bf16):
         return jax.ShapeDtypeStruct(shape, dtype)
 
-    pre = task_embed[None, :, None, :] + slot_embed[:, 0][:, None, :, :]
-    cond = jax.nn.silu(pre).reshape(blocks, combos, cond_width)
     mine = call(
         generate_kernel,
         shaped(blocks, 2, combos, width),
-        (cond.reshape(blocks * combos, cond_width), gen_down, gen_up),
+        (task_embed, slot_embed[:, 0], gen_down, gen_up),
         12 * blocks * combos * cond_width * width,
         5 << 18,
     )
@@ -255,7 +263,7 @@
         (filled, slots, normed, inv_items, normed_quarter, weights_items)
     )
     adapters = filled.reshape(ranks, quarters, blocks, 2, combos, width)
-    adapters = [adapters[:, :, j] for j in range(blocks)]
+    adapters = [adapters, adapters[:, :, 1]]
     pairs = [(i, (i - 1) % sections) for i in range(sections)]
     last = items + sections - 2
 
@@ -268,37 +276,27 @@
             3 << 20,
         )
 
-    def exchanged(block, low):
+    def exchanged(block, *lows):
         span = slice((blocks - 1 - block) * micros, (blocks - block) * micros + sections - 1)
         fresh = block == blocks - 1
         cots = [out_grad[0] if cot is None else cot for cot in incoming[span]]
         parts = call(
             functools.partial(pack_kernel, micros, sections, fresh),
-            [shaped(tokens, width + 2 * wide)] * quarters,
-            (where, low, out_grad, *cots, *dus[span]),
+            [shaped(tokens, width + (1 + len(lows)) * wide)] * quarters,
+            (where, *lows, out_grad, *cots, *dus[span]),
             0,
             3 << 20,
         )
         return swapped(parts, QUARTERS)
 
-    def partial_grads(block, mixed):
+    def partial_grads(block, mixed, lows):
         return call(
-            functools.partial(grads_kernel, block),
+            functools.partial(grads_kernel, block, width + (2 - block) * wide),
             shaped(ranks, 2 * combos, width),
-            (*mixed, *normed_quarter),
+            (*mixed, *lows, *normed_quarter),
             4 * quarters * tokens * wide * width,
             5 << 20,
         )
-
-    def summed(got):
-        scale = 1.0 / (micros * rows * lax.axis_size(DP))
-        return (jnp.sum(got.astype(f32), axis=0) * scale).astype(bf16)
-
-    def rank_rows(part):
-        part = part.reshape(lax.axis_size("x"), -1, *part.shape[1:])
-        got = lax.all_to_all(part, "x", 0, 0)
-        part = jnp.sum(got.astype(f32), axis=0).astype(bf16)
-        return lax.all_to_all(part, "zh", 0, 0)
 
     incoming, dus, results = [None], [], []
     for tick in range(last + 1):
@@ -328,19 +326,26 @@
         if tick == 1:
             low_first = low_of(1)
             arriving, low_first = lax.optimization_barrier((arriving, low_first))
+        if tick == 2:
+            whole, arriving = lax.optimization_barrier((adapters[0], arriving))
+            adapters[0] = whole[:, :, 0]
         if tick == 4:
             low_second = low_of(0)
             arriving, low_second = lax.optimization_barrier((arriving, low_second))
         if tick == micros + sections - 2:
-            mixed = exchanged(1, low_first)
-        if tick == micros + sections - 1:
-            early = partial_grads(1, mixed)
+            first = exchanged(1, low_first, low_second)
+        if tick == micros + sections:
+            early = partial_grads(1, first, first)
             arriving, early = lax.optimization_barrier((arriving, early))
-            early_got = lax.all_to_all(early, RANKS, 0, 0)
+            early = lax.psum_scatter(early, RANKS, scatter_dimension=0)
         incoming.append(arriving)
-    mixed = exchanged(0, low_second)
-    mixed[0], early_got = lax.optimization_barrier((mixed[0], early_got))
-    late_got = rank_rows(partial_grads(0, mixed))
+    part = partial_grads(0, exchanged(0), first)
+    part = part.reshape(lax.axis_size("x"), -1, 2 * combos, width)
+    part = lax.all_to_all(part, "x", 0, 0)
+    part = jnp.sum(part.astype(f32), axis=0).astype(bf16)
+    part = lax.all_to_all(part, "zh", 0, 0)
+    scale = 1.0 / (micros * rows * lax.axis_size(DP))
+    early = from_sections((early.astype(f32) * scale).astype(bf16))
 
     hidden_out = jnp.stack(
         [
@@ -351,18 +356,18 @@
             for m in range(micros)
         ]
     )
-    hidden_out, late_got = lax.optimization_barrier((hidden_out, late_got))
-    reduced = jnp.stack([summed(late_got), summed(early_got)])
-    pre_all = task_embed[None, None, :, None, :] + slots[:, :, None, :, :]
+    hidden_out, part, early = lax.optimization_barrier((hidden_out, part, early))
+    late = from_sections((jnp.sum(part.astype(f32), axis=0) * scale).astype(bf16))
+    pre_all = task_embed[None, None, :, None, :] + slots.swapaxes(0, 1)[:, :, None, :, :]
     cond_all = jax.nn.silu(pre_all).reshape(sections * blocks * combos, cond_width)
-    grads = from_sections(reduced).reshape(sections * blocks, 2, combos, width)
+    grads = jnp.stack([late, early]).reshape(sections * blocks, 2, combos, width)
     grad_a = grads[:, 0].reshape(-1, width)
     grad_b = grads[:, 1].reshape(-1, width)
     d_cond = jnp.einsum("nf,wf->nw", grad_a, gen_down, preferred_element_type=f32)
     d_cond = d_cond + jnp.einsum("nf,wf->nw", grad_b, gen_up, preferred_element_type=f32)
     gate = jax.nn.sigmoid(pre_all)
     d_pre = d_cond.reshape(pre_all.shape) * gate * (1.0 + pre_all * (1.0 - gate))
-    own = lax.dynamic_index_in_dim(d_pre, section_id, 0, keepdims=False)
+    own = lax.dynamic_index_in_dim(d_pre, section_id, 1, keepdims=False)
     d_slot = jnp.sum(own, axis=1).reshape(blocks * experts, cond_width)
     d_task = jnp.sum(d_pre, axis=(0, 1, 3))
     small = jnp.concatenate([d_slot, d_task])

time: 309 us -> 336 us (1.087)
  waiting for transfers between devices: 139 us -> 161 us
  starting transfers between devices: 80.7 us -> 75.7 us
  local copies, waits for them, and re-layouts: 15.3 us -> 19.7 us
  Pallas kernels: 33.2 us -> 37.3 us
    reduce_scatter x0 -> x1, waiting for transfers between devices: none -> 24.9 us  [on_device(): early = lax.psum_scatter(early, RANKS, scatter_dimension=0)]
    all_to_all x3 -> x2, starting transfers between devices: 15.8 us -> 7.52 us  [the longest x1 4.01 us: on_device(): part = lax.all_to_all(part, 'zh', 0, 0)]
    ppermute x10, starting transfers between devices: 32.8 us -> 25.3 us  [on_device(): arriving = lax.ppermute(result, 's', pairs)]
    ppermute x9, starting transfers between devices: 19.5 us -> 26.9 us  [swapped(): lax.ppermute(parts[d], axes, [(i, i ^ d) for i in range(count)])]
    ppermute x9, waiting for transfers between devices: 18.2 us -> 25.2 us  [swapped(): lax.ppermute(parts[d], axes, [(i, i ^ d) for i in range(count)])]
    all_to_all x3 -> x2, waiting for transfers between devices: 20.7 us -> 15 us  [the longest x1 15 us: on_device(): part = lax.all_to_all(part, 'x', 0, 0)]
    unnamed x62 -> x64, local copies, waits for them, and re-layouts: 7.64 us -> 12.6 us
    pallas_call x19, Pallas kernels: 33.2 us -> 37.3 us  [call(): pl.pallas_call(kernel, out_shape=out_shape, in_specs=[SMEM] * scalars + [...]
  transfers between devices with their start and end apart: 30 -> 33, of which waited for: 20 -> 22; matrix products, arithmetic and copies ran while one was open for 3% -> 4% of each run, Pallas kernels for 5% -> 6%
where the time goes in v2:
time: 336 us; the launch traced here: 330 us
  waiting for transfers between devices  161 us (48%)
  starting transfers between devices  75.7 us (23%)
  Pallas kernels  37.3 us (11%)
  local copies, waits for them, and re-layouts  19.7 us (6%)
  between operations  14.8 us (4%)
  blocking collectives  10.6 us (3%)
  other arithmetic  7.47 us (2%)
  matrix products  3.8 us (1%)
    all_gather x1, waiting for transfers between devices, on_device(): lax.all_gather(mine.reshape(blocks * 2 * combos, width), DP, axis=0, tile...  60.7 us
    pallas_call x19, Pallas kernels, call(): pl.pallas_call(kernel, out_shape=out_shape, in_specs=[SMEM] * scalars + [...  37.3 us
    ppermute x9, starting transfers between devices, swapped(): lax.ppermute(parts[d], axes, [(i, i ^ d) for i in range(count)])  26.9 us
    ppermute x10, starting transfers between devices, on_device(): arriving = lax.ppermute(result, 's', pairs)  25.3 us
    ppermute x9, waiting for transfers between devices, swapped(): lax.ppermute(parts[d], axes, [(i, i ^ d) for i in range(count)])  25.2 us
    reduce_scatter x1, waiting for transfers between devices, on_device(): early = lax.psum_scatter(early, RANKS, scatter_dimension=0)  24.9 us
    ppermute x10, waiting for transfers between devices, on_device(): arriving = lax.ppermute(result, 's', pairs)  17.3 us
    all_to_all x1, waiting for transfers between devices, on_device(): part = lax.all_to_all(part, 'x', 0, 0)  15 us
  transfers between devices with their start and end apart: 33, of which 22 were waited for; matrix products, arithmetic and copies ran while one was open for 4% of the time, Pallas kernels for 6%

profile of v2, /device:TPU:1, one launch (start us, length us, event | category | flops | bytes accessed | tf_op | source)
XLA Modules:
  0.0 330.2 jit_solution(13945977423118907674)
XLA Ops:
  11.8 3.6 %collective-permute-start = (f32[2,8,256]{2,1,0:T(8,128)}, f32[2,8,256]{2,1,0:T(8,128)S(1)}, u32[]{:S(2)}, u32[]{:S(2)}) collective-permute-start(f32[2,8,256]{2,1,0:T(8,128)} %bitcast.107), channel_id=1, source_target_pairs={{64,0},{128,64},{192,128},{0,192},{65,1},{129,65},{193,129},{1,193... | collective-permute-start | bytes 49160 | tf_op jit(solution)/shard_map/ppermute | solution.py:205
  27.6 2.9 collective-permute-done.4.refs_10_
  30.5 7.3 %collective-permute-done.5.refs_11_ = bf16[128,1024]{1,0:T(8,128)(2,1)S(1)} collective-permute-done((bf16[128,1024]{1,0:T(8,128)(2,1)}, bf16[128,1024]{1,0:T(8,128)(2,1)S(1)}, u32[]{:S(2)}, u32[]{:S(2)}) %collective-permute-start.5) | collective-permute-done | bytes 262176 | tf_op jit(solution)/shard_map/ppermute | solution.py:197
  38.5 60.7 %all-gather.2.cloned.1.call-done = bf16[4096,1024]{1,0:T(8,128)(2,1)} async-done(((bf16[64,1024]{1,0:T(8,128)(2,1)}), bf16[4096,1024]{1,0:T(8,128)(2,1)}) %all-gather.2.cloned.1.call-update) | async-done | bytes 8388624 | tf_op jit(solution)/shard_map/all_gather | solution.py:240
  111.5 3.5 %collective-permute-start.7 = (bf16[16,4096]{1,0:T(8,128)(2,1)S(1)}, bf16[16,4096]{1,0:T(8,128)(2,1)S(1)}, u32[]{:S(2)}, u32[]{:S(2)}) collective-permute-start(bf16[16,4096]{1,0:T(8,128)(2,1)S(1)} %get-tuple-element.71), channel_id=1, source_target_pairs={{0,192},{64,0},{128,64},{192,128},{1,193},{65,1},{129,65},{193,129... | collective-permute-start | bytes 393224 | tf_op jit(solution)/shard_map/ppermute | solution.py:325
  119.1 3.2 collective-permute-start.8
  126.5 3.4 %collective-permute-start.9 = (bf16[16,4096]{1,0:T(8,128)(2,1)S(1)}, bf16[16,4096]{1,0:T(8,128)(2,1)S(1)}, u32[]{:S(2)}, u32[]{:S(2)}) collective-permute-start(bf16[16,4096]{1,0:T(8,128)(2,1)S(1)} %get-tuple-element.76), channel_id=1, source_target_pairs={{0,192},{64,0},{128,64},{192,128},{1,193},{65,1},{129,65},{193,129... | collective-permute-start | bytes 393224 | tf_op jit(solution)/shard_map/ppermute | solution.py:325
  134.1 3.2 collective-permute-start.10
  141.4 3.2 collective-permute-start.11
  148.8 3.2 collective-permute-start.12
  156.3 3.2 collective-permute-start.13
  160.2 9.6 %collective-permute-start.15 = (bf16[64,1792]{1,0:T(8,128)(2,1)S(1)}, bf16[64,1792]{1,0:T(8,128)(2,1)S(1)}, u32[]{:S(2)}, u32[]{:S(2)}) collective-permute-start(bf16[64,1792]{1,0:T(8,128)(2,1)S(1)} %get-tuple-element.94), channel_id=1, source_target_pairs={{0,1},{1,0},{2,3},{3,2},{4,5},{5,4},{6,7},{7,6},{8,9},{9,8},{10,11... | collective-permute-start | bytes 688136 | tf_op jit(solution)/shard_map/ppermute | solution.py:197
  171.3 10.3 %collective-permute-start.17 = (bf16[64,1792]{1,0:T(8,128)(2,1)S(1)}, bf16[64,1792]{1,0:T(8,128)(2,1)S(1)}, u32[]{:S(2)}, u32[]{:S(2)}) collective-permute-start(bf16[64,1792]{1,0:T(8,128)(2,1)S(1)} %get-tuple-element.96), channel_id=1, source_target_pairs={{0,3},{1,2},{2,1},{3,0},{4,7},{5,6},{6,5},{7,4},{8,11},{9,10},{10,... | collective-permute-start | bytes 688136 | tf_op jit(solution)/shard_map/ppermute | solution.py:197
  184.5 4.8 %collective-permute-done.17.refs_3_.refs_7_ = bf16[64,1792]{1,0:T(8,128)(2,1)S(1)} collective-permute-done((bf16[64,1792]{1,0:T(8,128)(2,1)S(1)}, bf16[64,1792]{1,0:T(8,128)(2,1)S(1)}, u32[]{:S(2)}, u32[]{:S(2)}) %collective-permute-start.17) | collective-permute-done | bytes 229408 | tf_op jit(solution)/shard_map/ppermute | solution.py:197
  197.2 5.3 %collective-permute-done.18.refs_0_.refs_7_ = bf16[16,4096]{1,0:T(8,128)(2,1)S(1)} collective-permute-done((bf16[16,4096]{1,0:T(8,128)(2,1)S(1)}, bf16[16,4096]{1,0:T(8,128)(2,1)S(1)}, u32[]{:S(2)}, u32[]{:S(2)}) %collective-permute-start.18) | collective-permute-done | bytes 131104 | tf_op jit(solution)/shard_map/ppermute | solution.py:325
  209.6 5.4 %collective-permute-done.20.refs_2_ = bf16[64,1280]{1,0:T(8,128)(2,1)S(1)} collective-permute-done((bf16[64,1280]{1,0:T(8,128)(2,1)}, bf16[64,1280]{1,0:T(8,128)(2,1)S(1)}, u32[]{:S(2)}, u32[]{:S(2)}) %collective-permute-start.20) | collective-permute-done | bytes 163872 | tf_op jit(solution)/shard_map/ppermute | solution.py:197
  215.0 4.8 %collective-permute-done.21.refs_3_ = bf16[64,1280]{1,0:T(8,128)(2,1)S(1)} collective-permute-done((bf16[64,1280]{1,0:T(8,128)(2,1)}, bf16[64,1280]{1,0:T(8,128)(2,1)S(1)}, u32[]{:S(2)}, u32[]{:S(2)}) %collective-permute-start.21) | collective-permute-done | bytes 163872 | tf_op jit(solution)/shard_map/ppermute | solution.py:197
  225.1 3.5 %all-to-all-start = ((bf16[4,4,32,1024]{3,2,1,0:T(8,128)(2,1)}), bf16[4,4,32,1024]{3,2,1,0:T(8,128)(2,1)S(1)}, u32[]{:S(2)}, u32[]{:S(2)}) async-start(bf16[4,4,32,1024]{3,2,1,0:T(8,128)(2,1)} %bitcast.25), calls=%async_computation | async-start | bytes 2097152 | tf_op jit(solution)/shard_map/all_to_all | solution.py:344
  229.9 15.0 %all-to-all-done = bf16[4,4,32,1024]{3,2,1,0:T(8,128)(2,1)S(1)} async-done(((bf16[4,4,32,1024]{3,2,1,0:T(8,128)(2,1)}), bf16[4,4,32,1024]{3,2,1,0:T(8,128)(2,1)S(1)}, u32[]{:S(2)}, u32[]{:S(2)}) %all-to-all-start) | async-done | bytes 1048608 | tf_op jit(solution)/shard_map/all_to_all | solution.py:344
  245.8 4.0 %all-to-all-start.1 = ((bf16[4,32,1024]{2,1,0:T(8,128)(2,1)}), bf16[4,32,1024]{2,1,0:T(8,128)(2,1)S(1)}, u32[]{:S(2)}, u32[]{:S(2)}) async-start(bf16[4,32,1024]{2,1,0:T(8,128)(2,1)} %reduce_sum.57), calls=%async_computation.1 | async-start | bytes 524288 | tf_op jit(solution)/shard_map/all_to_all | solution.py:346
  249.8 24.9 %reduce-scatter.2.cloned.1.call-done = bf16[1,32,1024]{2,1,0:T(8,128)(2,1)} async-done(((bf16[16,32,1024]{2,1,0:T(8,128)(2,1)}), bf16[1,32,1024]{2,1,0:T(8,128)(2,1)}) %reduce-scatter.2.cloned.1.call-update) | async-done | bytes 65552 | tf_op jit(solution)/shard_map/reduce_scatter | solution.py:340
  291.2 10.6 %all_gather.7 = f32[160,128]{1,0:T(8,128)S(1)} all-gather(f32[40,128]{1,0:T(8,128)S(1)} %pad.4), channel_id=1, replica_groups=mesh['s'=4,'x'=4,'zh'=4,'zl'=2,'c'=2] {'zl','c'}, dimensions={0}, use_global_device_ids=true | all-gather | bytes 102400 | tf_op jit(solution)/shard_map/all_gather | solution.py:376
  302.5 5.6 %all-to-all-start.2 = ((f32[16,40,128]{2,1,0:T(8,128)}), f32[16,40,128]{2,1,0:T(8,128)S(1)}, u32[]{:S(2)}, u32[]{:S(2)}) async-start(f32[16,40,128]{2,1,0:T(8,128)} %broadcast_in_dim.60), calls=%async_computation.3 | async-start | bytes 655360 | tf_op jit(solution)/shard_map/all_to_all | solution.py:379
  311.3 10.6 %all-to-all-done.2 = f32[16,40,128]{2,1,0:T(8,128)S(1)} async-done(((f32[16,40,128]{2,1,0:T(8,128)}), f32[16,40,128]{2,1,0:T(8,128)S(1)}, u32[]{:S(2)}, u32[]{:S(2)}) %all-to-all-start.2) | async-done | bytes 327712 | tf_op jit(solution)/shard_map/all_to_all | solution.py:379
  (171 shorter events, 103.7 us)
Async XLA Ops:
  7.2 92.0 %all-gather.2.cloned.1.call-start = ((), (), s32[]{:S(2)}) async-start(), calls=%async_computation.4 | async-start | bytes 8519680 | tf_op jit(solution)/shard_map/all_gather | solution.py:240
  11.8 262.9 %reduce-scatter.2.cloned.1.call-start = ((), (), s32[]{:S(2)}) async-start(), calls=%async_computation.5 | async-start | bytes 1114112 | tf_op jit(solution)/shard_map/reduce_scatter | solution.py:340
  11.8 14.2 %collective-permute-start = (f32[2,8,256]{2,1,0:T(8,128)}, f32[2,8,256]{2,1,0:T(8,128)S(1)}, u32[]{:S(2)}, u32[]{:S(2)}) collective-permute-start(f32[2,8,256]{2,1,0:T(8,128)} %bitcast.107), channel_id=1, source_target_pairs={{64,0},{128,64},{192,128},{0,192},{65,1},{129,65},{193,129},{1,193... | collective-permute-start | bytes 49160 | tf_op jit(solution)/shard_map/ppermute | solution.py:205
  15.5 10.7 %collective-permute-start.1 = (f32[2,8,256]{2,1,0:T(8,128)}, f32[2,8,256]{2,1,0:T(8,128)S(1)}, u32[]{:S(2)}, u32[]{:S(2)}) collective-permute-start(f32[2,8,256]{2,1,0:T(8,128)} %bitcast.108), channel_id=1, source_target_pairs={{128,0},{192,64},{0,128},{64,192},{129,1},{193,65},{1,129},{65,193... | collective-permute-start | bytes 49160 | tf_op jit(solution)/shard_map/ppermute | solution.py:205
  15.8 10.4 %collective-permute-start.2 = (f32[2,8,256]{2,1,0:T(8,128)}, f32[2,8,256]{2,1,0:T(8,128)S(1)}, u32[]{:S(2)}, u32[]{:S(2)}) collective-permute-start(f32[2,8,256]{2,1,0:T(8,128)} %bitcast.109), channel_id=1, source_target_pairs={{192,0},{0,64},{64,128},{128,192},{193,1},{1,65},{65,129},{129,193... | collective-permute-start | bytes 49160 | tf_op jit(solution)/shard_map/ppermute | solution.py:205
  20.4 7.2 %collective-permute-start.3 = (bf16[128,1024]{1,0:T(8,128)(2,1)}, bf16[128,1024]{1,0:T(8,128)(2,1)S(1)}, u32[]{:S(2)}, u32[]{:S(2)}) collective-permute-start(bf16[128,1024]{1,0:T(8,128)(2,1)} %get-tuple-element.64), channel_id=1, source_target_pairs={{0,1},{1,0},{2,3},{3,2},{4,5},{5,4},{6,7},{7,6},{8,9},{9,8},{10,11... | collective-permute-start | bytes 786440 | tf_op jit(solution)/shard_map/ppermute | solution.py:197
  21.9 8.5 %collective-permute-start.4 = (bf16[128,1024]{1,0:T(8,128)(2,1)}, bf16[128,1024]{1,0:T(8,128)(2,1)}, u32[]{:S(2)}, u32[]{:S(2)}) collective-permute-start(bf16[128,1024]{1,0:T(8,128)(2,1)} %get-tuple-element.65), channel_id=1, source_target_pairs={{0,2},{1,3},{2,0},{3,1},{4,6},{5,7},{6,4},{7,5},{8,10},{9,11},{10,... | collective-permute-start | bytes 786440 | tf_op jit(solution)/shard_map/ppermute | solution.py:197
  26.1 11.7 %collective-permute-start.5 = (bf16[128,1024]{1,0:T(8,128)(2,1)}, bf16[128,1024]{1,0:T(8,128)(2,1)S(1)}, u32[]{:S(2)}, u32[]{:S(2)}) collective-permute-start(bf16[128,1024]{1,0:T(8,128)(2,1)} %copy-done.28), channel_id=1, source_target_pairs={{0,3},{1,2},{2,1},{3,0},{4,7},{5,6},{6,5},{7,4},{8,11},{9,10},{10,... | collective-permute-start | bytes 786440 | tf_op jit(solution)/shard_map/ppermute | solution.py:197
  104.1 5.2 %collective-permute-start.6 = (bf16[16,4096]{1,0:T(8,128)(2,1)S(1)}, bf16[16,4096]{1,0:T(8,128)(2,1)S(1)}, u32[]{:S(2)}, u32[]{:S(2)}) collective-permute-start(bf16[16,4096]{1,0:T(8,128)(2,1)S(1)} %get-tuple-element.70), channel_id=1, source_target_pairs={{0,192},{64,0},{128,64},{192,128},{1,193},{65,1},{129,65},{193,129... | collective-permute-start | bytes 393224 | tf_op jit(solution)/shard_map/ppermute | solution.py:325
  111.5 5.4 %collective-permute-start.7 = (bf16[16,4096]{1,0:T(8,128)(2,1)S(1)}, bf16[16,4096]{1,0:T(8,128)(2,1)S(1)}, u32[]{:S(2)}, u32[]{:S(2)}) collective-permute-start(bf16[16,4096]{1,0:T(8,128)(2,1)S(1)} %get-tuple-element.71), channel_id=1, source_target_pairs={{0,192},{64,0},{128,64},{192,128},{1,193},{65,1},{129,65},{193,129... | collective-permute-start | bytes 393224 | tf_op jit(solution)/shard_map/ppermute | solution.py:325
  119.1 5.1 %collective-permute-start.8 = (bf16[16,4096]{1,0:T(8,128)(2,1)S(1)}, bf16[16,4096]{1,0:T(8,128)(2,1)S(1)}, u32[]{:S(2)}, u32[]{:S(2)}) collective-permute-start(bf16[16,4096]{1,0:T(8,128)(2,1)S(1)} %get-tuple-element.74), channel_id=1, source_target_pairs={{0,192},{64,0},{128,64},{192,128},{1,193},{65,1},{129,65},{193,129... | collective-permute-start | bytes 393224 | tf_op jit(solution)/shard_map/ppermute | solution.py:325
  126.5 5.4 %collective-permute-start.9 = (bf16[16,4096]{1,0:T(8,128)(2,1)S(1)}, bf16[16,4096]{1,0:T(8,128)(2,1)S(1)}, u32[]{:S(2)}, u32[]{:S(2)}) collective-permute-start(bf16[16,4096]{1,0:T(8,128)(2,1)S(1)} %get-tuple-element.76), channel_id=1, source_target_pairs={{0,192},{64,0},{128,64},{192,128},{1,193},{65,1},{129,65},{193,129... | collective-permute-start | bytes 393224 | tf_op jit(solution)/shard_map/ppermute | solution.py:325
  148.8 5.2 %collective-permute-start.12 = (bf16[16,4096]{1,0:T(8,128)(2,1)S(1)}, bf16[16,4096]{1,0:T(8,128)(2,1)S(1)}, u32[]{:S(2)}, u32[]{:S(2)}) collective-permute-start(bf16[16,4096]{1,0:T(8,128)(2,1)S(1)} %get-tuple-element.81), channel_id=1, source_target_pairs={{0,192},{64,0},{128,64},{192,128},{1,193},{65,1},{129,65},{193,129... | collective-permute-start | bytes 393224 | tf_op jit(solution)/shard_map/ppermute | solution.py:325
  156.3 25.3 %collective-permute-start.13 = (bf16[16,4096]{1,0:T(8,128)(2,1)S(1)}, bf16[16,4096]{1,0:T(8,128)(2,1)S(1)}, u32[]{:S(2)}, u32[]{:S(2)}) collective-permute-start(bf16[16,4096]{1,0:T(8,128)(2,1)S(1)} %get-tuple-element.82), channel_id=1, source_target_pairs={{0,192},{64,0},{128,64},{192,128},{1,193},{65,1},{129,65},{193,129... | collective-permute-start | bytes 393224 | tf_op jit(solution)/shard_map/ppermute | solution.py:325
  160.2 24.3 %collective-permute-start.15 = (bf16[64,1792]{1,0:T(8,128)(2,1)S(1)}, bf16[64,1792]{1,0:T(8,128)(2,1)S(1)}, u32[]{:S(2)}, u32[]{:S(2)}) collective-permute-start(bf16[64,1792]{1,0:T(8,128)(2,1)S(1)} %get-tuple-element.94), channel_id=1, source_target_pairs={{0,1},{1,0},{2,3},{3,2},{4,5},{5,4},{6,7},{7,6},{8,9},{9,8},{10,11... | collective-permute-start | bytes 688136 | tf_op jit(solution)/shard_map/ppermute | solution.py:197
  169.8 14.7 %collective-permute-start.16 = (bf16[64,1792]{1,0:T(8,128)(2,1)S(1)}, bf16[64,1792]{1,0:T(8,128)(2,1)S(1)}, u32[]{:S(2)}, u32[]{:S(2)}) collective-permute-start(bf16[64,1792]{1,0:T(8,128)(2,1)S(1)} %get-tuple-element.95), channel_id=1, source_target_pairs={{0,2},{1,3},{2,0},{3,1},{4,6},{5,7},{6,4},{7,5},{8,10},{9,11},{10,... | collective-permute-start | bytes 688136 | tf_op jit(solution)/shard_map/ppermute | solution.py:197
  171.3 18.0 %collective-permute-start.17 = (bf16[64,1792]{1,0:T(8,128)(2,1)S(1)}, bf16[64,1792]{1,0:T(8,128)(2,1)S(1)}, u32[]{:S(2)}, u32[]{:S(2)}) collective-permute-start(bf16[64,1792]{1,0:T(8,128)(2,1)S(1)} %get-tuple-element.96), channel_id=1, source_target_pairs={{0,3},{1,2},{2,1},{3,0},{4,7},{5,6},{6,5},{7,4},{8,11},{9,10},{10,... | collective-permute-start | bytes 688136 | tf_op jit(solution)/shard_map/ppermute | solution.py:197
  184.5 7.2 %collective-permute-start.14 = (bf16[16,4096]{1,0:T(8,128)(2,1)}, bf16[16,4096]{1,0:T(8,128)(2,1)}, u32[]{:S(2)}, u32[]{:S(2)}) collective-permute-start(bf16[16,4096]{1,0:T(8,128)(2,1)} %get-tuple-element.83), channel_id=1, source_target_pairs={{0,192},{64,0},{128,64},{192,128},{1,193},{65,1},{129,65},{193,129... | collective-permute-start | bytes 393224 | tf_op jit(solution)/shard_map/ppermute | solution.py:325
  197.2 5.3 %collective-permute-start.18 = (bf16[16,4096]{1,0:T(8,128)(2,1)S(1)}, bf16[16,4096]{1,0:T(8,128)(2,1)S(1)}, u32[]{:S(2)}, u32[]{:S(2)}) collective-permute-start(bf16[16,4096]{1,0:T(8,128)(2,1)S(1)} %get-tuple-element.102), channel_id=1, source_target_pairs={{0,192},{64,0},{128,64},{192,128},{1,193},{65,1},{129,65},{193,129... | collective-permute-start | bytes 393224 | tf_op jit(solution)/shard_map/ppermute | solution.py:325
  207.9 7.1 %collective-permute-start.20 = (bf16[64,1280]{1,0:T(8,128)(2,1)}, bf16[64,1280]{1,0:T(8,128)(2,1)S(1)}, u32[]{:S(2)}, u32[]{:S(2)}) collective-permute-start(bf16[64,1280]{1,0:T(8,128)(2,1)} %get-tuple-element.110), channel_id=1, source_target_pairs={{0,2},{1,3},{2,0},{3,1},{4,6},{5,7},{6,4},{7,5},{8,10},{9,11},{10,... | collective-permute-start | bytes 491528 | tf_op jit(solution)/shard_map/ppermute | solution.py:197
  207.9 11.9 %collective-permute-start.21 = (bf16[64,1280]{1,0:T(8,128)(2,1)}, bf16[64,1280]{1,0:T(8,128)(2,1)S(1)}, u32[]{:S(2)}, u32[]{:S(2)}) collective-permute-start(bf16[64,1280]{1,0:T(8,128)(2,1)} %get-tuple-element.111), channel_id=1, source_target_pairs={{0,3},{1,2},{2,1},{3,0},{4,7},{5,6},{6,5},{7,4},{8,11},{9,10},{10,... | collective-permute-start | bytes 491528 | tf_op jit(solution)/shard_map/ppermute | solution.py:197
  225.1 19.8 %all-to-all-start = ((bf16[4,4,32,1024]{3,2,1,0:T(8,128)(2,1)}), bf16[4,4,32,1024]{3,2,1,0:T(8,128)(2,1)S(1)}, u32[]{:S(2)}, u32[]{:S(2)}) async-start(bf16[4,4,32,1024]{3,2,1,0:T(8,128)(2,1)} %bitcast.25), calls=%async_computation | async-start | bytes 2097152 | tf_op jit(solution)/shard_map/all_to_all | solution.py:344
  245.8 38.6 %all-to-all-start.1 = ((bf16[4,32,1024]{2,1,0:T(8,128)(2,1)}), bf16[4,32,1024]{2,1,0:T(8,128)(2,1)S(1)}, u32[]{:S(2)}, u32[]{:S(2)}) async-start(bf16[4,32,1024]{2,1,0:T(8,128)(2,1)} %reduce_sum.57), calls=%async_computation.1 | async-start | bytes 524288 | tf_op jit(solution)/shard_map/all_to_all | solution.py:346
  302.5 19.4 %all-to-all-start.2 = ((f32[16,40,128]{2,1,0:T(8,128)}), f32[16,40,128]{2,1,0:T(8,128)S(1)}, u32[]{:S(2)}, u32[]{:S(2)}) async-start(f32[16,40,128]{2,1,0:T(8,128)} %broadcast_in_dim.60), calls=%async_computation.3 | async-start | bytes 655360 | tf_op jit(solution)/shard_map/all_to_all | solution.py:379
  (41 other events, 915.9 us)
Sparse Core Ops, SparseCore 0:
  11.9 87.2 all-gather.1
  191.8 82.8 reduce-scatter.1

commit v3 on v2

--- a/solution.py
+++ b/solution.py
@@ -20,6 +20,7 @@
 LAST = (((1,), (1,)), ((), ()))
 FIRST = (((0,), (0,)), ((), ()))
 VMEM_LIMIT = 4 * 1024 * 1024
+HOP = 2
 
 
 def adapter_rows(g_ref, which, q):
@@ -68,7 +69,7 @@
     section = where_ref[0]
     if tick < micros:
         grad = refs.pop(0)[tick]
-        if tick:
+        if tick >= HOP:
             cot = jnp.where(section == sections - 1, grad, refs.pop(0)[...])
         else:
             cot = grad
@@ -77,9 +78,12 @@
     x_ref, inv_ref, weights_ref = refs[:3]
     dx_ref, du_ref = refs[-2:]
     adapters = refs[3:-2]
-    position = jnp.clip(tick - (sections - 1 - section), 0, x_ref.shape[0] - 1)
-
-    def layer(block, g_ref, item):
+    position = tick - HOP * (sections - 1 - section)
+    second = position - HOP * sections
+    first_item = micros + jnp.clip(position, 0, micros - 1)
+    second_item = jnp.clip(second, 0, micros - 1)
+
+    def layer(g_ref, item):
         quarters, width = g_ref.shape[1], g_ref.shape[4]
         back = jnp.zeros(du_ref.shape, f32)
         for q in range(quarters):
@@ -105,17 +109,17 @@
                 cot[:, cols].astype(f32) + inv * (dxn[q] - xf[q] * mean)
             ).astype(bf16)
 
-    if tick < micros:
-        layer(1, adapters[0], micros + position)
-    elif tick >= micros + sections - 1:
-        layer(0, adapters[0], position - micros)
+    if tick < HOP * sections:
+        layer(adapters[0], first_item)
+    elif tick >= HOP * (sections - 1) + micros:
+        layer(adapters[0], second_item)
     else:
-        pl.when(position < micros)(lambda: layer(1, adapters[0], micros + position))
-        pl.when(position >= micros)(lambda: layer(0, adapters[1], position - micros))
+        pl.when(second < 0)(lambda: layer(adapters[0], first_item))
+        pl.when(second >= 0)(lambda: layer(adapters[1], second_item))
 
 
 def pack_kernel(micros, sections, fresh, where_ref, *refs):
-    spans = micros + sections - 1
+    spans = micros + HOP * (sections - 1)
     lows = refs[:2] if fresh else ()
     refs = refs[len(lows) :]
     grad_ref, cots, dus, sent = refs[0], refs[1 : 1 + spans], refs[1 + spans : 1 + 2 * spans], refs[1 + 2 * spans :]
@@ -127,7 +131,7 @@
         cot = grad_ref[m] if fresh else cots[m][...]
         du = dus[m][...]
         for s in range(sections - 1):
-            at = m + sections - 1 - s
+            at = m + HOP * (sections - 1 - s)
             cot = jnp.where(section == s, cots[at][...], cot)
             du = jnp.where(section == s, dus[at][...], du)
         where = slice(m * rows, (m + 1) * rows)
@@ -264,8 +268,13 @@
     )
     adapters = filled.reshape(ranks, quarters, blocks, 2, combos, width)
     adapters = [adapters, adapters[:, :, 1]]
-    pairs = [(i, (i - 1) % sections) for i in range(sections)]
-    last = items + sections - 2
+    last = HOP * (2 * sections - 1) + micros - 1
+
+    def active(tick, section):
+        position = tick - HOP * (sections - 1 - section)
+        if 0 <= position < micros:
+            return 1
+        return 0 if 0 <= position - HOP * sections < micros else None
 
     def low_of(block):
         return call(
@@ -277,7 +286,8 @@
         )
 
     def exchanged(block, *lows):
-        span = slice((blocks - 1 - block) * micros, (blocks - block) * micros + sections - 1)
+        start = 0 if block == 1 else HOP * sections
+        span = slice(start, start + micros + HOP * (sections - 1))
         fresh = block == blocks - 1
         cots = [out_grad[0] if cot is None else cot for cot in incoming[span]]
         parts = call(
@@ -298,16 +308,17 @@
             5 << 20,
         )
 
-    incoming, dus, results = [None], [], []
+    incoming, dus, results = [None] * HOP, [], []
     for tick in range(last + 1):
         operands = [where]
         if tick < micros:
             operands.append(out_grad)
-        if tick:
+        if tick >= HOP:
+            incoming[tick], dus[-1] = lax.optimization_barrier((incoming[tick], dus[-1]))
             operands.append(incoming[tick])
-        if tick < micros:
+        if tick < HOP * sections:
             used = [adapters[1]]
-        elif tick >= micros + sections - 1:
+        elif tick >= HOP * (sections - 1) + micros:
             used = [adapters[0]]
         else:
             used = [adapters[1], adapters[0]]
@@ -320,38 +331,45 @@
         )
         results.append(result)
         dus.append(du)
-        if tick == last:
-            break
+        if tick > last - HOP:
+            continue
+        pairs = [
+            (i, (i - 1) % sections)
+            for i in range(sections)
+            if active(tick, i) == 1 or (i and active(tick, i) == 0)
+        ]
         arriving = lax.ppermute(result, "s", pairs)
         if tick == 1:
             low_first = low_of(1)
             arriving, low_first = lax.optimization_barrier((arriving, low_first))
-        if tick == 2:
+        if tick == 3:
             whole, arriving = lax.optimization_barrier((adapters[0], arriving))
             adapters[0] = whole[:, :, 0]
-        if tick == 4:
+        if tick == 6:
             low_second = low_of(0)
             arriving, low_second = lax.optimization_barrier((arriving, low_second))
-        if tick == micros + sections - 2:
+        if tick == HOP * (sections - 1) + micros - 1:
             first = exchanged(1, low_first, low_second)
-        if tick == micros + sections:
+        if tick == HOP * (sections - 1) + micros + 1:
             early = partial_grads(1, first, first)
             arriving, early = lax.optimization_barrier((arriving, early))
-            early = lax.psum_scatter(early, RANKS, scatter_dimension=0)
+            early = lax.all_to_all(early, RANKS, 0, 0)
         incoming.append(arriving)
-    part = partial_grads(0, exchanged(0), first)
+    mixed = exchanged(0)
+    mixed[0], early = lax.optimization_barrier((mixed[0], early))
+    part = partial_grads(0, mixed, first)
     part = part.reshape(lax.axis_size("x"), -1, 2 * combos, width)
     part = lax.all_to_all(part, "x", 0, 0)
     part = jnp.sum(part.astype(f32), axis=0).astype(bf16)
     part = lax.all_to_all(part, "zh", 0, 0)
     scale = 1.0 / (micros * rows * lax.axis_size(DP))
-    early = from_sections((early.astype(f32) * scale).astype(bf16))
+    early = from_sections((jnp.sum(early.astype(f32), axis=0) * scale).astype(bf16))
 
     hidden_out = jnp.stack(
         [
             lax.select_n(
                 section_id,
-                *[results[micros + m + sections - 1 - s] for s in range(sections)],
+                *[results[m + HOP * (2 * sections - 1 - s)] for s in range(sections)],
             )
             for m in range(micros)
         ]

time: 336 us -> 318 us (0.946)
  waiting for transfers between devices: 161 us -> 133 us
  Pallas kernels: 37.3 us -> 52.1 us
  starting transfers between devices: 75.7 us -> 71.2 us
    reduce_scatter x1 -> x0, waiting for transfers between devices: 24.9 us -> none  [on_device(): early = lax.psum_scatter(early, RANKS, scatter_dimension=0)]
    pallas_call x19 -> x26, Pallas kernels: 37.3 us -> 52.1 us  [call(): pl.pallas_call(kernel, out_shape=out_shape, in_specs=[SMEM] * scalars + [...]
    ppermute x9, starting transfers between devices: 26.9 us -> 12.2 us  [swapped(): lax.ppermute(parts[d], axes, [(i, i ^ d) for i in range(count)])]
    all_to_all x1, waiting for transfers between devices: 0.01 us -> 7.43 us  [on_device(): part = lax.all_to_all(part, 'zh', 0, 0)]
    ppermute x10 -> x16, starting transfers between devices: 25.3 us -> 32.2 us  [on_device(): arriving = lax.ppermute(result, 's', pairs)]
    all_to_all x0 -> x1, starting transfers between devices: none -> 5 us  [on_device(): early = lax.all_to_all(early, RANKS, 0, 0)]
    all_to_all x1, waiting for transfers between devices: 15 us -> 10.2 us  [on_device(): part = lax.all_to_all(part, 'x', 0, 0)]
    unnamed x64 -> x68, local copies, waits for them, and re-layouts: 12.6 us -> 11.9 us
  transfers between devices with their start and end apart: 33 -> 39, of which waited for: 22 -> 17; matrix products, arithmetic and copies ran while one was open for 4% -> 4% of each run, Pallas kernels for 6% -> 13%
where the time goes in v3:
time: 318 us; the launch traced here: 312 us
  waiting for transfers between devices  133 us (42%)
  starting transfers between devices  71.2 us (22%)
  Pallas kernels  52.1 us (16%)
  local copies, waits for them, and re-layouts  18.9 us (6%)
  between operations  15.2 us (5%)
  blocking collectives  10.5 us (3%)
  other arithmetic  7.31 us (2%)
  matrix products  3.8 us (1%)
    all_gather x1, waiting for transfers between devices, on_device(): lax.all_gather(mine.reshape(blocks * 2 * combos, width), DP, axis=0, tile...  60.7 us
    pallas_call x26, Pallas kernels, call(): pl.pallas_call(kernel, out_shape=out_shape, in_specs=[SMEM] * scalars + [...  52.1 us
    ppermute x16, starting transfers between devices, on_device(): arriving = lax.ppermute(result, 's', pairs)  32.2 us
    ppermute x9, waiting for transfers between devices, swapped(): lax.ppermute(parts[d], axes, [(i, i ^ d) for i in range(count)])  23.6 us
    ppermute x16, waiting for transfers between devices, on_device(): arriving = lax.ppermute(result, 's', pairs)  17.4 us
    ppermute x9, starting transfers between devices, swapped(): lax.ppermute(parts[d], axes, [(i, i ^ d) for i in range(count)])  12.2 us
    unnamed x68, local copies, waits for them, and re-layouts  11.9 us
    all_gather x1, blocking collectives, on_device(): got = lax.all_gather(held, QUARTERS, axis=0, tiled=True)  10.5 us
  transfers between devices with their start and end apart: 39, of which 17 were waited for; matrix products, arithmetic and copies ran while one was open for 4% of the time, Pallas kernels for 13%

profile of v3, /device:TPU:1, one launch (start us, length us, event | category | flops | bytes accessed | tf_op | source)
XLA Modules:
  0.0 312.5 jit_solution(1674591482610590947)
XLA Ops:
  11.8 3.6 %collective-permute-start = (f32[2,8,256]{2,1,0:T(8,128)}, f32[2,8,256]{2,1,0:T(8,128)S(1)}, u32[]{:S(2)}, u32[]{:S(2)}) collective-permute-start(f32[2,8,256]{2,1,0:T(8,128)} %bitcast.3.slot_ref), channel_id=1, source_target_pairs={{64,0},{128,64},{192,128},{0,192},{65,1},{129,65},{193,129},{1,193... | collective-permute-start | bytes 49160 | tf_op jit(solution)/shard_map/ppermute | solution.py:209
  27.5 2.9 collective-permute-done.4.refs_10_
  30.4 7.3 %collective-permute-done.5.refs_11_ = bf16[128,1024]{1,0:T(8,128)(2,1)S(1)} collective-permute-done((bf16[128,1024]{1,0:T(8,128)(2,1)}, bf16[128,1024]{1,0:T(8,128)(2,1)S(1)}, u32[]{:S(2)}, u32[]{:S(2)}) %collective-permute-start.5) | collective-permute-done | bytes 262176 | tf_op jit(solution)/shard_map/ppermute | solution.py:201
  38.4 60.7 %all-gather.2.cloned.1.call-done = bf16[4096,1024]{1,0:T(8,128)(2,1)} async-done(((bf16[64,1024]{1,0:T(8,128)(2,1)}), bf16[4096,1024]{1,0:T(8,128)(2,1)}) %all-gather.2.cloned.1.call-update) | async-done | bytes 8388624 | tf_op jit(solution)/shard_map/all_gather | solution.py:244
  99.2 2.6 slice_bitcast_fusion.1.refs_4_.refs_5_.g_ref
  121.8 11.7 %collective-permute-done.9.refs_0_.refs_9_ = bf16[16,4096]{1,0:T(8,128)(2,1)S(1)} collective-permute-done((bf16[16,4096]{1,0:T(8,128)(2,1)S(1)}, bf16[16,4096]{1,0:T(8,128)(2,1)S(1)}, u32[]{:S(2)}, u32[]{:S(2)}) %collective-permute-start.9) | collective-permute-done | bytes 131104 | tf_op jit(solution)/shard_map/ppermute | solution.py:341
  148.1 3.1 %collective-permute-start.13 = (bf16[16,4096]{1,0:T(8,128)(2,1)S(1)}, bf16[16,4096]{1,0:T(8,128)(2,1)S(1)}, u32[]{:S(2)}, u32[]{:S(2)}) collective-permute-start(bf16[16,4096]{1,0:T(8,128)(2,1)S(1)} %get-tuple-element.144), channel_id=1, source_target_pairs={{0,192},{192,128},{1,193},{193,129},{2,194},{194,130},{3,195},{195... | collective-permute-start | bytes 393224 | tf_op jit(solution)/shard_map/ppermute | solution.py:341
  151.2 2.5 collective-permute-start.16
  154.5 2.9 collective-permute-start.19
  164.5 5.1 %collective-permute-done.21.refs_3_.refs_7_ = bf16[64,1792]{1,0:T(8,128)(2,1)S(1)} collective-permute-done((bf16[64,1792]{1,0:T(8,128)(2,1)S(1)}, bf16[64,1792]{1,0:T(8,128)(2,1)S(1)}, u32[]{:S(2)}, u32[]{:S(2)}) %collective-permute-start.21) | collective-permute-done | bytes 229408 | tf_op jit(solution)/shard_map/ppermute | solution.py:201
  169.6 2.4 shard_map.146
  172.7 5.0 %all-to-all-start = ((bf16[16,32,1024]{2,1,0:T(8,128)(2,1)}), bf16[16,32,1024]{2,1,0:T(8,128)(2,1)}, u32[]{:S(2)}, u32[]{:S(2)}) async-start(bf16[16,32,1024]{2,1,0:T(8,128)(2,1)} %shard_map.146), calls=%async_computation | async-start | bytes 2097152 | tf_op jit(solution)/shard_map/all_to_all | solution.py:356
  182.8 11.6 %collective-permute-start.17 = (bf16[16,4096]{1,0:T(8,128)(2,1)S(1)}, bf16[16,4096]{1,0:T(8,128)(2,1)S(1)}, u32[]{:S(2)}, u32[]{:S(2)}) collective-permute-start(bf16[16,4096]{1,0:T(8,128)(2,1)S(1)} %get-tuple-element.156), channel_id=1, source_target_pairs={{64,0},{128,64},{65,1},{129,65},{66,2},{130,66},{67,3},{131,67},{6... | collective-permute-start | bytes 393224 | tf_op jit(solution)/shard_map/ppermute | solution.py:341
  198.8 2.9 collective-permute-done.17.refs_0_.refs_7_
  218.4 2.7 collective-permute-start.25
  222.7 4.5 %collective-permute-done.26.refs_2_ = bf16[64,1280]{1,0:T(8,128)(2,1)S(1)} collective-permute-done((bf16[64,1280]{1,0:T(8,128)(2,1)}, bf16[64,1280]{1,0:T(8,128)(2,1)S(1)}, u32[]{:S(2)}, u32[]{:S(2)}) %collective-permute-start.26) | collective-permute-done | bytes 163872 | tf_op jit(solution)/shard_map/ppermute | solution.py:201
  227.3 3.5 %collective-permute-done.27.refs_3_ = bf16[64,1280]{1,0:T(8,128)(2,1)S(1)} collective-permute-done((bf16[64,1280]{1,0:T(8,128)(2,1)}, bf16[64,1280]{1,0:T(8,128)(2,1)S(1)}, u32[]{:S(2)}, u32[]{:S(2)}) %collective-permute-start.27) | collective-permute-done | bytes 163872 | tf_op jit(solution)/shard_map/ppermute | solution.py:201
  235.1 3.9 %all-to-all-start.1 = ((bf16[4,4,32,1024]{3,2,1,0:T(8,128)(2,1)}), bf16[4,4,32,1024]{3,2,1,0:T(8,128)(2,1)S(1)}, u32[]{:S(2)}, u32[]{:S(2)}) async-start(bf16[4,4,32,1024]{3,2,1,0:T(8,128)(2,1)} %bitcast.25), calls=%async_computation.1 | async-start | bytes 2097152 | tf_op jit(solution)/shard_map/all_to_all | solution.py:362
  243.3 10.2 %all-to-all-done.1 = bf16[4,4,32,1024]{3,2,1,0:T(8,128)(2,1)S(1)} async-done(((bf16[4,4,32,1024]{3,2,1,0:T(8,128)(2,1)}), bf16[4,4,32,1024]{3,2,1,0:T(8,128)(2,1)S(1)}, u32[]{:S(2)}, u32[]{:S(2)}) %all-to-all-start.1) | async-done | bytes 1048608 | tf_op jit(solution)/shard_map/all_to_all | solution.py:362
  254.5 6.4 %all-to-all-start.2 = ((bf16[4,32,1024]{2,1,0:T(8,128)(2,1)}), bf16[4,32,1024]{2,1,0:T(8,128)(2,1)S(1)}, u32[]{:S(2)}, u32[]{:S(2)}) async-start(bf16[4,32,1024]{2,1,0:T(8,128)(2,1)} %reduce_sum.66), calls=%async_computation.2 | async-start | bytes 524288 | tf_op jit(solution)/shard_map/all_to_all | solution.py:364
  261.8 7.4 %all-to-all-done.2 = bf16[4,32,1024]{2,1,0:T(8,128)(2,1)S(1)} async-done(((bf16[4,32,1024]{2,1,0:T(8,128)(2,1)}), bf16[4,32,1024]{2,1,0:T(8,128)(2,1)S(1)}, u32[]{:S(2)}, u32[]{:S(2)}) %all-to-all-start.2) | async-done | bytes 262176 | tf_op jit(solution)/shard_map/all_to_all | solution.py:364
  276.3 10.5 %all_gather.7 = f32[160,128]{1,0:T(8,128)S(1)} all-gather(f32[40,128]{1,0:T(8,128)S(1)} %pad.4), channel_id=1, replica_groups=mesh['s'=4,'x'=4,'zh'=4,'zl'=2,'c'=2] {'zl','c'}, dimensions={0}, use_global_device_ids=true | all-gather | bytes 102400 | tf_op jit(solution)/shard_map/all_gather | solution.py:394
  287.6 3.7 %all-to-all-start.3 = ((f32[16,40,128]{2,1,0:T(8,128)}), f32[16,40,128]{2,1,0:T(8,128)S(1)}, u32[]{:S(2)}, u32[]{:S(2)}) async-start(f32[16,40,128]{2,1,0:T(8,128)} %broadcast_in_dim.60), calls=%async_computation.3 | async-start | bytes 655360 | tf_op jit(solution)/shard_map/all_to_all | solution.py:397
  294.5 9.7 %all-to-all-done.3 = f32[16,40,128]{2,1,0:T(8,128)S(1)} async-done(((f32[16,40,128]{2,1,0:T(8,128)}), f32[16,40,128]{2,1,0:T(8,128)S(1)}, u32[]{:S(2)}, u32[]{:S(2)}) %all-to-all-start.3) | async-done | bytes 327712 | tf_op jit(solution)/shard_map/all_to_all | solution.py:397
  (194 shorter events, 110.4 us)
Async XLA Ops:
  7.2 92.0 %all-gather.2.cloned.1.call-start = ((), (), s32[]{:S(2)}) async-start(), calls=%async_computation.4 | async-start | bytes 8519680 | tf_op jit(solution)/shard_map/all_gather | solution.py:244
  11.8 14.2 %collective-permute-start = (f32[2,8,256]{2,1,0:T(8,128)}, f32[2,8,256]{2,1,0:T(8,128)S(1)}, u32[]{:S(2)}, u32[]{:S(2)}) collective-permute-start(f32[2,8,256]{2,1,0:T(8,128)} %bitcast.3.slot_ref), channel_id=1, source_target_pairs={{64,0},{128,64},{192,128},{0,192},{65,1},{129,65},{193,129},{1,193... | collective-permute-start | bytes 49160 | tf_op jit(solution)/shard_map/ppermute | solution.py:209
  15.4 10.7 %collective-permute-start.1 = (f32[2,8,256]{2,1,0:T(8,128)}, f32[2,8,256]{2,1,0:T(8,128)S(1)}, u32[]{:S(2)}, u32[]{:S(2)}) collective-permute-start(f32[2,8,256]{2,1,0:T(8,128)} %bitcast.3.slot_ref), channel_id=1, source_target_pairs={{128,0},{192,64},{0,128},{64,192},{129,1},{193,65},{1,129},{65,193... | collective-permute-start | bytes 49160 | tf_op jit(solution)/shard_map/ppermute | solution.py:209
  15.8 10.4 %collective-permute-start.2 = (f32[2,8,256]{2,1,0:T(8,128)}, f32[2,8,256]{2,1,0:T(8,128)S(1)}, u32[]{:S(2)}, u32[]{:S(2)}) collective-permute-start(f32[2,8,256]{2,1,0:T(8,128)} %bitcast.3.slot_ref), channel_id=1, source_target_pairs={{192,0},{0,64},{64,128},{128,192},{193,1},{1,65},{65,129},{129,193... | collective-permute-start | bytes 49160 | tf_op jit(solution)/shard_map/ppermute | solution.py:209
  21.9 8.5 %collective-permute-start.4 = (bf16[128,1024]{1,0:T(8,128)(2,1)}, bf16[128,1024]{1,0:T(8,128)(2,1)}, u32[]{:S(2)}, u32[]{:S(2)}) collective-permute-start(bf16[128,1024]{1,0:T(8,128)(2,1)} %get-tuple-element.113), channel_id=1, source_target_pairs={{0,2},{1,3},{2,0},{3,1},{4,6},{5,7},{6,4},{7,5},{8,10},{9,11},{10,... | collective-permute-start | bytes 786440 | tf_op jit(solution)/shard_map/ppermute | solution.py:201
  26.0 11.7 %collective-permute-start.5 = (bf16[128,1024]{1,0:T(8,128)(2,1)}, bf16[128,1024]{1,0:T(8,128)(2,1)S(1)}, u32[]{:S(2)}, u32[]{:S(2)}) collective-permute-start(bf16[128,1024]{1,0:T(8,128)(2,1)} %copy-done.30), channel_id=1, source_target_pairs={{0,3},{1,2},{2,1},{3,0},{4,7},{5,6},{6,5},{7,4},{8,11},{9,10},{10,... | collective-permute-start | bytes 786440 | tf_op jit(solution)/shard_map/ppermute | solution.py:201
  116.5 17.1 %collective-permute-start.9 = (bf16[16,4096]{1,0:T(8,128)(2,1)S(1)}, bf16[16,4096]{1,0:T(8,128)(2,1)S(1)}, u32[]{:S(2)}, u32[]{:S(2)}) collective-permute-start(bf16[16,4096]{1,0:T(8,128)(2,1)S(1)} %get-tuple-element.129), channel_id=1, source_target_pairs={{64,0},{128,64},{65,1},{129,65},{66,2},{130,66},{67,3},{131,67},{6... | collective-permute-start | bytes 393224 | tf_op jit(solution)/shard_map/ppermute | solution.py:341
  120.3 17.4 %collective-permute-start.12 = (bf16[16,4096]{1,0:T(8,128)(2,1)S(1)}, bf16[16,4096]{1,0:T(8,128)(2,1)S(1)}, u32[]{:S(2)}, u32[]{:S(2)}) collective-permute-start(bf16[16,4096]{1,0:T(8,128)(2,1)S(1)} %get-tuple-element.139), channel_id=1, source_target_pairs={{64,0},{128,64},{65,1},{129,65},{66,2},{130,66},{67,3},{131,67},{6... | collective-permute-start | bytes 393224 | tf_op jit(solution)/shard_map/ppermute | solution.py:341
  135.8 7.7 %collective-permute-start.11 = (bf16[16,4096]{1,0:T(8,128)(2,1)S(1)}, bf16[16,4096]{1,0:T(8,128)(2,1)S(1)}, u32[]{:S(2)}, u32[]{:S(2)}) collective-permute-start(bf16[16,4096]{1,0:T(8,128)(2,1)S(1)} %get-tuple-element.136), channel_id=1, source_target_pairs={{0,192},{64,0},{1,193},{65,1},{2,194},{66,2},{3,195},{67,3},{4,196... | collective-permute-start | bytes 393224 | tf_op jit(solution)/shard_map/ppermute | solution.py:341
  148.1 11.0 %collective-permute-start.13 = (bf16[16,4096]{1,0:T(8,128)(2,1)S(1)}, bf16[16,4096]{1,0:T(8,128)(2,1)S(1)}, u32[]{:S(2)}, u32[]{:S(2)}) collective-permute-start(bf16[16,4096]{1,0:T(8,128)(2,1)S(1)} %get-tuple-element.144), channel_id=1, source_target_pairs={{0,192},{192,128},{1,193},{193,129},{2,194},{194,130},{3,195},{195... | collective-permute-start | bytes 393224 | tf_op jit(solution)/shard_map/ppermute | solution.py:341
  151.2 10.1 %collective-permute-start.16 = (bf16[16,4096]{1,0:T(8,128)(2,1)S(1)}, bf16[16,4096]{1,0:T(8,128)(2,1)S(1)}, u32[]{:S(2)}, u32[]{:S(2)}) collective-permute-start(bf16[16,4096]{1,0:T(8,128)(2,1)S(1)} %get-tuple-element.151), channel_id=1, source_target_pairs={{0,192},{192,128},{1,193},{193,129},{2,194},{194,130},{3,195},{195... | collective-permute-start | bytes 393224 | tf_op jit(solution)/shard_map/ppermute | solution.py:341
  154.5 9.8 %collective-permute-start.19 = (bf16[64,1792]{1,0:T(8,128)(2,1)S(1)}, bf16[64,1792]{1,0:T(8,128)(2,1)S(1)}, u32[]{:S(2)}, u32[]{:S(2)}) collective-permute-start(bf16[64,1792]{1,0:T(8,128)(2,1)S(1)} %get-tuple-element.170), channel_id=1, source_target_pairs={{0,1},{1,0},{2,3},{3,2},{4,5},{5,4},{6,7},{7,6},{8,9},{9,8},{10,11... | collective-permute-start | bytes 688136 | tf_op jit(solution)/shard_map/ppermute | solution.py:201
  158.8 10.8 %collective-permute-start.21 = (bf16[64,1792]{1,0:T(8,128)(2,1)S(1)}, bf16[64,1792]{1,0:T(8,128)(2,1)S(1)}, u32[]{:S(2)}, u32[]{:S(2)}) collective-permute-start(bf16[64,1792]{1,0:T(8,128)(2,1)S(1)} %get-tuple-element.172), channel_id=1, source_target_pairs={{0,3},{1,2},{2,1},{3,0},{4,7},{5,6},{6,5},{7,4},{8,11},{9,10},{10,... | collective-permute-start | bytes 688136 | tf_op jit(solution)/shard_map/ppermute | solution.py:201
  163.6 8.4 %collective-permute-start.18 = (bf16[16,4096]{1,0:T(8,128)(2,1)S(1)}, bf16[16,4096]{1,0:T(8,128)(2,1)S(1)}, u32[]{:S(2)}, u32[]{:S(2)}) collective-permute-start(bf16[16,4096]{1,0:T(8,128)(2,1)S(1)} %get-tuple-element.157), channel_id=1, source_target_pairs={{128,64},{192,128},{129,65},{193,129},{130,66},{194,130},{131,67},... | collective-permute-start | bytes 393224 | tf_op jit(solution)/shard_map/ppermute | solution.py:341
  172.7 50.0 %all-to-all-start = ((bf16[16,32,1024]{2,1,0:T(8,128)(2,1)}), bf16[16,32,1024]{2,1,0:T(8,128)(2,1)}, u32[]{:S(2)}, u32[]{:S(2)}) async-start(bf16[16,32,1024]{2,1,0:T(8,128)(2,1)} %shard_map.146), calls=%async_computation | async-start | bytes 2097152 | tf_op jit(solution)/shard_map/all_to_all | solution.py:356
  182.8 18.9 %collective-permute-start.17 = (bf16[16,4096]{1,0:T(8,128)(2,1)S(1)}, bf16[16,4096]{1,0:T(8,128)(2,1)S(1)}, u32[]{:S(2)}, u32[]{:S(2)}) collective-permute-start(bf16[16,4096]{1,0:T(8,128)(2,1)S(1)} %get-tuple-element.156), channel_id=1, source_target_pairs={{64,0},{128,64},{65,1},{129,65},{66,2},{130,66},{67,3},{131,67},{6... | collective-permute-start | bytes 393224 | tf_op jit(solution)/shard_map/ppermute | solution.py:341
  197.5 9.1 %collective-permute-start.22 = (bf16[16,4096]{1,0:T(8,128)(2,1)S(1)}, bf16[16,4096]{1,0:T(8,128)(2,1)S(1)}, u32[]{:S(2)}, u32[]{:S(2)}) collective-permute-start(bf16[16,4096]{1,0:T(8,128)(2,1)S(1)} %get-tuple-element.183), channel_id=1, source_target_pairs={{64,0},{128,64},{65,1},{129,65},{66,2},{130,66},{67,3},{131,67},{6... | collective-permute-start | bytes 393224 | tf_op jit(solution)/shard_map/ppermute | solution.py:341
  222.6 8.2 %collective-permute-start.27 = (bf16[64,1280]{1,0:T(8,128)(2,1)}, bf16[64,1280]{1,0:T(8,128)(2,1)S(1)}, u32[]{:S(2)}, u32[]{:S(2)}) collective-permute-start(bf16[64,1280]{1,0:T(8,128)(2,1)} %get-tuple-element.207), channel_id=1, source_target_pairs={{0,3},{1,2},{2,1},{3,0},{4,7},{5,6},{6,5},{7,4},{8,11},{9,10},{10,... | collective-permute-start | bytes 491528 | tf_op jit(solution)/shard_map/ppermute | solution.py:201
  235.1 18.5 %all-to-all-start.1 = ((bf16[4,4,32,1024]{3,2,1,0:T(8,128)(2,1)}), bf16[4,4,32,1024]{3,2,1,0:T(8,128)(2,1)S(1)}, u32[]{:S(2)}, u32[]{:S(2)}) async-start(bf16[4,4,32,1024]{3,2,1,0:T(8,128)(2,1)} %bitcast.25), calls=%async_computation.1 | async-start | bytes 2097152 | tf_op jit(solution)/shard_map/all_to_all | solution.py:362
  241.8 19.9 %collective-permute-start.28 = (bf16[32,1024]{1,0:T(8,128)(2,1)S(1)}, bf16[32,1024]{1,0:T(8,128)(2,1)S(1)}, u32[]{:S(2)}, u32[]{:S(2)}) collective-permute-start(bf16[32,1024]{1,0:T(8,128)(2,1)S(1)} %multiply_convert_fusion.1), channel_id=1, source_target_pairs={{64,0},{128,64},{192,128},{0,192},{65,1},{129,65},{193,129},{1,193... | collective-permute-start | bytes 196616 | tf_op jit(solution)/shard_map/ppermute | solution.py:209
  241.9 19.9 %collective-permute-start.29 = (bf16[32,1024]{1,0:T(8,128)(2,1)S(1)}, bf16[32,1024]{1,0:T(8,128)(2,1)S(1)}, u32[]{:S(2)}, u32[]{:S(2)}) collective-permute-start(bf16[32,1024]{1,0:T(8,128)(2,1)S(1)} %multiply_convert_fusion.1), channel_id=1, source_target_pairs={{128,0},{192,64},{0,128},{64,192},{129,1},{193,65},{1,129},{65,193... | collective-permute-start | bytes 196616 | tf_op jit(solution)/shard_map/ppermute | solution.py:209
  243.3 18.4 %collective-permute-start.30 = (bf16[32,1024]{1,0:T(8,128)(2,1)S(1)}, bf16[32,1024]{1,0:T(8,128)(2,1)S(1)}, u32[]{:S(2)}, u32[]{:S(2)}) collective-permute-start(bf16[32,1024]{1,0:T(8,128)(2,1)S(1)} %multiply_convert_fusion.1), channel_id=1, source_target_pairs={{192,0},{0,64},{64,128},{128,192},{193,1},{1,65},{65,129},{129,193... | collective-permute-start | bytes 196616 | tf_op jit(solution)/shard_map/ppermute | solution.py:209
  254.5 14.8 %all-to-all-start.2 = ((bf16[4,32,1024]{2,1,0:T(8,128)(2,1)}), bf16[4,32,1024]{2,1,0:T(8,128)(2,1)S(1)}, u32[]{:S(2)}, u32[]{:S(2)}) async-start(bf16[4,32,1024]{2,1,0:T(8,128)(2,1)} %reduce_sum.66), calls=%async_computation.2 | async-start | bytes 524288 | tf_op jit(solution)/shard_map/all_to_all | solution.py:364
  287.6 16.6 %all-to-all-start.3 = ((f32[16,40,128]{2,1,0:T(8,128)}), f32[16,40,128]{2,1,0:T(8,128)S(1)}, u32[]{:S(2)}, u32[]{:S(2)}) async-start(f32[16,40,128]{2,1,0:T(8,128)} %broadcast_in_dim.60), calls=%async_computation.3 | async-start | bytes 655360 | tf_op jit(solution)/shard_map/all_to_all | solution.py:397
  (49 other events, 746.6 us)
Sparse Core Ops, SparseCore 0:
  11.9 87.2 all-gather.1

commit v4 on v3

--- a/solution.py
+++ b/solution.py
@@ -20,7 +20,7 @@
 LAST = (((1,), (1,)), ((), ()))
 FIRST = (((0,), (0,)), ((), ()))
 VMEM_LIMIT = 4 * 1024 * 1024
-HOP = 2
+HOP = 1
 
 
 def adapter_rows(g_ref, which, q):
@@ -342,17 +342,17 @@
         if tick == 1:
             low_first = low_of(1)
             arriving, low_first = lax.optimization_barrier((arriving, low_first))
-        if tick == 3:
+        if tick == HOP + 1:
             whole, arriving = lax.optimization_barrier((adapters[0], arriving))
             adapters[0] = whole[:, :, 0]
-        if tick == 6:
+        if tick == 2 * HOP + 2:
             low_second = low_of(0)
             arriving, low_second = lax.optimization_barrier((arriving, low_second))
         if tick == HOP * (sections - 1) + micros - 1:
             first = exchanged(1, low_first, low_second)
         if tick == HOP * (sections - 1) + micros + 1:
             early = partial_grads(1, first, first)
-            arriving, early = lax.optimization_barrier((arriving, early))
+            arriving, _ = lax.optimization_barrier((arriving, early))
             early = lax.all_to_all(early, RANKS, 0, 0)
         incoming.append(arriving)
     mixed = exchanged(0)

time: 318 us -> 310 us (0.975); the launches traced: 312 us -> 308 us
  waiting for transfers between devices: 133 us -> 157 us
  Pallas kernels: 52.1 us -> 36.7 us
  starting transfers between devices: 71.2 us -> 61.1 us
    ppermute x16 -> x10, waiting for transfers between devices: 17.4 us -> 35.8 us  [on_device(): arriving = lax.ppermute(result, 's', pairs)]
    pallas_call x26 -> x19, Pallas kernels: 52.1 us -> 36.7 us  [call(): pl.pallas_call(kernel, out_shape=out_shape, in_specs=[SMEM] * scalars + [...]
    ppermute x16 -> x10, starting transfers between devices: 32.2 us -> 17.1 us  [on_device(): arriving = lax.ppermute(result, 's', pairs)]
    ppermute x9, waiting for transfers between devices: 23.6 us -> 28.8 us  [swapped(): lax.ppermute(parts[d], axes, [(i, i ^ d) for i in range(count)])]
    ppermute x9, starting transfers between devices: 12.2 us -> 17.1 us  [swapped(): lax.ppermute(parts[d], axes, [(i, i ^ d) for i in range(count)])]
    unnamed x68 -> x54, local copies, waits for them, and re-layouts: 11.9 us -> 10.2 us
  transfers between devices with their start and end apart: 39 -> 33, of which waited for: 17 -> 21; matrix products, arithmetic and copies ran while one was open for 4% -> 4% of each run, Pallas kernels for 13% -> 4%
where the time goes in v4:
time: 310 us; the launch traced here: 308 us
  waiting for transfers between devices  157 us (51%)
  starting transfers between devices  61.1 us (20%)
  Pallas kernels  36.7 us (12%)
  local copies, waits for them, and re-layouts  17.3 us (6%)
  between operations  14.6 us (5%)
  blocking collectives  10.5 us (3%)
  other arithmetic  7.21 us (2%)
  matrix products  3.8 us (1%)
    all_gather x1, waiting for transfers between devices, on_device(): lax.all_gather(mine.reshape(blocks * 2 * combos, width), DP, axis=0, tile...  60.8 us
    pallas_call x19, Pallas kernels, call(): pl.pallas_call(kernel, out_shape=out_shape, in_specs=[SMEM] * scalars + [...  36.7 us
    ppermute x10, waiting for transfers between devices, on_device(): arriving = lax.ppermute(result, 's', pairs)  35.8 us
    ppermute x9, waiting for transfers between devices, swapped(): lax.ppermute(parts[d], axes, [(i, i ^ d) for i in range(count)])  28.8 us
    ppermute x10, starting transfers between devices, on_device(): arriving = lax.ppermute(result, 's', pairs)  17.1 us
    ppermute x9, starting transfers between devices, swapped(): lax.ppermute(parts[d], axes, [(i, i ^ d) for i in range(count)])  17.1 us
    all_gather x1, blocking collectives, on_device(): got = lax.all_gather(held, QUARTERS, axis=0, tiled=True)  10.5 us
    all_to_all x1, waiting for transfers between devices, on_device(): part = lax.all_to_all(part, 'x', 0, 0)  10.3 us
  transfers between devices with their start and end apart: 33, of which 21 were waited for; matrix products, arithmetic and copies ran while one was open for 4% of the time, Pallas kernels for 4%

profile of v4, /device:TPU:1, one launch (start us, length us, event | category | flops | bytes accessed | tf_op | source)
XLA Modules:
  0.0 308.1 jit_solution(15032354989109541932)
XLA Ops:
  11.8 3.6 %collective-permute-start = (f32[2,8,256]{2,1,0:T(8,128)}, f32[2,8,256]{2,1,0:T(8,128)S(1)}, u32[]{:S(2)}, u32[]{:S(2)}) collective-permute-start(f32[2,8,256]{2,1,0:T(8,128)} %bitcast.2.slot_ref), channel_id=1, source_target_pairs={{64,0},{128,64},{192,128},{0,192},{65,1},{129,65},{193,129},{1,193... | collective-permute-start | bytes 49160 | tf_op jit(solution)/shard_map/ppermute | solution.py:209
  27.5 2.9 collective-permute-done.4.refs_10_
  30.4 7.3 %collective-permute-done.5.refs_11_ = bf16[128,1024]{1,0:T(8,128)(2,1)S(1)} collective-permute-done((bf16[128,1024]{1,0:T(8,128)(2,1)}, bf16[128,1024]{1,0:T(8,128)(2,1)S(1)}, u32[]{:S(2)}, u32[]{:S(2)}) %collective-permute-start.5) | collective-permute-done | bytes 262176 | tf_op jit(solution)/shard_map/ppermute | solution.py:201
  38.4 60.8 %all-gather.2.cloned.1.call-done = bf16[4096,1024]{1,0:T(8,128)(2,1)} async-done(((bf16[64,1024]{1,0:T(8,128)(2,1)}), bf16[4096,1024]{1,0:T(8,128)(2,1)}) %all-gather.2.cloned.1.call-update) | async-done | bytes 8388624 | tf_op jit(solution)/shard_map/all_gather | solution.py:244
  112.0 14.6 %collective-permute-done.8.refs_1_.refs_6_ = bf16[16,4096]{1,0:T(8,128)(2,1)S(1)} collective-permute-done((bf16[16,4096]{1,0:T(8,128)(2,1)S(1)}, bf16[16,4096]{1,0:T(8,128)(2,1)S(1)}, u32[]{:S(2)}, u32[]{:S(2)}) %collective-permute-start.8) | collective-permute-done | bytes 131104 | tf_op jit(solution)/shard_map/ppermute | solution.py:341
  141.9 3.2 %collective-permute-start.11 = (bf16[16,4096]{1,0:T(8,128)(2,1)S(1)}, bf16[16,4096]{1,0:T(8,128)(2,1)S(1)}, u32[]{:S(2)}, u32[]{:S(2)}) collective-permute-start(bf16[16,4096]{1,0:T(8,128)(2,1)S(1)} %get-tuple-element.111), channel_id=1, source_target_pairs={{0,192},{64,0},{128,64},{192,128},{1,193},{65,1},{129,65},{193,129... | collective-permute-start | bytes 393224 | tf_op jit(solution)/shard_map/ppermute | solution.py:341
  150.6 6.3 %collective-permute-start.15 = (bf16[64,1792]{1,0:T(8,128)(2,1)S(1)}, bf16[64,1792]{1,0:T(8,128)(2,1)S(1)}, u32[]{:S(2)}, u32[]{:S(2)}) collective-permute-start(bf16[64,1792]{1,0:T(8,128)(2,1)S(1)} %get-tuple-element.130), channel_id=1, source_target_pairs={{0,1},{1,0},{2,3},{3,2},{4,5},{5,4},{6,7},{7,6},{8,9},{9,8},{10,11... | collective-permute-start | bytes 688136 | tf_op jit(solution)/shard_map/ppermute | solution.py:201
  158.6 5.4 %collective-permute-done.16.refs_2_.refs_6_ = bf16[64,1792]{1,0:T(8,128)(2,1)S(1)} collective-permute-done((bf16[64,1792]{1,0:T(8,128)(2,1)S(1)}, bf16[64,1792]{1,0:T(8,128)(2,1)S(1)}, u32[]{:S(2)}, u32[]{:S(2)}) %collective-permute-start.16) | collective-permute-done | bytes 229408 | tf_op jit(solution)/shard_map/ppermute | solution.py:201
  164.0 5.1 %collective-permute-done.17.refs_3_.refs_7_ = bf16[64,1792]{1,0:T(8,128)(2,1)S(1)} collective-permute-done((bf16[64,1792]{1,0:T(8,128)(2,1)S(1)}, bf16[64,1792]{1,0:T(8,128)(2,1)S(1)}, u32[]{:S(2)}, u32[]{:S(2)}) %collective-permute-start.17) | collective-permute-done | bytes 229408 | tf_op jit(solution)/shard_map/ppermute | solution.py:201
  171.5 5.0 %all-to-all-start = ((bf16[16,32,1024]{2,1,0:T(8,128)(2,1)}), bf16[16,32,1024]{2,1,0:T(8,128)(2,1)}, u32[]{:S(2)}, u32[]{:S(2)}) async-start(bf16[16,32,1024]{2,1,0:T(8,128)(2,1)} %shard_map.142), calls=%async_computation | async-start | bytes 2097152 | tf_op jit(solution)/shard_map/all_to_all | solution.py:356
  176.5 3.5 %collective-permute-start.12 = (bf16[16,4096]{1,0:T(8,128)(2,1)}, bf16[16,4096]{1,0:T(8,128)(2,1)S(1)}, u32[]{:S(2)}, u32[]{:S(2)}) collective-permute-start(bf16[16,4096]{1,0:T(8,128)(2,1)} %copy-done.16), channel_id=1, source_target_pairs={{0,192},{64,0},{128,64},{192,128},{1,193},{65,1},{129,65},{193,129... | collective-permute-start | bytes 393224 | tf_op jit(solution)/shard_map/ppermute | solution.py:341
  188.6 4.6 %collective-permute-done.13.refs_0_.refs_5_ = bf16[16,4096]{1,0:T(8,128)(2,1)S(1)} collective-permute-done((bf16[16,4096]{1,0:T(8,128)(2,1)S(1)}, bf16[16,4096]{1,0:T(8,128)(2,1)S(1)}, u32[]{:S(2)}, u32[]{:S(2)}) %collective-permute-start.13) | collective-permute-done | bytes 131104 | tf_op jit(solution)/shard_map/ppermute | solution.py:341
  196.7 4.7 %collective-permute-done.14.refs_0_.refs_6_ = bf16[16,4096]{1,0:T(8,128)(2,1)S(1)} collective-permute-done((bf16[16,4096]{1,0:T(8,128)(2,1)S(1)}, bf16[16,4096]{1,0:T(8,128)(2,1)S(1)}, u32[]{:S(2)}, u32[]{:S(2)}) %collective-permute-start.14) | collective-permute-done | bytes 131104 | tf_op jit(solution)/shard_map/ppermute | solution.py:341
  204.9 4.4 %collective-permute-done.18.refs_0_.refs_7_ = bf16[16,4096]{1,0:T(8,128)(2,1)S(1)} collective-permute-done((bf16[16,4096]{1,0:T(8,128)(2,1)S(1)}, bf16[16,4096]{1,0:T(8,128)(2,1)S(1)}, u32[]{:S(2)}, u32[]{:S(2)}) %collective-permute-start.18) | collective-permute-done | bytes 131104 | tf_op jit(solution)/shard_map/ppermute | solution.py:341
  213.0 4.2 %collective-permute-start.19 = (bf16[64,1280]{1,0:T(8,128)(2,1)}, bf16[64,1280]{1,0:T(8,128)(2,1)S(1)}, u32[]{:S(2)}, u32[]{:S(2)}) collective-permute-start(bf16[64,1280]{1,0:T(8,128)(2,1)} %get-tuple-element.151), channel_id=1, source_target_pairs={{0,1},{1,0},{2,3},{3,2},{4,5},{5,4},{6,7},{7,6},{8,9},{9,8},{10,11... | collective-permute-start | bytes 491528 | tf_op jit(solution)/shard_map/ppermute | solution.py:201
  218.8 4.4 %collective-permute-done.20.refs_2_ = bf16[64,1280]{1,0:T(8,128)(2,1)S(1)} collective-permute-done((bf16[64,1280]{1,0:T(8,128)(2,1)}, bf16[64,1280]{1,0:T(8,128)(2,1)S(1)}, u32[]{:S(2)}, u32[]{:S(2)}) %collective-permute-start.20) | collective-permute-done | bytes 163872 | tf_op jit(solution)/shard_map/ppermute | solution.py:201
  223.3 3.6 %collective-permute-done.21.refs_3_ = bf16[64,1280]{1,0:T(8,128)(2,1)S(1)} collective-permute-done((bf16[64,1280]{1,0:T(8,128)(2,1)}, bf16[64,1280]{1,0:T(8,128)(2,1)S(1)}, u32[]{:S(2)}, u32[]{:S(2)}) %collective-permute-start.21) | collective-permute-done | bytes 163872 | tf_op jit(solution)/shard_map/ppermute | solution.py:201
  231.2 4.0 %all-to-all-start.1 = ((bf16[4,4,32,1024]{3,2,1,0:T(8,128)(2,1)}), bf16[4,4,32,1024]{3,2,1,0:T(8,128)(2,1)S(1)}, u32[]{:S(2)}, u32[]{:S(2)}) async-start(bf16[4,4,32,1024]{3,2,1,0:T(8,128)(2,1)} %bitcast.25), calls=%async_computation.1 | async-start | bytes 2097152 | tf_op jit(solution)/shard_map/all_to_all | solution.py:362
  239.5 10.3 %all-to-all-done.1 = bf16[4,4,32,1024]{3,2,1,0:T(8,128)(2,1)S(1)} async-done(((bf16[4,4,32,1024]{3,2,1,0:T(8,128)(2,1)}), bf16[4,4,32,1024]{3,2,1,0:T(8,128)(2,1)S(1)}, u32[]{:S(2)}, u32[]{:S(2)}) %all-to-all-start.1) | async-done | bytes 1048608 | tf_op jit(solution)/shard_map/all_to_all | solution.py:362
  250.7 6.4 %all-to-all-start.2 = ((bf16[4,32,1024]{2,1,0:T(8,128)(2,1)}), bf16[4,32,1024]{2,1,0:T(8,128)(2,1)S(1)}, u32[]{:S(2)}, u32[]{:S(2)}) async-start(bf16[4,32,1024]{2,1,0:T(8,128)(2,1)} %reduce_sum.66), calls=%async_computation.2 | async-start | bytes 524288 | tf_op jit(solution)/shard_map/all_to_all | solution.py:364
  258.0 7.4 %all-to-all-done.2 = bf16[4,32,1024]{2,1,0:T(8,128)(2,1)S(1)} async-done(((bf16[4,32,1024]{2,1,0:T(8,128)(2,1)}), bf16[4,32,1024]{2,1,0:T(8,128)(2,1)S(1)}, u32[]{:S(2)}, u32[]{:S(2)}) %all-to-all-start.2) | async-done | bytes 262176 | tf_op jit(solution)/shard_map/all_to_all | solution.py:364
  272.1 10.5 %all_gather.7 = f32[160,128]{1,0:T(8,128)S(1)} all-gather(f32[40,128]{1,0:T(8,128)S(1)} %pad.4), channel_id=1, replica_groups=mesh['s'=4,'x'=4,'zh'=4,'zl'=2,'c'=2] {'zl','c'}, dimensions={0}, use_global_device_ids=true | all-gather | bytes 102400 | tf_op jit(solution)/shard_map/all_gather | solution.py:394
  283.4 3.7 %all-to-all-start.3 = ((f32[16,40,128]{2,1,0:T(8,128)}), f32[16,40,128]{2,1,0:T(8,128)S(1)}, u32[]{:S(2)}, u32[]{:S(2)}) async-start(f32[16,40,128]{2,1,0:T(8,128)} %broadcast_in_dim.60), calls=%async_computation.3 | async-start | bytes 655360 | tf_op jit(solution)/shard_map/all_to_all | solution.py:397
  290.2 9.7 %all-to-all-done.3 = f32[16,40,128]{2,1,0:T(8,128)S(1)} async-done(((f32[16,40,128]{2,1,0:T(8,128)}), f32[16,40,128]{2,1,0:T(8,128)S(1)}, u32[]{:S(2)}, u32[]{:S(2)}) %all-to-all-start.3) | async-done | bytes 327712 | tf_op jit(solution)/shard_map/all_to_all | solution.py:397
  (161 shorter events, 97.9 us)
Async XLA Ops:
  7.2 92.0 %all-gather.2.cloned.1.call-start = ((), (), s32[]{:S(2)}) async-start(), calls=%async_computation.4 | async-start | bytes 8519680 | tf_op jit(solution)/shard_map/all_gather | solution.py:244
  11.8 14.2 %collective-permute-start = (f32[2,8,256]{2,1,0:T(8,128)}, f32[2,8,256]{2,1,0:T(8,128)S(1)}, u32[]{:S(2)}, u32[]{:S(2)}) collective-permute-start(f32[2,8,256]{2,1,0:T(8,128)} %bitcast.2.slot_ref), channel_id=1, source_target_pairs={{64,0},{128,64},{192,128},{0,192},{65,1},{129,65},{193,129},{1,193... | collective-permute-start | bytes 49160 | tf_op jit(solution)/shard_map/ppermute | solution.py:209
  15.4 10.7 %collective-permute-start.1 = (f32[2,8,256]{2,1,0:T(8,128)}, f32[2,8,256]{2,1,0:T(8,128)S(1)}, u32[]{:S(2)}, u32[]{:S(2)}) collective-permute-start(f32[2,8,256]{2,1,0:T(8,128)} %bitcast.2.slot_ref), channel_id=1, source_target_pairs={{128,0},{192,64},{0,128},{64,192},{129,1},{193,65},{1,129},{65,193... | collective-permute-start | bytes 49160 | tf_op jit(solution)/shard_map/ppermute | solution.py:209
  15.8 10.4 %collective-permute-start.2 = (f32[2,8,256]{2,1,0:T(8,128)}, f32[2,8,256]{2,1,0:T(8,128)S(1)}, u32[]{:S(2)}, u32[]{:S(2)}) collective-permute-start(f32[2,8,256]{2,1,0:T(8,128)} %bitcast.2.slot_ref), channel_id=1, source_target_pairs={{192,0},{0,64},{64,128},{128,192},{193,1},{1,65},{65,129},{129,193... | collective-permute-start | bytes 49160 | tf_op jit(solution)/shard_map/ppermute | solution.py:209
  20.4 7.1 %collective-permute-start.3 = (bf16[128,1024]{1,0:T(8,128)(2,1)}, bf16[128,1024]{1,0:T(8,128)(2,1)S(1)}, u32[]{:S(2)}, u32[]{:S(2)}) collective-permute-start(bf16[128,1024]{1,0:T(8,128)(2,1)} %get-tuple-element.85), channel_id=1, source_target_pairs={{0,1},{1,0},{2,3},{3,2},{4,5},{5,4},{6,7},{7,6},{8,9},{9,8},{10,11... | collective-permute-start | bytes 786440 | tf_op jit(solution)/shard_map/ppermute | solution.py:201
  21.9 8.5 %collective-permute-start.4 = (bf16[128,1024]{1,0:T(8,128)(2,1)}, bf16[128,1024]{1,0:T(8,128)(2,1)}, u32[]{:S(2)}, u32[]{:S(2)}) collective-permute-start(bf16[128,1024]{1,0:T(8,128)(2,1)} %get-tuple-element.86), channel_id=1, source_target_pairs={{0,2},{1,3},{2,0},{3,1},{4,6},{5,7},{6,4},{7,5},{8,10},{9,11},{10,... | collective-permute-start | bytes 786440 | tf_op jit(solution)/shard_map/ppermute | solution.py:201
  26.0 11.7 %collective-permute-start.5 = (bf16[128,1024]{1,0:T(8,128)(2,1)}, bf16[128,1024]{1,0:T(8,128)(2,1)S(1)}, u32[]{:S(2)}, u32[]{:S(2)}) collective-permute-start(bf16[128,1024]{1,0:T(8,128)(2,1)} %copy-done.23), channel_id=1, source_target_pairs={{0,3},{1,2},{2,1},{3,0},{4,7},{5,6},{6,5},{7,4},{8,11},{9,10},{10,... | collective-permute-start | bytes 786440 | tf_op jit(solution)/shard_map/ppermute | solution.py:201
  110.7 15.9 %collective-permute-start.8 = (bf16[16,4096]{1,0:T(8,128)(2,1)S(1)}, bf16[16,4096]{1,0:T(8,128)(2,1)S(1)}, u32[]{:S(2)}, u32[]{:S(2)}) collective-permute-start(bf16[16,4096]{1,0:T(8,128)(2,1)S(1)} %get-tuple-element.99), channel_id=1, source_target_pairs={{64,0},{128,64},{192,128},{65,1},{129,65},{193,129},{66,2},{130,66... | collective-permute-start | bytes 393224 | tf_op jit(solution)/shard_map/ppermute | solution.py:341
  150.6 8.0 %collective-permute-start.15 = (bf16[64,1792]{1,0:T(8,128)(2,1)S(1)}, bf16[64,1792]{1,0:T(8,128)(2,1)S(1)}, u32[]{:S(2)}, u32[]{:S(2)}) collective-permute-start(bf16[64,1792]{1,0:T(8,128)(2,1)S(1)} %get-tuple-element.130), channel_id=1, source_target_pairs={{0,1},{1,0},{2,3},{3,2},{4,5},{5,4},{6,7},{7,6},{8,9},{9,8},{10,11... | collective-permute-start | bytes 688136 | tf_op jit(solution)/shard_map/ppermute | solution.py:201
  156.9 7.2 %collective-permute-start.16 = (bf16[64,1792]{1,0:T(8,128)(2,1)S(1)}, bf16[64,1792]{1,0:T(8,128)(2,1)S(1)}, u32[]{:S(2)}, u32[]{:S(2)}) collective-permute-start(bf16[64,1792]{1,0:T(8,128)(2,1)S(1)} %get-tuple-element.131), channel_id=1, source_target_pairs={{0,2},{1,3},{2,0},{3,1},{4,6},{5,7},{6,4},{7,5},{8,10},{9,11},{10,... | collective-permute-start | bytes 688136 | tf_op jit(solution)/shard_map/ppermute | solution.py:201
  158.3 10.8 %collective-permute-start.17 = (bf16[64,1792]{1,0:T(8,128)(2,1)S(1)}, bf16[64,1792]{1,0:T(8,128)(2,1)S(1)}, u32[]{:S(2)}, u32[]{:S(2)}) collective-permute-start(bf16[64,1792]{1,0:T(8,128)(2,1)S(1)} %get-tuple-element.132), channel_id=1, source_target_pairs={{0,3},{1,2},{2,1},{3,0},{4,7},{5,6},{6,5},{7,4},{8,11},{9,10},{10,... | collective-permute-start | bytes 688136 | tf_op jit(solution)/shard_map/ppermute | solution.py:201
  171.5 47.3 %all-to-all-start = ((bf16[16,32,1024]{2,1,0:T(8,128)(2,1)}), bf16[16,32,1024]{2,1,0:T(8,128)(2,1)}, u32[]{:S(2)}, u32[]{:S(2)}) async-start(bf16[16,32,1024]{2,1,0:T(8,128)(2,1)} %shard_map.142), calls=%async_computation | async-start | bytes 2097152 | tf_op jit(solution)/shard_map/all_to_all | solution.py:356
  176.5 6.1 %collective-permute-start.12 = (bf16[16,4096]{1,0:T(8,128)(2,1)}, bf16[16,4096]{1,0:T(8,128)(2,1)S(1)}, u32[]{:S(2)}, u32[]{:S(2)}) collective-permute-start(bf16[16,4096]{1,0:T(8,128)(2,1)} %copy-done.16), channel_id=1, source_target_pairs={{0,192},{64,0},{128,64},{192,128},{1,193},{65,1},{129,65},{193,129... | collective-permute-start | bytes 393224 | tf_op jit(solution)/shard_map/ppermute | solution.py:341
  187.1 6.1 %collective-permute-start.13 = (bf16[16,4096]{1,0:T(8,128)(2,1)S(1)}, bf16[16,4096]{1,0:T(8,128)(2,1)S(1)}, u32[]{:S(2)}, u32[]{:S(2)}) collective-permute-start(bf16[16,4096]{1,0:T(8,128)(2,1)S(1)} %get-tuple-element.117), channel_id=1, source_target_pairs={{64,0},{128,64},{192,128},{65,1},{129,65},{193,129},{66,2},{130,66... | collective-permute-start | bytes 393224 | tf_op jit(solution)/shard_map/ppermute | solution.py:341
  195.4 6.0 %collective-permute-start.14 = (bf16[16,4096]{1,0:T(8,128)(2,1)S(1)}, bf16[16,4096]{1,0:T(8,128)(2,1)S(1)}, u32[]{:S(2)}, u32[]{:S(2)}) collective-permute-start(bf16[16,4096]{1,0:T(8,128)(2,1)S(1)} %get-tuple-element.120), channel_id=1, source_target_pairs={{64,0},{128,64},{65,1},{129,65},{66,2},{130,66},{67,3},{131,67},{6... | collective-permute-start | bytes 393224 | tf_op jit(solution)/shard_map/ppermute | solution.py:341
  213.0 5.8 %collective-permute-start.19 = (bf16[64,1280]{1,0:T(8,128)(2,1)}, bf16[64,1280]{1,0:T(8,128)(2,1)S(1)}, u32[]{:S(2)}, u32[]{:S(2)}) collective-permute-start(bf16[64,1280]{1,0:T(8,128)(2,1)} %get-tuple-element.151), channel_id=1, source_target_pairs={{0,1},{1,0},{2,3},{3,2},{4,5},{5,4},{6,7},{7,6},{8,9},{9,8},{10,11... | collective-permute-start | bytes 491528 | tf_op jit(solution)/shard_map/ppermute | solution.py:201
  217.2 6.1 %collective-permute-start.20 = (bf16[64,1280]{1,0:T(8,128)(2,1)}, bf16[64,1280]{1,0:T(8,128)(2,1)S(1)}, u32[]{:S(2)}, u32[]{:S(2)}) collective-permute-start(bf16[64,1280]{1,0:T(8,128)(2,1)} %get-tuple-element.152), channel_id=1, source_target_pairs={{0,2},{1,3},{2,0},{3,1},{4,6},{5,7},{6,4},{7,5},{8,10},{9,11},{10,... | collective-permute-start | bytes 491528 | tf_op jit(solution)/shard_map/ppermute | solution.py:201
  218.7 8.2 %collective-permute-start.21 = (bf16[64,1280]{1,0:T(8,128)(2,1)}, bf16[64,1280]{1,0:T(8,128)(2,1)S(1)}, u32[]{:S(2)}, u32[]{:S(2)}) collective-permute-start(bf16[64,1280]{1,0:T(8,128)(2,1)} %get-tuple-element.153), channel_id=1, source_target_pairs={{0,3},{1,2},{2,1},{3,0},{4,7},{5,6},{6,5},{7,4},{8,11},{9,10},{10,... | collective-permute-start | bytes 491528 | tf_op jit(solution)/shard_map/ppermute | solution.py:201
  231.2 18.6 %all-to-all-start.1 = ((bf16[4,4,32,1024]{3,2,1,0:T(8,128)(2,1)}), bf16[4,4,32,1024]{3,2,1,0:T(8,128)(2,1)S(1)}, u32[]{:S(2)}, u32[]{:S(2)}) async-start(bf16[4,4,32,1024]{3,2,1,0:T(8,128)(2,1)} %bitcast.25), calls=%async_computation.1 | async-start | bytes 2097152 | tf_op jit(solution)/shard_map/all_to_all | solution.py:362
  237.9 20.0 %collective-permute-start.22 = (bf16[32,1024]{1,0:T(8,128)(2,1)S(1)}, bf16[32,1024]{1,0:T(8,128)(2,1)S(1)}, u32[]{:S(2)}, u32[]{:S(2)}) collective-permute-start(bf16[32,1024]{1,0:T(8,128)(2,1)S(1)} %multiply_convert_fusion.1), channel_id=1, source_target_pairs={{64,0},{128,64},{192,128},{0,192},{65,1},{129,65},{193,129},{1,193... | collective-permute-start | bytes 196616 | tf_op jit(solution)/shard_map/ppermute | solution.py:209
  238.0 19.9 %collective-permute-start.23 = (bf16[32,1024]{1,0:T(8,128)(2,1)S(1)}, bf16[32,1024]{1,0:T(8,128)(2,1)S(1)}, u32[]{:S(2)}, u32[]{:S(2)}) collective-permute-start(bf16[32,1024]{1,0:T(8,128)(2,1)S(1)} %multiply_convert_fusion.1), channel_id=1, source_target_pairs={{128,0},{192,64},{0,128},{64,192},{129,1},{193,65},{1,129},{65,193... | collective-permute-start | bytes 196616 | tf_op jit(solution)/shard_map/ppermute | solution.py:209
  239.0 18.9 %collective-permute-start.24 = (bf16[32,1024]{1,0:T(8,128)(2,1)S(1)}, bf16[32,1024]{1,0:T(8,128)(2,1)S(1)}, u32[]{:S(2)}, u32[]{:S(2)}) collective-permute-start(bf16[32,1024]{1,0:T(8,128)(2,1)S(1)} %multiply_convert_fusion.1), channel_id=1, source_target_pairs={{192,0},{0,64},{64,128},{128,192},{193,1},{1,65},{65,129},{129,193... | collective-permute-start | bytes 196616 | tf_op jit(solution)/shard_map/ppermute | solution.py:209
  250.7 14.8 %all-to-all-start.2 = ((bf16[4,32,1024]{2,1,0:T(8,128)(2,1)}), bf16[4,32,1024]{2,1,0:T(8,128)(2,1)S(1)}, u32[]{:S(2)}, u32[]{:S(2)}) async-start(bf16[4,32,1024]{2,1,0:T(8,128)(2,1)} %reduce_sum.66), calls=%async_computation.2 | async-start | bytes 524288 | tf_op jit(solution)/shard_map/all_to_all | solution.py:364
  283.4 16.6 %all-to-all-start.3 = ((f32[16,40,128]{2,1,0:T(8,128)}), f32[16,40,128]{2,1,0:T(8,128)S(1)}, u32[]{:S(2)}, u32[]{:S(2)}) async-start(f32[16,40,128]{2,1,0:T(8,128)} %broadcast_in_dim.60), calls=%async_computation.3 | async-start | bytes 655360 | tf_op jit(solution)/shard_map/all_to_all | solution.py:397
  (36 other events, 648.8 us)
Sparse Core Ops, SparseCore 0:
  11.9 87.2 all-gather.1

commit v5 on v4

--- a/solution.py
+++ b/solution.py
@@ -349,10 +349,11 @@
             low_second = low_of(0)
             arriving, low_second = lax.optimization_barrier((arriving, low_second))
         if tick == HOP * (sections - 1) + micros - 1:
+            arriving, dus[-1] = lax.optimization_barrier((arriving, dus[-1]))
             first = exchanged(1, low_first, low_second)
-        if tick == HOP * (sections - 1) + micros + 1:
+        if tick == HOP * (sections - 1) + micros:
             early = partial_grads(1, first, first)
-            arriving, _ = lax.optimization_barrier((arriving, early))
+            arriving, early = lax.optimization_barrier((arriving, early))
             early = lax.all_to_all(early, RANKS, 0, 0)
         incoming.append(arriving)
     mixed = exchanged(0)

time: 310 us -> 303 us (0.977)
  waiting for transfers between devices: 157 us -> 149 us
    ppermute x10, waiting for transfers between devices: 35.8 us -> 31.5 us  [on_device(): arriving = lax.ppermute(result, 's', pairs)]
    ppermute x9, waiting for transfers between devices: 28.8 us -> 25.2 us  [swapped(): lax.ppermute(parts[d], axes, [(i, i ^ d) for i in range(count)])]
    unnamed x54 -> x66, local copies, waits for them, and re-layouts: 10.2 us -> 12.7 us
  transfers between devices with their start and end apart: 33 -> 33, of which waited for: 21 -> 20; matrix products, arithmetic and copies ran while one was open for 4% -> 4% of each run, Pallas kernels for 4% -> 5%
where the time goes in v5:
time: 303 us; the launch traced here: 301 us
  waiting for transfers between devices  149 us (49%)
  starting transfers between devices  59.6 us (20%)
  Pallas kernels  36.7 us (12%)
  local copies, waits for them, and re-layouts  19.8 us (7%)
  between operations  14.7 us (5%)
  blocking collectives  10.5 us (3%)
  other arithmetic  7.21 us (2%)
  matrix products  3.8 us (1%)
    all_gather x1, waiting for transfers between devices, on_device(): lax.all_gather(mine.reshape(blocks * 2 * combos, width), DP, axis=0, tile...  60.8 us
    pallas_call x19, Pallas kernels, call(): pl.pallas_call(kernel, out_shape=out_shape, in_specs=[SMEM] * scalars + [...  36.7 us
    ppermute x10, waiting for transfers between devices, on_device(): arriving = lax.ppermute(result, 's', pairs)  31.5 us
    ppermute x9, waiting for transfers between devices, swapped(): lax.ppermute(parts[d], axes, [(i, i ^ d) for i in range(count)])  25.2 us
    ppermute x10, starting transfers between devices, on_device(): arriving = lax.ppermute(result, 's', pairs)  16.6 us
    ppermute x9, starting transfers between devices, swapped(): lax.ppermute(parts[d], axes, [(i, i ^ d) for i in range(count)])  16.1 us
    unnamed x66, local copies, waits for them, and re-layouts  12.7 us
    all_gather x1, blocking collectives, on_device(): got = lax.all_gather(held, QUARTERS, axis=0, tiled=True)  10.5 us
  transfers between devices with their start and end apart: 33, of which 20 were waited for; matrix products, arithmetic and copies ran while one was open for 4% of the time, Pallas kernels for 5%

profile of v5, /device:TPU:1, one launch (start us, length us, event | category | flops | bytes accessed | tf_op | source)
XLA Modules:
  0.0 301.3 jit_solution(13692865318641016256)
XLA Ops:
  11.8 3.6 %collective-permute-start = (f32[2,8,256]{2,1,0:T(8,128)}, f32[2,8,256]{2,1,0:T(8,128)S(1)}, u32[]{:S(2)}, u32[]{:S(2)}) collective-permute-start(f32[2,8,256]{2,1,0:T(8,128)} %bitcast.2.slot_ref), channel_id=1, source_target_pairs={{64,0},{128,64},{192,128},{0,192},{65,1},{129,65},{193,129},{1,193... | collective-permute-start | bytes 49160 | tf_op jit(solution)/shard_map/ppermute | solution.py:209
  27.5 2.9 collective-permute-done.4.refs_10_
  30.4 7.3 %collective-permute-done.5.refs_11_ = bf16[128,1024]{1,0:T(8,128)(2,1)S(1)} collective-permute-done((bf16[128,1024]{1,0:T(8,128)(2,1)}, bf16[128,1024]{1,0:T(8,128)(2,1)S(1)}, u32[]{:S(2)}, u32[]{:S(2)}) %collective-permute-start.5) | collective-permute-done | bytes 262176 | tf_op jit(solution)/shard_map/ppermute | solution.py:201
  38.4 60.8 %all-gather.2.cloned.1.call-done = bf16[4096,1024]{1,0:T(8,128)(2,1)} async-done(((bf16[64,1024]{1,0:T(8,128)(2,1)}), bf16[4096,1024]{1,0:T(8,128)(2,1)}) %all-gather.2.cloned.1.call-update) | async-done | bytes 8388624 | tf_op jit(solution)/shard_map/all_gather | solution.py:244
  99.2 2.6 slice_bitcast_fusion.1.refs_4_.refs_5_.g_ref
  112.0 14.6 %collective-permute-done.8.refs_1_.refs_6_ = bf16[16,4096]{1,0:T(8,128)(2,1)S(1)} collective-permute-done((bf16[16,4096]{1,0:T(8,128)(2,1)S(1)}, bf16[16,4096]{1,0:T(8,128)(2,1)S(1)}, u32[]{:S(2)}, u32[]{:S(2)}) %collective-permute-start.8) | collective-permute-done | bytes 131104 | tf_op jit(solution)/shard_map/ppermute | solution.py:341
  132.7 2.4 shard_map.135
  135.2 2.5 collective-permute-start.10
  141.9 3.2 %collective-permute-start.11 = (bf16[16,4096]{1,0:T(8,128)(2,1)S(1)}, bf16[16,4096]{1,0:T(8,128)(2,1)S(1)}, u32[]{:S(2)}, u32[]{:S(2)}) collective-permute-start(bf16[16,4096]{1,0:T(8,128)(2,1)S(1)} %get-tuple-element.113), channel_id=1, source_target_pairs={{0,192},{64,0},{128,64},{192,128},{1,193},{65,1},{129,65},{193,129... | collective-permute-start | bytes 393224 | tf_op jit(solution)/shard_map/ppermute | solution.py:341
  149.2 3.2 %collective-permute-start.12 = (bf16[16,4096]{1,0:T(8,128)(2,1)S(1)}, bf16[16,4096]{1,0:T(8,128)(2,1)S(1)}, u32[]{:S(2)}, u32[]{:S(2)}) collective-permute-start(bf16[16,4096]{1,0:T(8,128)(2,1)S(1)} %get-tuple-element.116), channel_id=1, source_target_pairs={{0,192},{64,0},{128,64},{192,128},{1,193},{65,1},{129,65},{193,129... | collective-permute-start | bytes 393224 | tf_op jit(solution)/shard_map/ppermute | solution.py:341
  155.1 7.5 %collective-permute-start.14 = (bf16[64,1792]{1,0:T(8,128)(2,1)S(1)}, bf16[64,1792]{1,0:T(8,128)(2,1)S(1)}, u32[]{:S(2)}, u32[]{:S(2)}) collective-permute-start(bf16[64,1792]{1,0:T(8,128)(2,1)S(1)} %get-tuple-element.130), channel_id=1, source_target_pairs={{0,1},{1,0},{2,3},{3,2},{4,5},{5,4},{6,7},{7,6},{8,9},{9,8},{10,11... | collective-permute-start | bytes 688136 | tf_op jit(solution)/shard_map/ppermute | solution.py:201
  169.7 5.1 %collective-permute-done.16.refs_3_.refs_7_ = bf16[64,1792]{1,0:T(8,128)(2,1)S(1)} collective-permute-done((bf16[64,1792]{1,0:T(8,128)(2,1)S(1)}, bf16[64,1792]{1,0:T(8,128)(2,1)S(1)}, u32[]{:S(2)}, u32[]{:S(2)}) %collective-permute-start.16) | collective-permute-done | bytes 229408 | tf_op jit(solution)/shard_map/ppermute | solution.py:201
  177.8 5.0 %all-to-all-start = ((bf16[16,32,1024]{2,1,0:T(8,128)(2,1)}), bf16[16,32,1024]{2,1,0:T(8,128)(2,1)}, u32[]{:S(2)}, u32[]{:S(2)}) async-start(bf16[16,32,1024]{2,1,0:T(8,128)(2,1)} %shard_map.141), calls=%async_computation | async-start | bytes 2097152 | tf_op jit(solution)/shard_map/all_to_all | solution.py:357
  189.5 5.2 %collective-permute-done.17.refs_0_.refs_6_ = bf16[16,4096]{1,0:T(8,128)(2,1)S(1)} collective-permute-done((bf16[16,4096]{1,0:T(8,128)(2,1)S(1)}, bf16[16,4096]{1,0:T(8,128)(2,1)S(1)}, u32[]{:S(2)}, u32[]{:S(2)}) %collective-permute-start.17) | collective-permute-done | bytes 131104 | tf_op jit(solution)/shard_map/ppermute | solution.py:341
  198.2 4.8 %collective-permute-done.18.refs_0_.refs_7_ = bf16[16,4096]{1,0:T(8,128)(2,1)S(1)} collective-permute-done((bf16[16,4096]{1,0:T(8,128)(2,1)S(1)}, bf16[16,4096]{1,0:T(8,128)(2,1)S(1)}, u32[]{:S(2)}, u32[]{:S(2)}) %collective-permute-start.18) | collective-permute-done | bytes 131104 | tf_op jit(solution)/shard_map/ppermute | solution.py:341
  211.1 4.4 %collective-permute-done.20.refs_2_ = bf16[64,1280]{1,0:T(8,128)(2,1)S(1)} collective-permute-done((bf16[64,1280]{1,0:T(8,128)(2,1)}, bf16[64,1280]{1,0:T(8,128)(2,1)S(1)}, u32[]{:S(2)}, u32[]{:S(2)}) %collective-permute-start.20) | collective-permute-done | bytes 163872 | tf_op jit(solution)/shard_map/ppermute | solution.py:201
  215.5 3.6 %collective-permute-done.21.refs_3_ = bf16[64,1280]{1,0:T(8,128)(2,1)S(1)} collective-permute-done((bf16[64,1280]{1,0:T(8,128)(2,1)}, bf16[64,1280]{1,0:T(8,128)(2,1)S(1)}, u32[]{:S(2)}, u32[]{:S(2)}) %collective-permute-start.21) | collective-permute-done | bytes 163872 | tf_op jit(solution)/shard_map/ppermute | solution.py:201
  224.4 4.1 %all-to-all-start.1 = ((bf16[4,4,32,1024]{3,2,1,0:T(8,128)(2,1)}), bf16[4,4,32,1024]{3,2,1,0:T(8,128)(2,1)S(1)}, u32[]{:S(2)}, u32[]{:S(2)}) async-start(bf16[4,4,32,1024]{3,2,1,0:T(8,128)(2,1)} %bitcast.25), calls=%async_computation.1 | async-start | bytes 2097152 | tf_op jit(solution)/shard_map/all_to_all | solution.py:363
  232.7 10.3 %all-to-all-done.1 = bf16[4,4,32,1024]{3,2,1,0:T(8,128)(2,1)S(1)} async-done(((bf16[4,4,32,1024]{3,2,1,0:T(8,128)(2,1)}), bf16[4,4,32,1024]{3,2,1,0:T(8,128)(2,1)S(1)}, u32[]{:S(2)}, u32[]{:S(2)}) %all-to-all-start.1) | async-done | bytes 1048608 | tf_op jit(solution)/shard_map/all_to_all | solution.py:363
  244.0 6.4 %all-to-all-start.2 = ((bf16[4,32,1024]{2,1,0:T(8,128)(2,1)}), bf16[4,32,1024]{2,1,0:T(8,128)(2,1)S(1)}, u32[]{:S(2)}, u32[]{:S(2)}) async-start(bf16[4,32,1024]{2,1,0:T(8,128)(2,1)} %reduce_sum.66), calls=%async_computation.2 | async-start | bytes 524288 | tf_op jit(solution)/shard_map/all_to_all | solution.py:365
  251.3 7.4 %all-to-all-done.2 = bf16[4,32,1024]{2,1,0:T(8,128)(2,1)S(1)} async-done(((bf16[4,32,1024]{2,1,0:T(8,128)(2,1)}), bf16[4,32,1024]{2,1,0:T(8,128)(2,1)S(1)}, u32[]{:S(2)}, u32[]{:S(2)}) %all-to-all-start.2) | async-done | bytes 262176 | tf_op jit(solution)/shard_map/all_to_all | solution.py:365
  265.4 10.5 %all_gather.7 = f32[160,128]{1,0:T(8,128)S(1)} all-gather(f32[40,128]{1,0:T(8,128)S(1)} %pad.4), channel_id=1, replica_groups=mesh['s'=4,'x'=4,'zh'=4,'zl'=2,'c'=2] {'zl','c'}, dimensions={0}, use_global_device_ids=true | all-gather | bytes 102400 | tf_op jit(solution)/shard_map/all_gather | solution.py:395
  276.6 3.7 %all-to-all-start.3 = ((f32[16,40,128]{2,1,0:T(8,128)}), f32[16,40,128]{2,1,0:T(8,128)S(1)}, u32[]{:S(2)}, u32[]{:S(2)}) async-start(f32[16,40,128]{2,1,0:T(8,128)} %broadcast_in_dim.60), calls=%async_computation.3 | async-start | bytes 655360 | tf_op jit(solution)/shard_map/all_to_all | solution.py:398
  283.5 9.7 %all-to-all-done.3 = f32[16,40,128]{2,1,0:T(8,128)S(1)} async-done(((f32[16,40,128]{2,1,0:T(8,128)}), f32[16,40,128]{2,1,0:T(8,128)S(1)}, u32[]{:S(2)}, u32[]{:S(2)}) %all-to-all-start.3) | async-done | bytes 327712 | tf_op jit(solution)/shard_map/all_to_all | solution.py:398
  (173 shorter events, 95.9 us)
Async XLA Ops:
  7.2 92.0 %all-gather.2.cloned.1.call-start = ((), (), s32[]{:S(2)}) async-start(), calls=%async_computation.4 | async-start | bytes 8519680 | tf_op jit(solution)/shard_map/all_gather | solution.py:244
  11.8 14.2 %collective-permute-start = (f32[2,8,256]{2,1,0:T(8,128)}, f32[2,8,256]{2,1,0:T(8,128)S(1)}, u32[]{:S(2)}, u32[]{:S(2)}) collective-permute-start(f32[2,8,256]{2,1,0:T(8,128)} %bitcast.2.slot_ref), channel_id=1, source_target_pairs={{64,0},{128,64},{192,128},{0,192},{65,1},{129,65},{193,129},{1,193... | collective-permute-start | bytes 49160 | tf_op jit(solution)/shard_map/ppermute | solution.py:209
  15.4 10.7 %collective-permute-start.1 = (f32[2,8,256]{2,1,0:T(8,128)}, f32[2,8,256]{2,1,0:T(8,128)S(1)}, u32[]{:S(2)}, u32[]{:S(2)}) collective-permute-start(f32[2,8,256]{2,1,0:T(8,128)} %bitcast.2.slot_ref), channel_id=1, source_target_pairs={{128,0},{192,64},{0,128},{64,192},{129,1},{193,65},{1,129},{65,193... | collective-permute-start | bytes 49160 | tf_op jit(solution)/shard_map/ppermute | solution.py:209
  15.8 10.4 %collective-permute-start.2 = (f32[2,8,256]{2,1,0:T(8,128)}, f32[2,8,256]{2,1,0:T(8,128)S(1)}, u32[]{:S(2)}, u32[]{:S(2)}) collective-permute-start(f32[2,8,256]{2,1,0:T(8,128)} %bitcast.2.slot_ref), channel_id=1, source_target_pairs={{192,0},{0,64},{64,128},{128,192},{193,1},{1,65},{65,129},{129,193... | collective-permute-start | bytes 49160 | tf_op jit(solution)/shard_map/ppermute | solution.py:209
  20.4 7.1 %collective-permute-start.3 = (bf16[128,1024]{1,0:T(8,128)(2,1)}, bf16[128,1024]{1,0:T(8,128)(2,1)S(1)}, u32[]{:S(2)}, u32[]{:S(2)}) collective-permute-start(bf16[128,1024]{1,0:T(8,128)(2,1)} %get-tuple-element.87), channel_id=1, source_target_pairs={{0,1},{1,0},{2,3},{3,2},{4,5},{5,4},{6,7},{7,6},{8,9},{9,8},{10,11... | collective-permute-start | bytes 786440 | tf_op jit(solution)/shard_map/ppermute | solution.py:201
  21.9 8.5 %collective-permute-start.4 = (bf16[128,1024]{1,0:T(8,128)(2,1)}, bf16[128,1024]{1,0:T(8,128)(2,1)}, u32[]{:S(2)}, u32[]{:S(2)}) collective-permute-start(bf16[128,1024]{1,0:T(8,128)(2,1)} %get-tuple-element.88), channel_id=1, source_target_pairs={{0,2},{1,3},{2,0},{3,1},{4,6},{5,7},{6,4},{7,5},{8,10},{9,11},{10,... | collective-permute-start | bytes 786440 | tf_op jit(solution)/shard_map/ppermute | solution.py:201
  26.0 11.7 %collective-permute-start.5 = (bf16[128,1024]{1,0:T(8,128)(2,1)}, bf16[128,1024]{1,0:T(8,128)(2,1)S(1)}, u32[]{:S(2)}, u32[]{:S(2)}) collective-permute-start(bf16[128,1024]{1,0:T(8,128)(2,1)} %copy-done.29), channel_id=1, source_target_pairs={{0,3},{1,2},{2,1},{3,0},{4,7},{5,6},{6,5},{7,4},{8,11},{9,10},{10,... | collective-permute-start | bytes 786440 | tf_op jit(solution)/shard_map/ppermute | solution.py:201
  110.7 15.9 %collective-permute-start.8 = (bf16[16,4096]{1,0:T(8,128)(2,1)S(1)}, bf16[16,4096]{1,0:T(8,128)(2,1)S(1)}, u32[]{:S(2)}, u32[]{:S(2)}) collective-permute-start(bf16[16,4096]{1,0:T(8,128)(2,1)S(1)} %get-tuple-element.101), channel_id=1, source_target_pairs={{64,0},{128,64},{192,128},{65,1},{129,65},{193,129},{66,2},{130,66... | collective-permute-start | bytes 393224 | tf_op jit(solution)/shard_map/ppermute | solution.py:341
  141.9 5.1 %collective-permute-start.11 = (bf16[16,4096]{1,0:T(8,128)(2,1)S(1)}, bf16[16,4096]{1,0:T(8,128)(2,1)S(1)}, u32[]{:S(2)}, u32[]{:S(2)}) collective-permute-start(bf16[16,4096]{1,0:T(8,128)(2,1)S(1)} %get-tuple-element.113), channel_id=1, source_target_pairs={{0,192},{64,0},{128,64},{192,128},{1,193},{65,1},{129,65},{193,129... | collective-permute-start | bytes 393224 | tf_op jit(solution)/shard_map/ppermute | solution.py:341
  155.1 12.7 %collective-permute-start.14 = (bf16[64,1792]{1,0:T(8,128)(2,1)S(1)}, bf16[64,1792]{1,0:T(8,128)(2,1)S(1)}, u32[]{:S(2)}, u32[]{:S(2)}) collective-permute-start(bf16[64,1792]{1,0:T(8,128)(2,1)S(1)} %get-tuple-element.130), channel_id=1, source_target_pairs={{0,1},{1,0},{2,3},{3,2},{4,5},{5,4},{6,7},{7,6},{8,9},{9,8},{10,11... | collective-permute-start | bytes 688136 | tf_op jit(solution)/shard_map/ppermute | solution.py:201
  162.5 7.2 %collective-permute-start.15 = (bf16[64,1792]{1,0:T(8,128)(2,1)S(1)}, bf16[64,1792]{1,0:T(8,128)(2,1)S(1)}, u32[]{:S(2)}, u32[]{:S(2)}) collective-permute-start(bf16[64,1792]{1,0:T(8,128)(2,1)S(1)} %get-tuple-element.131), channel_id=1, source_target_pairs={{0,2},{1,3},{2,0},{3,1},{4,6},{5,7},{6,4},{7,5},{8,10},{9,11},{10,... | collective-permute-start | bytes 688136 | tf_op jit(solution)/shard_map/ppermute | solution.py:201
  163.9 10.8 %collective-permute-start.16 = (bf16[64,1792]{1,0:T(8,128)(2,1)S(1)}, bf16[64,1792]{1,0:T(8,128)(2,1)S(1)}, u32[]{:S(2)}, u32[]{:S(2)}) collective-permute-start(bf16[64,1792]{1,0:T(8,128)(2,1)S(1)} %get-tuple-element.132), channel_id=1, source_target_pairs={{0,3},{1,2},{2,1},{3,0},{4,7},{5,6},{6,5},{7,4},{8,11},{9,10},{10,... | collective-permute-start | bytes 688136 | tf_op jit(solution)/shard_map/ppermute | solution.py:201
  166.5 10.7 %collective-permute-start.13 = (bf16[16,4096]{1,0:T(8,128)(2,1)S(1)}, bf16[16,4096]{1,0:T(8,128)(2,1)S(1)}, u32[]{:S(2)}, u32[]{:S(2)}) collective-permute-start(bf16[16,4096]{1,0:T(8,128)(2,1)S(1)} %get-tuple-element.119), channel_id=1, source_target_pairs={{64,0},{128,64},{192,128},{65,1},{129,65},{193,129},{66,2},{130,66... | collective-permute-start | bytes 393224 | tf_op jit(solution)/shard_map/ppermute | solution.py:341
  177.8 33.3 %all-to-all-start = ((bf16[16,32,1024]{2,1,0:T(8,128)(2,1)}), bf16[16,32,1024]{2,1,0:T(8,128)(2,1)}, u32[]{:S(2)}, u32[]{:S(2)}) async-start(bf16[16,32,1024]{2,1,0:T(8,128)(2,1)} %shard_map.141), calls=%async_computation | async-start | bytes 2097152 | tf_op jit(solution)/shard_map/all_to_all | solution.py:357
  188.2 6.5 %collective-permute-start.17 = (bf16[16,4096]{1,0:T(8,128)(2,1)S(1)}, bf16[16,4096]{1,0:T(8,128)(2,1)S(1)}, u32[]{:S(2)}, u32[]{:S(2)}) collective-permute-start(bf16[16,4096]{1,0:T(8,128)(2,1)S(1)} %get-tuple-element.140), channel_id=1, source_target_pairs={{64,0},{128,64},{65,1},{129,65},{66,2},{130,66},{67,3},{131,67},{6... | collective-permute-start | bytes 393224 | tf_op jit(solution)/shard_map/ppermute | solution.py:341
  196.9 6.1 %collective-permute-start.18 = (bf16[16,4096]{1,0:T(8,128)(2,1)S(1)}, bf16[16,4096]{1,0:T(8,128)(2,1)S(1)}, u32[]{:S(2)}, u32[]{:S(2)}) collective-permute-start(bf16[16,4096]{1,0:T(8,128)(2,1)S(1)} %get-tuple-element.143), channel_id=1, source_target_pairs={{64,0},{65,1},{66,2},{67,3},{68,4},{69,5},{70,6},{71,7},{72,8},{73... | collective-permute-start | bytes 393224 | tf_op jit(solution)/shard_map/ppermute | solution.py:341
  209.5 6.1 %collective-permute-start.20 = (bf16[64,1280]{1,0:T(8,128)(2,1)}, bf16[64,1280]{1,0:T(8,128)(2,1)S(1)}, u32[]{:S(2)}, u32[]{:S(2)}) collective-permute-start(bf16[64,1280]{1,0:T(8,128)(2,1)} %get-tuple-element.156), channel_id=1, source_target_pairs={{0,2},{1,3},{2,0},{3,1},{4,6},{5,7},{6,4},{7,5},{8,10},{9,11},{10,... | collective-permute-start | bytes 491528 | tf_op jit(solution)/shard_map/ppermute | solution.py:201
  210.9 8.2 %collective-permute-start.21 = (bf16[64,1280]{1,0:T(8,128)(2,1)}, bf16[64,1280]{1,0:T(8,128)(2,1)S(1)}, u32[]{:S(2)}, u32[]{:S(2)}) collective-permute-start(bf16[64,1280]{1,0:T(8,128)(2,1)} %get-tuple-element.157), channel_id=1, source_target_pairs={{0,3},{1,2},{2,1},{3,0},{4,7},{5,6},{6,5},{7,4},{8,11},{9,10},{10,... | collective-permute-start | bytes 491528 | tf_op jit(solution)/shard_map/ppermute | solution.py:201
  224.4 18.7 %all-to-all-start.1 = ((bf16[4,4,32,1024]{3,2,1,0:T(8,128)(2,1)}), bf16[4,4,32,1024]{3,2,1,0:T(8,128)(2,1)S(1)}, u32[]{:S(2)}, u32[]{:S(2)}) async-start(bf16[4,4,32,1024]{3,2,1,0:T(8,128)(2,1)} %bitcast.25), calls=%async_computation.1 | async-start | bytes 2097152 | tf_op jit(solution)/shard_map/all_to_all | solution.py:363
  231.1 20.0 %collective-permute-start.22 = (bf16[32,1024]{1,0:T(8,128)(2,1)S(1)}, bf16[32,1024]{1,0:T(8,128)(2,1)S(1)}, u32[]{:S(2)}, u32[]{:S(2)}) collective-permute-start(bf16[32,1024]{1,0:T(8,128)(2,1)S(1)} %multiply_convert_fusion.1), channel_id=1, source_target_pairs={{64,0},{128,64},{192,128},{0,192},{65,1},{129,65},{193,129},{1,193... | collective-permute-start | bytes 196616 | tf_op jit(solution)/shard_map/ppermute | solution.py:209
  231.2 19.9 %collective-permute-start.23 = (bf16[32,1024]{1,0:T(8,128)(2,1)S(1)}, bf16[32,1024]{1,0:T(8,128)(2,1)S(1)}, u32[]{:S(2)}, u32[]{:S(2)}) collective-permute-start(bf16[32,1024]{1,0:T(8,128)(2,1)S(1)} %multiply_convert_fusion.1), channel_id=1, source_target_pairs={{128,0},{192,64},{0,128},{64,192},{129,1},{193,65},{1,129},{65,193... | collective-permute-start | bytes 196616 | tf_op jit(solution)/shard_map/ppermute | solution.py:209
  232.3 18.9 %collective-permute-start.24 = (bf16[32,1024]{1,0:T(8,128)(2,1)S(1)}, bf16[32,1024]{1,0:T(8,128)(2,1)S(1)}, u32[]{:S(2)}, u32[]{:S(2)}) collective-permute-start(bf16[32,1024]{1,0:T(8,128)(2,1)S(1)} %multiply_convert_fusion.1), channel_id=1, source_target_pairs={{192,0},{0,64},{64,128},{128,192},{193,1},{1,65},{65,129},{129,193... | collective-permute-start | bytes 196616 | tf_op jit(solution)/shard_map/ppermute | solution.py:209
  244.0 14.8 %all-to-all-start.2 = ((bf16[4,32,1024]{2,1,0:T(8,128)(2,1)}), bf16[4,32,1024]{2,1,0:T(8,128)(2,1)S(1)}, u32[]{:S(2)}, u32[]{:S(2)}) async-start(bf16[4,32,1024]{2,1,0:T(8,128)(2,1)} %reduce_sum.66), calls=%async_computation.2 | async-start | bytes 524288 | tf_op jit(solution)/shard_map/all_to_all | solution.py:365
  276.6 16.6 %all-to-all-start.3 = ((f32[16,40,128]{2,1,0:T(8,128)}), f32[16,40,128]{2,1,0:T(8,128)S(1)}, u32[]{:S(2)}, u32[]{:S(2)}) async-start(f32[16,40,128]{2,1,0:T(8,128)} %broadcast_in_dim.60), calls=%async_computation.3 | async-start | bytes 655360 | tf_op jit(solution)/shard_map/all_to_all | solution.py:398
  (42 other events, 712.3 us)
Sparse Core Ops, SparseCore 0:
  11.9 87.2 all-gather.1

commit v6 on v5

--- a/solution.py
+++ b/solution.py
@@ -336,7 +336,7 @@
         pairs = [
             (i, (i - 1) % sections)
             for i in range(sections)
-            if active(tick, i) == 1 or (i and active(tick, i) == 0)
+            if active(tick, i) == 1 or tick >= HOP * sections + micros - 1 or (i and active(tick, i) == 0)
         ]
         arriving = lax.ppermute(result, "s", pairs)
         if tick == 1:

time: 303 us -> 318 us (1.050); the launches traced: 301 us -> 313 us
  starting transfers between devices: 59.6 us -> 81.5 us
  waiting for transfers between devices: 149 us -> 139 us
    all_to_all x1, starting transfers between devices: 5.01 us -> 15.1 us  [on_device(): early = lax.all_to_all(early, RANKS, 0, 0)]
    ppermute x10, starting transfers between devices: 16.6 us -> 23.3 us  [on_device(): arriving = lax.ppermute(result, 's', pairs)]
    ppermute x10, waiting for transfers between devices: 31.5 us -> 25.7 us  [on_device(): arriving = lax.ppermute(result, 's', pairs)]
    ppermute x9, starting transfers between devices: 7.76 us -> 12.9 us  [from_sections(): lax.ppermute(part, 's', [((i + d) % count, i) for i in range(count)])]
  transfers between devices with their start and end apart: 33 -> 33, of which waited for: 20 -> 19; matrix products, arithmetic and copies ran while one was open for 4% -> 4% of each run, Pallas kernels for 5% -> 5%
where the time goes in v6:
time: 318 us; the launch traced here: 313 us
  waiting for transfers between devices  139 us (44%)
  starting transfers between devices  81.5 us (26%)
  Pallas kernels  36.8 us (12%)
  local copies, waits for them, and re-layouts  19.8 us (6%)
  between operations  14.8 us (5%)
  blocking collectives  10.3 us (3%)
  other arithmetic  7.21 us (2%)
  matrix products  3.81 us (1%)
    all_gather x1, waiting for transfers between devices, on_device(): lax.all_gather(mine.reshape(blocks * 2 * combos, width), DP, axis=0, tile...  60.7 us
    pallas_call x19, Pallas kernels, call(): pl.pallas_call(kernel, out_shape=out_shape, in_specs=[SMEM] * scalars + [...  36.8 us
    ppermute x10, waiting for transfers between devices, on_device(): arriving = lax.ppermute(result, 's', pairs)  25.7 us
    ppermute x10, starting transfers between devices, on_device(): arriving = lax.ppermute(result, 's', pairs)  23.3 us
    ppermute x9, waiting for transfers between devices, swapped(): lax.ppermute(parts[d], axes, [(i, i ^ d) for i in range(count)])  23.1 us
    ppermute x9, starting transfers between devices, swapped(): lax.ppermute(parts[d], axes, [(i, i ^ d) for i in range(count)])  16.2 us
    all_to_all x1, starting transfers between devices, on_device(): early = lax.all_to_all(early, RANKS, 0, 0)  15.1 us
    ppermute x9, starting transfers between devices, from_sections(): lax.ppermute(part, 's', [((i + d) % count, i) for i in range(count)])  12.9 us
  transfers between devices with their start and end apart: 33, of which 19 were waited for; matrix products, arithmetic and copies ran while one was open for 4% of the time, Pallas kernels for 5%

profile of v6, /device:TPU:1, one launch (start us, length us, event | category | flops | bytes accessed | tf_op | source)
XLA Modules:
  0.0 313.1 jit_solution(5658801262271202565)
XLA Ops:
  11.8 3.6 %collective-permute-start = (f32[2,8,256]{2,1,0:T(8,128)}, f32[2,8,256]{2,1,0:T(8,128)S(1)}, u32[]{:S(2)}, u32[]{:S(2)}) collective-permute-start(f32[2,8,256]{2,1,0:T(8,128)} %bitcast.2.slot_ref), channel_id=1, source_target_pairs={{64,0},{128,64},{192,128},{0,192},{65,1},{129,65},{193,129},{1,193... | collective-permute-start | bytes 49160 | tf_op jit(solution)/shard_map/ppermute | solution.py:209
  30.4 7.3 %collective-permute-done.5.refs_11_ = bf16[128,1024]{1,0:T(8,128)(2,1)S(1)} collective-permute-done((bf16[128,1024]{1,0:T(8,128)(2,1)}, bf16[128,1024]{1,0:T(8,128)(2,1)S(1)}, u32[]{:S(2)}, u32[]{:S(2)}) %collective-permute-start.5) | collective-permute-done | bytes 262176 | tf_op jit(solution)/shard_map/ppermute | solution.py:201
  38.4 60.7 %all-gather.2.cloned.1.call-done = bf16[4096,1024]{1,0:T(8,128)(2,1)} async-done(((bf16[64,1024]{1,0:T(8,128)(2,1)}), bf16[4096,1024]{1,0:T(8,128)(2,1)}) %all-gather.2.cloned.1.call-update) | async-done | bytes 8388624 | tf_op jit(solution)/shard_map/all_gather | solution.py:244
  112.0 14.6 %collective-permute-done.8.refs_1_.refs_6_ = bf16[16,4096]{1,0:T(8,128)(2,1)S(1)} collective-permute-done((bf16[16,4096]{1,0:T(8,128)(2,1)S(1)}, bf16[16,4096]{1,0:T(8,128)(2,1)S(1)}, u32[]{:S(2)}, u32[]{:S(2)}) %collective-permute-start.8) | collective-permute-done | bytes 131104 | tf_op jit(solution)/shard_map/ppermute | solution.py:341
  141.9 3.2 %collective-permute-start.11 = (bf16[16,4096]{1,0:T(8,128)(2,1)S(1)}, bf16[16,4096]{1,0:T(8,128)(2,1)S(1)}, u32[]{:S(2)}, u32[]{:S(2)}) collective-permute-start(bf16[16,4096]{1,0:T(8,128)(2,1)S(1)} %get-tuple-element.113), channel_id=1, source_target_pairs={{0,192},{64,0},{128,64},{192,128},{1,193},{65,1},{129,65},{193,129... | collective-permute-start | bytes 393224 | tf_op jit(solution)/shard_map/ppermute | solution.py:341
  149.3 3.2 %collective-permute-start.12 = (bf16[16,4096]{1,0:T(8,128)(2,1)S(1)}, bf16[16,4096]{1,0:T(8,128)(2,1)S(1)}, u32[]{:S(2)}, u32[]{:S(2)}) collective-permute-start(bf16[16,4096]{1,0:T(8,128)(2,1)S(1)} %get-tuple-element.116), channel_id=1, source_target_pairs={{0,192},{64,0},{128,64},{192,128},{1,193},{65,1},{129,65},{193,129... | collective-permute-start | bytes 393224 | tf_op jit(solution)/shard_map/ppermute | solution.py:341
  155.1 7.5 %collective-permute-start.14 = (bf16[64,1792]{1,0:T(8,128)(2,1)S(1)}, bf16[64,1792]{1,0:T(8,128)(2,1)S(1)}, u32[]{:S(2)}, u32[]{:S(2)}) collective-permute-start(bf16[64,1792]{1,0:T(8,128)(2,1)S(1)} %get-tuple-element.130), channel_id=1, source_target_pairs={{0,1},{1,0},{2,3},{3,2},{4,5},{5,4},{6,7},{7,6},{8,9},{9,8},{10,11... | collective-permute-start | bytes 688136 | tf_op jit(solution)/shard_map/ppermute | solution.py:201
  166.6 3.5 %collective-permute-start.13 = (bf16[16,4096]{1,0:T(8,128)(2,1)S(1)}, bf16[16,4096]{1,0:T(8,128)(2,1)S(1)}, u32[]{:S(2)}, u32[]{:S(2)}) collective-permute-start(bf16[16,4096]{1,0:T(8,128)(2,1)S(1)} %get-tuple-element.119), channel_id=1, source_target_pairs={{0,192},{64,0},{128,64},{192,128},{1,193},{65,1},{129,65},{193,129... | collective-permute-start | bytes 393224 | tf_op jit(solution)/shard_map/ppermute | solution.py:341
  170.0 4.8 %collective-permute-done.16.refs_3_.refs_7_ = bf16[64,1792]{1,0:T(8,128)(2,1)S(1)} collective-permute-done((bf16[64,1792]{1,0:T(8,128)(2,1)S(1)}, bf16[64,1792]{1,0:T(8,128)(2,1)S(1)}, u32[]{:S(2)}, u32[]{:S(2)}) %collective-permute-start.16) | collective-permute-done | bytes 229408 | tf_op jit(solution)/shard_map/ppermute | solution.py:201
  177.9 15.1 %all-to-all-start = ((bf16[16,32,1024]{2,1,0:T(8,128)(2,1)}), bf16[16,32,1024]{2,1,0:T(8,128)(2,1)}, u32[]{:S(2)}, u32[]{:S(2)}) async-start(bf16[16,32,1024]{2,1,0:T(8,128)(2,1)} %shard_map.141), calls=%async_computation | async-start | bytes 2097152 | tf_op jit(solution)/shard_map/all_to_all | solution.py:357
  198.3 3.5 %collective-permute-start.17 = (bf16[16,4096]{1,0:T(8,128)(2,1)S(1)}, bf16[16,4096]{1,0:T(8,128)(2,1)S(1)}, u32[]{:S(2)}, u32[]{:S(2)}) collective-permute-start(bf16[16,4096]{1,0:T(8,128)(2,1)S(1)} %get-tuple-element.140), channel_id=1, source_target_pairs={{0,192},{64,0},{128,64},{192,128},{1,193},{65,1},{129,65},{193,129... | collective-permute-start | bytes 393224 | tf_op jit(solution)/shard_map/ppermute | solution.py:341
  206.3 3.6 %collective-permute-start.18 = (bf16[16,4096]{1,0:T(8,128)(2,1)S(1)}, bf16[16,4096]{1,0:T(8,128)(2,1)S(1)}, u32[]{:S(2)}, u32[]{:S(2)}) collective-permute-start(bf16[16,4096]{1,0:T(8,128)(2,1)S(1)} %get-tuple-element.143), channel_id=1, source_target_pairs={{0,192},{64,0},{128,64},{192,128},{1,193},{65,1},{129,65},{193,129... | collective-permute-start | bytes 393224 | tf_op jit(solution)/shard_map/ppermute | solution.py:341
  220.0 4.4 %collective-permute-done.20.refs_2_ = bf16[64,1280]{1,0:T(8,128)(2,1)S(1)} collective-permute-done((bf16[64,1280]{1,0:T(8,128)(2,1)}, bf16[64,1280]{1,0:T(8,128)(2,1)S(1)}, u32[]{:S(2)}, u32[]{:S(2)}) %collective-permute-start.20) | collective-permute-done | bytes 163872 | tf_op jit(solution)/shard_map/ppermute | solution.py:201
  224.4 3.6 %collective-permute-done.21.refs_3_ = bf16[64,1280]{1,0:T(8,128)(2,1)S(1)} collective-permute-done((bf16[64,1280]{1,0:T(8,128)(2,1)}, bf16[64,1280]{1,0:T(8,128)(2,1)S(1)}, u32[]{:S(2)}, u32[]{:S(2)}) %collective-permute-start.21) | collective-permute-done | bytes 163872 | tf_op jit(solution)/shard_map/ppermute | solution.py:201
  233.2 4.1 %all-to-all-start.1 = ((bf16[4,4,32,1024]{3,2,1,0:T(8,128)(2,1)}), bf16[4,4,32,1024]{3,2,1,0:T(8,128)(2,1)S(1)}, u32[]{:S(2)}, u32[]{:S(2)}) async-start(bf16[4,4,32,1024]{3,2,1,0:T(8,128)(2,1)} %bitcast.25), calls=%async_computation.1 | async-start | bytes 2097152 | tf_op jit(solution)/shard_map/all_to_all | solution.py:363
  240.1 3.5 %collective-permute-start.22 = (bf16[32,1024]{1,0:T(8,128)(2,1)S(1)}, bf16[32,1024]{1,0:T(8,128)(2,1)S(1)}, u32[]{:S(2)}, u32[]{:S(2)}) collective-permute-start(bf16[32,1024]{1,0:T(8,128)(2,1)S(1)} %multiply_convert_fusion.1), channel_id=1, source_target_pairs={{64,0},{128,64},{192,128},{0,192},{65,1},{129,65},{193,129},{1,193... | collective-permute-start | bytes 196616 | tf_op jit(solution)/shard_map/ppermute | solution.py:209
  244.2 7.7 %all-to-all-done.1 = bf16[4,4,32,1024]{3,2,1,0:T(8,128)(2,1)S(1)} async-done(((bf16[4,4,32,1024]{3,2,1,0:T(8,128)(2,1)}), bf16[4,4,32,1024]{3,2,1,0:T(8,128)(2,1)S(1)}, u32[]{:S(2)}, u32[]{:S(2)}) %all-to-all-start.1) | async-done | bytes 1048608 | tf_op jit(solution)/shard_map/all_to_all | solution.py:363
  252.9 6.4 %all-to-all-start.2 = ((bf16[4,32,1024]{2,1,0:T(8,128)(2,1)}), bf16[4,32,1024]{2,1,0:T(8,128)(2,1)S(1)}, u32[]{:S(2)}, u32[]{:S(2)}) async-start(bf16[4,32,1024]{2,1,0:T(8,128)(2,1)} %reduce_sum.66), calls=%async_computation.2 | async-start | bytes 524288 | tf_op jit(solution)/shard_map/all_to_all | solution.py:365
  260.2 7.5 %all-to-all-done.2 = bf16[4,32,1024]{2,1,0:T(8,128)(2,1)S(1)} async-done(((bf16[4,32,1024]{2,1,0:T(8,128)(2,1)}), bf16[4,32,1024]{2,1,0:T(8,128)(2,1)S(1)}, u32[]{:S(2)}, u32[]{:S(2)}) %all-to-all-start.2) | async-done | bytes 262176 | tf_op jit(solution)/shard_map/all_to_all | solution.py:365
  267.7 3.4 %collective-permute-start.25 = (bf16[32,1024]{1,0:T(8,128)(2,1)S(1)}, bf16[32,1024]{1,0:T(8,128)(2,1)S(1)}, u32[]{:S(2)}, u32[]{:S(2)}) collective-permute-start(bf16[32,1024]{1,0:T(8,128)(2,1)S(1)} %multiply_convert_fusion), channel_id=1, source_target_pairs={{64,0},{128,64},{192,128},{0,192},{65,1},{129,65},{193,129},{1,193... | collective-permute-start | bytes 196616 | tf_op jit(solution)/shard_map/ppermute | solution.py:209
  272.5 3.4 %collective-permute-done.26 = bf16[32,1024]{1,0:T(8,128)(2,1)S(1)} collective-permute-done((bf16[32,1024]{1,0:T(8,128)(2,1)S(1)}, bf16[32,1024]{1,0:T(8,128)(2,1)S(1)}, u32[]{:S(2)}, u32[]{:S(2)}) %collective-permute-start.26) | collective-permute-done | bytes 65568 | tf_op jit(solution)/shard_map/ppermute | solution.py:209
  277.2 10.3 %all_gather.7 = f32[160,128]{1,0:T(8,128)S(1)} all-gather(f32[40,128]{1,0:T(8,128)S(1)} %pad.4), channel_id=1, replica_groups=mesh['s'=4,'x'=4,'zh'=4,'zl'=2,'c'=2] {'zl','c'}, dimensions={0}, use_global_device_ids=true | all-gather | bytes 102400 | tf_op jit(solution)/shard_map/all_gather | solution.py:395
  288.2 3.7 %all-to-all-start.3 = ((f32[16,40,128]{2,1,0:T(8,128)}), f32[16,40,128]{2,1,0:T(8,128)S(1)}, u32[]{:S(2)}, u32[]{:S(2)}) async-start(f32[16,40,128]{2,1,0:T(8,128)} %broadcast_in_dim.60), calls=%async_computation.3 | async-start | bytes 655360 | tf_op jit(solution)/shard_map/all_to_all | solution.py:398
  295.1 9.7 %all-to-all-done.3 = f32[16,40,128]{2,1,0:T(8,128)S(1)} async-done(((f32[16,40,128]{2,1,0:T(8,128)}), f32[16,40,128]{2,1,0:T(8,128)S(1)}, u32[]{:S(2)}, u32[]{:S(2)}) %all-to-all-start.3) | async-done | bytes 327712 | tf_op jit(solution)/shard_map/all_to_all | solution.py:398
  (173 shorter events, 100.2 us)
Async XLA Ops:
  7.2 92.0 %all-gather.2.cloned.1.call-start = ((), (), s32[]{:S(2)}) async-start(), calls=%async_computation.4 | async-start | bytes 8519680 | tf_op jit(solution)/shard_map/all_gather | solution.py:244
  11.8 14.2 %collective-permute-start = (f32[2,8,256]{2,1,0:T(8,128)}, f32[2,8,256]{2,1,0:T(8,128)S(1)}, u32[]{:S(2)}, u32[]{:S(2)}) collective-permute-start(f32[2,8,256]{2,1,0:T(8,128)} %bitcast.2.slot_ref), channel_id=1, source_target_pairs={{64,0},{128,64},{192,128},{0,192},{65,1},{129,65},{193,129},{1,193... | collective-permute-start | bytes 49160 | tf_op jit(solution)/shard_map/ppermute | solution.py:209
  15.4 10.7 %collective-permute-start.1 = (f32[2,8,256]{2,1,0:T(8,128)}, f32[2,8,256]{2,1,0:T(8,128)S(1)}, u32[]{:S(2)}, u32[]{:S(2)}) collective-permute-start(f32[2,8,256]{2,1,0:T(8,128)} %bitcast.2.slot_ref), channel_id=1, source_target_pairs={{128,0},{192,64},{0,128},{64,192},{129,1},{193,65},{1,129},{65,193... | collective-permute-start | bytes 49160 | tf_op jit(solution)/shard_map/ppermute | solution.py:209
  15.8 10.4 %collective-permute-start.2 = (f32[2,8,256]{2,1,0:T(8,128)}, f32[2,8,256]{2,1,0:T(8,128)S(1)}, u32[]{:S(2)}, u32[]{:S(2)}) collective-permute-start(f32[2,8,256]{2,1,0:T(8,128)} %bitcast.2.slot_ref), channel_id=1, source_target_pairs={{192,0},{0,64},{64,128},{128,192},{193,1},{1,65},{65,129},{129,193... | collective-permute-start | bytes 49160 | tf_op jit(solution)/shard_map/ppermute | solution.py:209
  20.4 7.2 %collective-permute-start.3 = (bf16[128,1024]{1,0:T(8,128)(2,1)}, bf16[128,1024]{1,0:T(8,128)(2,1)S(1)}, u32[]{:S(2)}, u32[]{:S(2)}) collective-permute-start(bf16[128,1024]{1,0:T(8,128)(2,1)} %get-tuple-element.87), channel_id=1, source_target_pairs={{0,1},{1,0},{2,3},{3,2},{4,5},{5,4},{6,7},{7,6},{8,9},{9,8},{10,11... | collective-permute-start | bytes 786440 | tf_op jit(solution)/shard_map/ppermute | solution.py:201
  21.9 8.5 %collective-permute-start.4 = (bf16[128,1024]{1,0:T(8,128)(2,1)}, bf16[128,1024]{1,0:T(8,128)(2,1)}, u32[]{:S(2)}, u32[]{:S(2)}) collective-permute-start(bf16[128,1024]{1,0:T(8,128)(2,1)} %get-tuple-element.88), channel_id=1, source_target_pairs={{0,2},{1,3},{2,0},{3,1},{4,6},{5,7},{6,4},{7,5},{8,10},{9,11},{10,... | collective-permute-start | bytes 786440 | tf_op jit(solution)/shard_map/ppermute | solution.py:201
  26.0 11.7 %collective-permute-start.5 = (bf16[128,1024]{1,0:T(8,128)(2,1)}, bf16[128,1024]{1,0:T(8,128)(2,1)S(1)}, u32[]{:S(2)}, u32[]{:S(2)}) collective-permute-start(bf16[128,1024]{1,0:T(8,128)(2,1)} %copy-done.29), channel_id=1, source_target_pairs={{0,3},{1,2},{2,1},{3,0},{4,7},{5,6},{6,5},{7,4},{8,11},{9,10},{10,... | collective-permute-start | bytes 786440 | tf_op jit(solution)/shard_map/ppermute | solution.py:201
  110.7 15.9 %collective-permute-start.8 = (bf16[16,4096]{1,0:T(8,128)(2,1)S(1)}, bf16[16,4096]{1,0:T(8,128)(2,1)S(1)}, u32[]{:S(2)}, u32[]{:S(2)}) collective-permute-start(bf16[16,4096]{1,0:T(8,128)(2,1)S(1)} %get-tuple-element.101), channel_id=1, source_target_pairs={{64,0},{128,64},{192,128},{65,1},{129,65},{193,129},{66,2},{130,66... | collective-permute-start | bytes 393224 | tf_op jit(solution)/shard_map/ppermute | solution.py:341
  141.9 5.1 %collective-permute-start.11 = (bf16[16,4096]{1,0:T(8,128)(2,1)S(1)}, bf16[16,4096]{1,0:T(8,128)(2,1)S(1)}, u32[]{:S(2)}, u32[]{:S(2)}) collective-permute-start(bf16[16,4096]{1,0:T(8,128)(2,1)S(1)} %get-tuple-element.113), channel_id=1, source_target_pairs={{0,192},{64,0},{128,64},{192,128},{1,193},{65,1},{129,65},{193,129... | collective-permute-start | bytes 393224 | tf_op jit(solution)/shard_map/ppermute | solution.py:341
  155.1 14.9 %collective-permute-start.14 = (bf16[64,1792]{1,0:T(8,128)(2,1)S(1)}, bf16[64,1792]{1,0:T(8,128)(2,1)S(1)}, u32[]{:S(2)}, u32[]{:S(2)}) collective-permute-start(bf16[64,1792]{1,0:T(8,128)(2,1)S(1)} %get-tuple-element.130), channel_id=1, source_target_pairs={{0,1},{1,0},{2,3},{3,2},{4,5},{5,4},{6,7},{7,6},{8,9},{9,8},{10,11... | collective-permute-start | bytes 688136 | tf_op jit(solution)/shard_map/ppermute | solution.py:201
  162.6 7.4 %collective-permute-start.15 = (bf16[64,1792]{1,0:T(8,128)(2,1)S(1)}, bf16[64,1792]{1,0:T(8,128)(2,1)S(1)}, u32[]{:S(2)}, u32[]{:S(2)}) collective-permute-start(bf16[64,1792]{1,0:T(8,128)(2,1)S(1)} %get-tuple-element.131), channel_id=1, source_target_pairs={{0,2},{1,3},{2,0},{3,1},{4,6},{5,7},{6,4},{7,5},{8,10},{9,11},{10,... | collective-permute-start | bytes 688136 | tf_op jit(solution)/shard_map/ppermute | solution.py:201
  164.0 10.8 %collective-permute-start.16 = (bf16[64,1792]{1,0:T(8,128)(2,1)S(1)}, bf16[64,1792]{1,0:T(8,128)(2,1)S(1)}, u32[]{:S(2)}, u32[]{:S(2)}) collective-permute-start(bf16[64,1792]{1,0:T(8,128)(2,1)S(1)} %get-tuple-element.132), channel_id=1, source_target_pairs={{0,3},{1,2},{2,1},{3,0},{4,7},{5,6},{6,5},{7,4},{8,11},{9,10},{10,... | collective-permute-start | bytes 688136 | tf_op jit(solution)/shard_map/ppermute | solution.py:201
  166.6 10.7 %collective-permute-start.13 = (bf16[16,4096]{1,0:T(8,128)(2,1)S(1)}, bf16[16,4096]{1,0:T(8,128)(2,1)S(1)}, u32[]{:S(2)}, u32[]{:S(2)}) collective-permute-start(bf16[16,4096]{1,0:T(8,128)(2,1)S(1)} %get-tuple-element.119), channel_id=1, source_target_pairs={{0,192},{64,0},{128,64},{192,128},{1,193},{65,1},{129,65},{193,129... | collective-permute-start | bytes 393224 | tf_op jit(solution)/shard_map/ppermute | solution.py:341
  177.9 42.1 %all-to-all-start = ((bf16[16,32,1024]{2,1,0:T(8,128)(2,1)}), bf16[16,32,1024]{2,1,0:T(8,128)(2,1)}, u32[]{:S(2)}, u32[]{:S(2)}) async-start(bf16[16,32,1024]{2,1,0:T(8,128)(2,1)} %shard_map.141), calls=%async_computation | async-start | bytes 2097152 | tf_op jit(solution)/shard_map/all_to_all | solution.py:357
  198.3 5.8 %collective-permute-start.17 = (bf16[16,4096]{1,0:T(8,128)(2,1)S(1)}, bf16[16,4096]{1,0:T(8,128)(2,1)S(1)}, u32[]{:S(2)}, u32[]{:S(2)}) collective-permute-start(bf16[16,4096]{1,0:T(8,128)(2,1)S(1)} %get-tuple-element.140), channel_id=1, source_target_pairs={{0,192},{64,0},{128,64},{192,128},{1,193},{65,1},{129,65},{193,129... | collective-permute-start | bytes 393224 | tf_op jit(solution)/shard_map/ppermute | solution.py:341
  206.3 5.5 %collective-permute-start.18 = (bf16[16,4096]{1,0:T(8,128)(2,1)S(1)}, bf16[16,4096]{1,0:T(8,128)(2,1)S(1)}, u32[]{:S(2)}, u32[]{:S(2)}) collective-permute-start(bf16[16,4096]{1,0:T(8,128)(2,1)S(1)} %get-tuple-element.143), channel_id=1, source_target_pairs={{0,192},{64,0},{128,64},{192,128},{1,193},{65,1},{129,65},{193,129... | collective-permute-start | bytes 393224 | tf_op jit(solution)/shard_map/ppermute | solution.py:341
  218.3 6.1 %collective-permute-start.20 = (bf16[64,1280]{1,0:T(8,128)(2,1)}, bf16[64,1280]{1,0:T(8,128)(2,1)S(1)}, u32[]{:S(2)}, u32[]{:S(2)}) collective-permute-start(bf16[64,1280]{1,0:T(8,128)(2,1)} %get-tuple-element.156), channel_id=1, source_target_pairs={{0,2},{1,3},{2,0},{3,1},{4,6},{5,7},{6,4},{7,5},{8,10},{9,11},{10,... | collective-permute-start | bytes 491528 | tf_op jit(solution)/shard_map/ppermute | solution.py:201
  219.8 8.2 %collective-permute-start.21 = (bf16[64,1280]{1,0:T(8,128)(2,1)}, bf16[64,1280]{1,0:T(8,128)(2,1)S(1)}, u32[]{:S(2)}, u32[]{:S(2)}) collective-permute-start(bf16[64,1280]{1,0:T(8,128)(2,1)} %get-tuple-element.157), channel_id=1, source_target_pairs={{0,3},{1,2},{2,1},{3,0},{4,7},{5,6},{6,5},{7,4},{8,11},{9,10},{10,... | collective-permute-start | bytes 491528 | tf_op jit(solution)/shard_map/ppermute | solution.py:201
  233.2 18.7 %all-to-all-start.1 = ((bf16[4,4,32,1024]{3,2,1,0:T(8,128)(2,1)}), bf16[4,4,32,1024]{3,2,1,0:T(8,128)(2,1)S(1)}, u32[]{:S(2)}, u32[]{:S(2)}) async-start(bf16[4,4,32,1024]{3,2,1,0:T(8,128)(2,1)} %bitcast.25), calls=%async_computation.1 | async-start | bytes 2097152 | tf_op jit(solution)/shard_map/all_to_all | solution.py:363
  240.1 20.0 %collective-permute-start.22 = (bf16[32,1024]{1,0:T(8,128)(2,1)S(1)}, bf16[32,1024]{1,0:T(8,128)(2,1)S(1)}, u32[]{:S(2)}, u32[]{:S(2)}) collective-permute-start(bf16[32,1024]{1,0:T(8,128)(2,1)S(1)} %multiply_convert_fusion.1), channel_id=1, source_target_pairs={{64,0},{128,64},{192,128},{0,192},{65,1},{129,65},{193,129},{1,193... | collective-permute-start | bytes 196616 | tf_op jit(solution)/shard_map/ppermute | solution.py:209
  243.5 16.6 %collective-permute-start.23 = (bf16[32,1024]{1,0:T(8,128)(2,1)S(1)}, bf16[32,1024]{1,0:T(8,128)(2,1)S(1)}, u32[]{:S(2)}, u32[]{:S(2)}) collective-permute-start(bf16[32,1024]{1,0:T(8,128)(2,1)S(1)} %multiply_convert_fusion.1), channel_id=1, source_target_pairs={{128,0},{192,64},{0,128},{64,192},{129,1},{193,65},{1,129},{65,193... | collective-permute-start | bytes 196616 | tf_op jit(solution)/shard_map/ppermute | solution.py:209
  243.5 16.6 %collective-permute-start.24 = (bf16[32,1024]{1,0:T(8,128)(2,1)S(1)}, bf16[32,1024]{1,0:T(8,128)(2,1)S(1)}, u32[]{:S(2)}, u32[]{:S(2)}) collective-permute-start(bf16[32,1024]{1,0:T(8,128)(2,1)S(1)} %multiply_convert_fusion.1), channel_id=1, source_target_pairs={{192,0},{0,64},{64,128},{128,192},{193,1},{1,65},{65,129},{129,193... | collective-permute-start | bytes 196616 | tf_op jit(solution)/shard_map/ppermute | solution.py:209
  252.9 14.8 %all-to-all-start.2 = ((bf16[4,32,1024]{2,1,0:T(8,128)(2,1)}), bf16[4,32,1024]{2,1,0:T(8,128)(2,1)S(1)}, u32[]{:S(2)}, u32[]{:S(2)}) async-start(bf16[4,32,1024]{2,1,0:T(8,128)(2,1)} %reduce_sum.66), calls=%async_computation.2 | async-start | bytes 524288 | tf_op jit(solution)/shard_map/all_to_all | solution.py:365
  288.2 16.6 %all-to-all-start.3 = ((f32[16,40,128]{2,1,0:T(8,128)}), f32[16,40,128]{2,1,0:T(8,128)S(1)}, u32[]{:S(2)}, u32[]{:S(2)}) async-start(f32[16,40,128]{2,1,0:T(8,128)} %broadcast_in_dim.60), calls=%async_computation.3 | async-start | bytes 655360 | tf_op jit(solution)/shard_map/all_to_all | solution.py:398
  (42 other events, 723.3 us)
Sparse Core Ops, SparseCore 0:
  11.9 87.2 all-gather.1
